TPU v7x, 256 devices: a whole 4x4x8 slice. The times are simulated.
256 devices in a mesh: slab: 8 (over y, core), tile: 32 (over z, x).
Axes of the slice: x: 4, y: 4, z: 8, core: 2. Of those that a mesh axis runs over, the one named last changes fastest.
Arguments:
- volume: float32 [3072, 512, 128], P('tile', 'slab'), may hold values from 0 to 2
- footprints: bfloat16 [32, 128, 128], replicated, may hold values from -0.02734375 to 0.02734375
- foot_index: int32 [3072, 8], P('tile'), may hold values from 0 to 31
- ray_block: int32 [3072, 8], replicated, may hold values from 0 to 63, as said below
- ray_slot: int32 [64], replicated, may hold values from 0 to 63, as said below
- measured: float32 [64, 512, 128], P('tile', 'slab'), may hold values from -6 to 6
- weights: float32 [64, 512, 128], P('tile', 'slab'), may hold values from 0.25 to 4
Outputs:
- updated_volume: float32 [3072, 512, 128], P('tile', 'slab')
Inputs may be any that keep to these rules, and one draw needn't show every extreme that they name: A permutation of the 64 ray blocks; ray block b is held by index ray_slot[b] // 2 of tile, and its rows of measured and weights are row ray_slot[b]. `ray_block`: the crossings of the rows held by one index of tile name at most 16 distinct ray blocks, no two of them held by the same owner.
All inputs are finite; a program needn't handle non-finite values.
Results may differ from a plain program's by a relative error of at most 0.002.
Values may be sent and summed in bfloat16 or wider, within the bound.
No kernel may reach another device: no remote copies, remote signals or barrier semaphores. Data moves between devices by JAX's collectives and lax.ppermute only.
A program may use at most 128 MiB of HBM per device.

v0:
```python
import math

import jax
import jax.numpy as jnp
from jax import lax
from jax.sharding import PartitionSpec as P

smoothing = 0.04
step_length = 2.0
variation_weight = 1.0
block_limit = 32


def with_halo(cells, sides, width):
    for axis, dim in sides:
        count = lax.axis_size(axis)
        ends = count - 1
        head = lax.slice_in_dim(cells, 0, width, axis=dim)
        tail = lax.slice_in_dim(cells, cells.shape[dim] - width, cells.shape[dim], axis=dim)
        cells = jnp.concatenate(
            [
                lax.ppermute(tail, axis, [(i, (i + 1) % count) for i in range(ends)]),
                cells,
                lax.ppermute(head, axis, [((i + 1) % count, i) for i in range(ends)]),
            ],
            axis=dim,
        )
    return cells


def flux_parts(grad_rows, grad_slices, grad_cols):
    magnitude = jnp.sqrt(
        grad_rows * grad_rows + grad_slices * grad_slices + grad_cols * grad_cols + smoothing
    )
    return (grad_rows / magnitude, grad_slices / magnitude, grad_cols / magnitude)


def column_grad(density):
    return jnp.concatenate(
        [density[:, :, 1:] - density[:, :, :-1], jnp.zeros_like(density[:, :, :1])], axis=2
    )


def column_div(flux):
    return jnp.concatenate([jnp.zeros_like(flux[:, :, :1]), flux[:, :, :-1]], axis=2) - flux


def per_device(volume, footprints, foot_index, ray_block, ray_slot, measured, weights):
    row_count, slice_count, column_count = volume.shape
    ray_width = footprints.shape[2]
    crossings = foot_index.shape[1]
    owners = lax.axis_size("tile")
    owned_count = measured.shape[0]
    position = lax.axis_index("tile")
    layer = lax.axis_index("slab")
    my_blocks = lax.dynamic_slice_in_dim(ray_block, position * row_count, row_count, 0)
    my_slots = jnp.take(ray_slot, my_blocks, axis=0)
    targets = my_slots // owned_count
    touch_count = owners // 2
    labels = jnp.arange(owners, dtype=jnp.int32)
    present = jnp.any(targets.reshape(-1)[:, None] == labels[None, :], axis=0)
    rank = jnp.cumsum(present.astype(jnp.int32)) - 1
    compact_targets = jnp.take(rank, targets, axis=0)
    compact_labels = jnp.arange(touch_count, dtype=jnp.int32)
    rounded = volume.astype(jnp.bfloat16)
    block_rows = math.gcd(row_count, block_limit)
    turns = row_count // block_rows
    pixel_groups = rounded.reshape(turns, block_rows, slice_count, column_count)
    offset_groups = foot_index.reshape(turns, block_rows, crossings)
    target_groups = targets.reshape(turns, block_rows, crossings)
    compact_groups = compact_targets.reshape(turns, block_rows, crossings)

    def project(running_sum, inputs):
        pixels, offsets, destinations = inputs
        stencil = jnp.take(footprints, offsets, axis=0)
        partial_value = jnp.einsum(
            "rzp,rkpq->rkzq", pixels, stencil, preferred_element_type=jnp.float32
        )
        flat = partial_value.reshape(block_rows * crossings, slice_count * ray_width)
        high = flat.astype(jnp.bfloat16)
        low = (flat - high.astype(jnp.float32)).astype(jnp.bfloat16)
        selector = (destinations.reshape(-1)[:, None] == compact_labels[None, :]).astype(
            jnp.bfloat16
        )
        dims = (((0,), (0,)), ((), ()))
        contrib = lax.dot_general(selector, high, dims, preferred_element_type=jnp.float32)
        contrib = contrib + lax.dot_general(selector, low, dims, preferred_element_type=jnp.float32)
        return (running_sum + contrib, None)

    start = jnp.zeros((touch_count, slice_count * ray_width), jnp.float32)
    compact_totals, _ = lax.scan(project, start, (pixel_groups, offset_groups, compact_groups))
    picked = jnp.take(compact_totals, jnp.clip(rank, 0, touch_count - 1), axis=0)
    totals = jnp.where(present[:, None], picked, 0.0)
    totals = totals.reshape(owners, slice_count, ray_width)
    arrived = lax.all_to_all(totals, "tile", split_axis=0, concat_axis=0, tiled=True)
    every_slot = jnp.take(ray_slot, ray_block, axis=0).reshape(owners, row_count * crossings)
    owned_here = every_slot // owned_count == position
    local_index = jnp.max(jnp.where(owned_here, every_slot % owned_count, 0), axis=1)
    chooser = jnp.arange(owned_count, dtype=jnp.int32)[:, None] == local_index[None, :]
    own_sums = jnp.sum(jnp.where(chooser[:, :, None, None], arrived[None], 0.0), axis=1)
    residual = (weights * (own_sums - measured)).astype(jnp.bfloat16)
    returned = lax.all_to_all(
        jnp.take(residual, local_index, axis=0), "tile", split_axis=0, concat_axis=0, tiled=True
    )

    def backproject(running, inputs):
        offsets, destinations = inputs
        stencil = jnp.take(footprints, offsets, axis=0)
        values = jnp.take(returned, destinations, axis=0)
        return (
            running,
            jnp.einsum("rkzq,rkpq->rzp", values, stencil, preferred_element_type=jnp.float32),
        )

    _, pieces = lax.scan(backproject, jnp.zeros((), jnp.float32), (offset_groups, target_groups))
    data_grad = pieces.reshape(row_count, slice_count, column_count)
    total_rows = row_count * owners
    total_slices = slice_count * lax.axis_size("slab")
    extended = with_halo(volume, (("slab", 1), ("tile", 0)), 1)
    center = extended[0 : row_count + 1, 0 : slice_count + 1]
    grad_rows = extended[1 : row_count + 2, 0 : slice_count + 1] - center
    grad_slices = extended[0 : row_count + 1, 1 : slice_count + 2] - center
    grad_cols = column_grad(center)
    row_ids = position * row_count - 1 + jnp.arange(row_count + 1, dtype=jnp.int32)
    slice_ids = layer * slice_count - 1 + jnp.arange(slice_count + 1, dtype=jnp.int32)
    grad_rows = jnp.where((row_ids == total_rows - 1)[:, None, None], 0.0, grad_rows)
    grad_slices = jnp.where((slice_ids == total_slices - 1)[None, :, None], 0.0, grad_slices)
    flux_rows, flux_slices, flux_cols = flux_parts(grad_rows, grad_slices, grad_cols)
    inside = (row_ids >= 0)[:, None, None] & (slice_ids >= 0)[None, :, None]
    flux_rows = jnp.where(inside, flux_rows, 0.0)
    flux_slices = jnp.where(inside, flux_slices, 0.0)
    flux_cols = jnp.where(inside, flux_cols, 0.0)
    variation = flux_rows[0:row_count, 1:] - flux_rows[1:, 1:]
    variation = variation + (flux_slices[1:, 0:slice_count] - flux_slices[1:, 1:])
    variation = variation + column_div(flux_cols[1:, 1:])
    updated = volume - step_length * (data_grad + variation_weight * variation)
    return jnp.maximum(updated, 0.0)


def solution(mesh):
    in_specs = (
        P("tile", "slab", None),
        P(),
        P("tile", None),
        P(),
        P(),
        P("tile", "slab", None),
        P("tile", "slab", None),
    )
    out_specs = P("tile", "slab", None)
    return jax.shard_map(
        per_device, mesh=mesh, in_specs=in_specs, out_specs=out_specs, check_vma=False
    )
```

profile of v0, /device:TPU:8, one launch (start us, length us, event | category | flops | bytes accessed | tf_op | source)
XLA Modules:
  0.0 264.0 jit_solution(16533665087758707706)
XLA Ops:
  0.0 1.9 fusion.65
  1.9 1.9 collective-permute-start
  3.8 3.6 %collective-permute-start.1 = (f32[96,1,128]{2,1,0:T(1,128)}, f32[96,1,128]{2,1,0:T(1,128)S(1)}, u32[]{:S(2)}, u32[]{:S(2)}) collective-permute-start(f32[96,1,128]{2,1,0:T(1,128)} %get-tuple-element.152), channel_id=1, source_target_pairs={{32,0},{64,32},{96,64},{128,96},{160,128},{192,160},{224,192},{33,... | collective-permute-start | bytes 147464 | tf_op jit(solution)/shard_map/ppermute | solution.py:24
  7.5 2.2 convert_element_type.31
  9.8 0.1 copy.33
  10.0 4.8 %gather_fusion.3 = s32[768]{0:T(1024)S(1)} fusion(s32[64]{0:T(128)S(1)} %copy-done, s32[1024]{0:T(1024)S(1)} %pad_clamp_fusion.6), kind=kCustom, calls=%fused_computation.3 | custom fusion | bytes 9216 | tf_op jit(solution)/shard_map/jit(_take)/gather | solution.py:57
  15.2 0.1 fusion.51
  15.3 0.1 copy.23
  15.4 0.1 fusion.57
  15.6 4.8 %gather_fusion.4 = s32[768]{0:T(1024)S(1)} fusion(s32[32]{0:T(128)S(1)} %get-tuple-element.113, s32[1024]{0:T(1024)S(1)} %pad_clamp_fusion.5), kind=kCustom, calls=%fused_computation.4 | custom fusion | bytes 9216 | tf_op jit(solution)/shard_map/jit(_take)/gather | solution.py:63
  20.6 0.1 copy.25
  20.7 67.1 %while.22 = (s32[]{:T(128)}, f32[16,8192]{1,0:T(8,128)S(1)}, s32[3,32,8]{2,1,0:T(8,128)S(1)}, s32[3,32,8]{2,1,0:T(8,128)S(1)}, bf16[32,128,128]{2,1,0:T(8,128)(2...) while((s32[]{:T(128)}, f32[16,8192]{1,0:T(8,128)S(1)}, ...), condition=%wide.region_5.7_spmd.clone, body=%wide.region_4.6_spmd.clone.sunk | while | flops 684075520 | bytes 52973936 | solution.py:91
  20.9 8.6 %gather_fusion.2 = bf16[256,128,128]{2,1,0:T(8,128)(2,1)} fusion(bf16[32,128,128]{2,1,0:T(8,128)(2,1)S(1)} %get-tuple-element.325, s32[1024]{0:T(1024)S(1)} %pad_clamp_fusion.12), kind=kCustom, calls=%fused_computation.clone.clone.1 | custom fusion | bytes 16778240 | tf_op jit(solution)/shard_map/while/body/eval_jaxpr/jit(_take)/gather | solution.py:75
  29.5 4.4 %fusion.85 = f32[32,8,64,128]{3,2,1,0:T(8,128)S(1)} fusion(bf16[32,8,128,128]{3,2,1,0:T(8,128)(2,1)} %bitcast.138, pred[32,8]{1,0:T(8,128)(4,1)S(1)} %get-tuple-element.304, bf16[3,32,64,128]{3,2,1,0:T(8,128)(2,1)S(1)} %get-tuple-element.326, s32[]{:T(128)S(6)} %copy.49), kind=kOutput, calls=%fused_computation.35.clone.1 | convolution fusion | flops 541065216 | bytes 17305604 | tf_op jit(solution)/shard_map/while/body/eval_jaxpr/rzp,rkpq->rkzq/dot_general | solution.py:76
  33.9 4.5 %fusion.86 = f32[16,8192]{1,0:T(8,128)S(1)} fusion(f32[32,8,64,128]{3,2,1,0:T(8,128)S(1)} %fusion.85, s32[256]{0:T(256)S(1)} %eq.129), kind=kOutput, calls=%fused_computation.33.clone.1 | convolution fusion | flops 67112960 | bytes 8913920 | tf_op jit(solution)/shard_map/while/body/eval_jaxpr/dot_general | solution.py:86
  38.4 4.5 %fusion.87 = f32[16,8192]{1,0:T(8,128)S(1)} fusion(f32[16,8192]{1,0:T(8,128)S(1)} %fusion.86, f32[32,8,64,128]{3,2,1,0:T(8,128)S(1)} %fusion.85, f32[16,8192]{1,0:T(8,128)S(1)} %get-tuple-element.314, pred[]{:T(512)S(6)} %compare.281, s32[256]{0:T(256)S(1)} %eq.129), kind=kOutput, calls=%fused_computation.26.clone.1 | convolution fusion | flops 75894784 | bytes 9962497 | tf_op jit(solution)/shard_map/while/body/eval_jaxpr/dot_general | solution.py:87
  43.2 8.6 %gather_fusion.2 = bf16[256,128,128]{2,1,0:T(8,128)(2,1)} fusion(bf16[32,128,128]{2,1,0:T(8,128)(2,1)S(1)} %get-tuple-element.325, s32[1024]{0:T(1024)S(1)} %pad_clamp_fusion.12), kind=kCustom, calls=%fused_computation.clone.clone.1 | custom fusion | bytes 16778240 | tf_op jit(solution)/shard_map/while/body/eval_jaxpr/jit(_take)/gather | solution.py:75
  51.8 4.4 %fusion.85 = f32[32,8,64,128]{3,2,1,0:T(8,128)S(1)} fusion(bf16[32,8,128,128]{3,2,1,0:T(8,128)(2,1)} %bitcast.138, pred[32,8]{1,0:T(8,128)(4,1)S(1)} %get-tuple-element.304, bf16[3,32,64,128]{3,2,1,0:T(8,128)(2,1)S(1)} %get-tuple-element.326, s32[]{:T(128)S(6)} %copy.49), kind=kOutput, calls=%fused_computation.35.clone.1 | convolution fusion | flops 541065216 | bytes 17305604 | tf_op jit(solution)/shard_map/while/body/eval_jaxpr/rzp,rkpq->rkzq/dot_general | solution.py:76
  56.2 4.5 %fusion.86 = f32[16,8192]{1,0:T(8,128)S(1)} fusion(f32[32,8,64,128]{3,2,1,0:T(8,128)S(1)} %fusion.85, s32[256]{0:T(256)S(1)} %eq.129), kind=kOutput, calls=%fused_computation.33.clone.1 | convolution fusion | flops 67112960 | bytes 8913920 | tf_op jit(solution)/shard_map/while/body/eval_jaxpr/dot_general | solution.py:86
  60.7 4.5 %fusion.87 = f32[16,8192]{1,0:T(8,128)S(1)} fusion(f32[16,8192]{1,0:T(8,128)S(1)} %fusion.86, f32[32,8,64,128]{3,2,1,0:T(8,128)S(1)} %fusion.85, f32[16,8192]{1,0:T(8,128)S(1)} %get-tuple-element.314, pred[]{:T(512)S(6)} %compare.281, s32[256]{0:T(256)S(1)} %eq.129), kind=kOutput, calls=%fused_computation.26.clone.1 | convolution fusion | flops 75894784 | bytes 9962497 | tf_op jit(solution)/shard_map/while/body/eval_jaxpr/dot_general | solution.py:87
  65.5 8.6 %gather_fusion.2 = bf16[256,128,128]{2,1,0:T(8,128)(2,1)} fusion(bf16[32,128,128]{2,1,0:T(8,128)(2,1)S(1)} %get-tuple-element.325, s32[1024]{0:T(1024)S(1)} %pad_clamp_fusion.12), kind=kCustom, calls=%fused_computation.clone.clone.1 | custom fusion | bytes 16778240 | tf_op jit(solution)/shard_map/while/body/eval_jaxpr/jit(_take)/gather | solution.py:75
  74.1 4.4 %fusion.85 = f32[32,8,64,128]{3,2,1,0:T(8,128)S(1)} fusion(bf16[32,8,128,128]{3,2,1,0:T(8,128)(2,1)} %bitcast.138, pred[32,8]{1,0:T(8,128)(4,1)S(1)} %get-tuple-element.304, bf16[3,32,64,128]{3,2,1,0:T(8,128)(2,1)S(1)} %get-tuple-element.326, s32[]{:T(128)S(6)} %copy.49), kind=kOutput, calls=%fused_computation.35.clone.1 | convolution fusion | flops 541065216 | bytes 17305604 | tf_op jit(solution)/shard_map/while/body/eval_jaxpr/rzp,rkpq->rkzq/dot_general | solution.py:76
  78.6 4.5 %fusion.86 = f32[16,8192]{1,0:T(8,128)S(1)} fusion(f32[32,8,64,128]{3,2,1,0:T(8,128)S(1)} %fusion.85, s32[256]{0:T(256)S(1)} %eq.129), kind=kOutput, calls=%fused_computation.33.clone.1 | convolution fusion | flops 67112960 | bytes 8913920 | tf_op jit(solution)/shard_map/while/body/eval_jaxpr/dot_general | solution.py:86
  83.0 4.5 %fusion.87 = f32[16,8192]{1,0:T(8,128)S(1)} fusion(f32[16,8192]{1,0:T(8,128)S(1)} %fusion.86, f32[32,8,64,128]{3,2,1,0:T(8,128)S(1)} %fusion.85, f32[16,8192]{1,0:T(8,128)S(1)} %get-tuple-element.314, pred[]{:T(512)S(6)} %compare.281, s32[256]{0:T(256)S(1)} %eq.129), kind=kOutput, calls=%fused_computation.26.clone.1 | convolution fusion | flops 75894784 | bytes 9962497 | tf_op jit(solution)/shard_map/while/body/eval_jaxpr/dot_general | solution.py:87
  87.8 0.9 gather_fusion.5
  88.7 0.2 copy.35
  88.9 1.2 fusion.46
  90.0 11.3 %all-to-all-start = ((f32[32,64,128]{2,1,0:T(8,128)}), f32[32,64,128]{2,1,0:T(8,128)S(1)}, u32[]{:S(2)}, u32[]{:S(2)}) async-start(f32[32,64,128]{2,1,0:T(8,128)} %fusion.46), calls=%async_computation | async-start | bytes 2097152 | tf_op jit(solution)/shard_map/all_to_all | solution.py:95
  101.4 0.7 fusion.69
  102.0 0.7 fusion.67
  102.7 0.7 fusion.66
  103.5 0.7 fusion.68
  104.2 40.4 %fusion.49 = s32[3072]{0:T(1024)S(1)} fusion(s32[3072,8]{0,1:T(8,128)S(1)} %copy-done.6, s32[]{:T(128)} %bitcast.9, s32[]{:T(128)} %bitcast.10, s32[]{:T(128)} %bitcast.11, s32[]{:T(128)} %bitcast.12, s32[]{:T(128)} %bitcast.13, s32[]{:T(128)} %bitcast.14, s32[]{:T(128)} %bitcast.15, s32[]{:T(128)} %bitcast.16, s32[]{:T(128)} %bitcast.17, s32[]{:T(128)} %bitcast.18, ...), kind=kLoop, calls=%fused_computation.83 | loop fusion | flops 3806208 | bytes 110852 | tf_op jit(solution)/shard_map/reduce_max | solution.py:98
  144.7 0.1 reduce_max.20
  145.0 0.1 fusion.58
  145.2 0.8 pad_maximum_fusion.5
  146.0 3.7 %collective-permute-start.3 = (f32[1,66,128]{2,1,0:T(8,128)S(1)}, f32[1,66,128]{2,1,0:T(8,128)S(1)}, u32[]{:S(2)}, u32[]{:S(2)}) collective-permute-start(f32[1,66,128]{2,1,0:T(8,128)S(1)} %get-tuple-element.150), channel_id=1, source_target_pairs={{0,1},{1,2},{2,3},{3,4},{4,5},{5,6},{6,7},{7,8},{8,9},{9,10},{10,1... | collective-permute-start | bytes 101384 | tf_op jit(solution)/shard_map/ppermute | solution.py:22
  149.7 1.3 collective-permute-start.2
  151.0 0.3 collective-permute-done.3
  151.3 2.3 maximum_maximum_fusion
  153.6 1.0 slice_subtract_fusion
  154.6 0.9 collective-permute-done.2
  155.5 1.6 copy-done.4
  157.1 0.7 copy-done.3
  157.8 7.2 %divide_select_fusion.2 = (f32[97,65,128]{2,1,0:T(8,128)}, f32[97,65,128]{2,1,0:T(8,128)}) fusion(pred[97,65]{1,0:T(8,128)(4,1)S(1)} %broadcast_and_fusion, f32[97,66,128]{2,1,0:T(8,128)S(1)} %maximum_maximum_fusion, f32[1,66,128]{2,1,0:T(8,128)S(1)} %collective-permute-done.2, f32[96,1,128]{2,1,0:T(1,128)S(1)} %collective-permute-done.1, ...), kind=kLoop, calls=%fused_computation.58 | loop fusion | flops 12105600 | bytes 19399872 | tf_op jit(solution)/shard_map/jit(_where)/select_n | solution.py:130
  165.0 0.2 select_reduce_fusion
  165.3 0.6 gather_fusion.6
  165.9 0.9 broadcast_select_fusion
  166.8 11.3 %all-to-all-start.1 = ((bf16[32,64,128]{2,1,0:T(8,128)(2,1)}), bf16[32,64,128]{2,1,0:T(8,128)(2,1)S(1)}, u32[]{:S(2)}, u32[]{:S(2)}) async-start(bf16[32,64,128]{2,1,0:T(8,128)(2,1)} %broadcast_select_fusion), calls=%async_computation.1 | async-start | bytes 1048576 | tf_op jit(solution)/shard_map/all_to_all | solution.py:102
  178.1 8.0 %divide_select_fusion.1 = (f32[97,65,128]{2,1,0:T(8,128)}, f32[97,65,128]{2,1,0:T(8,128)S(1)}) fusion(f32[97,65,128]{2,1,0:T(8,128)} %get-tuple-element.145, pred[97,65]{1,0:T(8,128)(4,1)S(1)} %broadcast_and_fusion, f32[97,66,128]{2,1,0:T(8,128)} %copy-done.2, pred[65]{0:T(512)(128)(4,1)S(1)} %get-tuple-element.217, f32[97,65,127]{2,1,0:T(8,128)} %copy-done.4), kind=kLoop, calls=%fused_computation.57 | loop fusion | flops 4842240 | bytes 19350110 | tf_op jit(solution)/shard_map/jit(_where)/select_n | solution.py:131
  186.1 1.8 copy-done.5
  188.0 2.2 slice.153
  190.2 4.7 %all-to-all-done.1 = bf16[32,64,128]{2,1,0:T(8,128)(2,1)S(1)} async-done(((bf16[32,64,128]{2,1,0:T(8,128)(2,1)}), bf16[32,64,128]{2,1,0:T(8,128)(2,1)S(1)}, u32[]{:S(2)}, u32[]{:S(2)}) %all-to-all-start.1) | async-done | bytes 524320 | tf_op jit(solution)/shard_map/all_to_all | solution.py:102
  195.0 57.6 %while.21 = (s32[]{:T(128)}, f32[3,32,64,128]{3,2,1,0:T(8,128)}, s32[3,32,8]{2,1,0:T(8,128)S(1)}, bf16[32,64,128]{2,1,0:T(8,128)(2,1)S(1)}, s32[3,32,8]{2,1,0:T(...) while((s32[]{:T(128)}, f32[3,32,64,128]{3,2,1,0:T(8,128)}, s32[3,32,8]{2,1,0:T(8,128)S(1)}, ...), condition=%wide.region_8.10_spmd, body=%wide.region_7.9_spmd.sunk | while | flops 543168256 | bytes 38819936 | solution.py:115
  195.2 3.1 %gather_fusion.1 = bf16[256,64,128]{2,1,0:T(8,128)(2,1)} fusion(bf16[32,64,128]{2,1,0:T(8,128)(2,1)S(1)} %get-tuple-element.346, s32[1024]{0:T(1024)S(1)} %pad_clamp_fusion.11), kind=kCustom, calls=%fused_computation.2.clone.1 | custom fusion | bytes 8389632 | tf_op jit(solution)/shard_map/while/body/eval_jaxpr/jit(_take)/gather | solution.py:109
  198.3 8.6 %gather_fusion = bf16[256,128,128]{2,1,0:T(8,128)(2,1)} fusion(bf16[32,128,128]{2,1,0:T(8,128)(2,1)S(1)} %get-tuple-element.348, s32[1024]{0:T(1024)S(1)} %pad_clamp_fusion.10), kind=kCustom, calls=%fused_computation.1.clone.clone.1 | custom fusion | bytes 16778240 | tf_op jit(solution)/shard_map/while/body/eval_jaxpr/jit(_take)/gather | solution.py:108
  206.9 7.3 %fusion.81 = f32[3,32,64,128]{3,2,1,0:T(8,128)} fusion(f32[3,32,64,128]{3,2,1,0:T(8,128)} %get-tuple-element.337, s32[]{:T(128)S(6)} %copy.55, bf16[32,8,128,128]{3,2,1,0:T(8,128)(2,1)} %bitcast.139, pred[32,8]{1,0:T(8,128)(4,1)S(1)} %get-tuple-element.295, bf16[32,8,64,128]{3,2,1,0:T(8,128)(2,1)} %bitcast.140, pred[32,8]{1,0:T(8,128)(4,1)S(1)} %get-tuple-element.296), kind=kOutput, calls=%fused_computation.16.clone.1 | convolution fusion | flops 543162368 | bytes 13632004 | tf_op jit(solution)/shard_map/while/body/eval_jaxpr/rkzq,rkpq->rzp/dot_general | solution.py:112
  214.4 3.1 %gather_fusion.1 = bf16[256,64,128]{2,1,0:T(8,128)(2,1)} fusion(bf16[32,64,128]{2,1,0:T(8,128)(2,1)S(1)} %get-tuple-element.346, s32[1024]{0:T(1024)S(1)} %pad_clamp_fusion.11), kind=kCustom, calls=%fused_computation.2.clone.1 | custom fusion | bytes 8389632 | tf_op jit(solution)/shard_map/while/body/eval_jaxpr/jit(_take)/gather | solution.py:109
  217.5 8.6 %gather_fusion = bf16[256,128,128]{2,1,0:T(8,128)(2,1)} fusion(bf16[32,128,128]{2,1,0:T(8,128)(2,1)S(1)} %get-tuple-element.348, s32[1024]{0:T(1024)S(1)} %pad_clamp_fusion.10), kind=kCustom, calls=%fused_computation.1.clone.clone.1 | custom fusion | bytes 16778240 | tf_op jit(solution)/shard_map/while/body/eval_jaxpr/jit(_take)/gather | solution.py:108
  226.1 7.3 %fusion.81 = f32[3,32,64,128]{3,2,1,0:T(8,128)} fusion(f32[3,32,64,128]{3,2,1,0:T(8,128)} %get-tuple-element.337, s32[]{:T(128)S(6)} %copy.55, bf16[32,8,128,128]{3,2,1,0:T(8,128)(2,1)} %bitcast.139, pred[32,8]{1,0:T(8,128)(4,1)S(1)} %get-tuple-element.295, bf16[32,8,64,128]{3,2,1,0:T(8,128)(2,1)} %bitcast.140, pred[32,8]{1,0:T(8,128)(4,1)S(1)} %get-tuple-element.296), kind=kOutput, calls=%fused_computation.16.clone.1 | convolution fusion | flops 543162368 | bytes 13632004 | tf_op jit(solution)/shard_map/while/body/eval_jaxpr/rkzq,rkpq->rzp/dot_general | solution.py:112
  233.6 3.1 %gather_fusion.1 = bf16[256,64,128]{2,1,0:T(8,128)(2,1)} fusion(bf16[32,64,128]{2,1,0:T(8,128)(2,1)S(1)} %get-tuple-element.346, s32[1024]{0:T(1024)S(1)} %pad_clamp_fusion.11), kind=kCustom, calls=%fused_computation.2.clone.1 | custom fusion | bytes 8389632 | tf_op jit(solution)/shard_map/while/body/eval_jaxpr/jit(_take)/gather | solution.py:109
  236.6 8.6 %gather_fusion = bf16[256,128,128]{2,1,0:T(8,128)(2,1)} fusion(bf16[32,128,128]{2,1,0:T(8,128)(2,1)S(1)} %get-tuple-element.348, s32[1024]{0:T(1024)S(1)} %pad_clamp_fusion.10), kind=kCustom, calls=%fused_computation.1.clone.clone.1 | custom fusion | bytes 16778240 | tf_op jit(solution)/shard_map/while/body/eval_jaxpr/jit(_take)/gather | solution.py:108
  245.3 7.3 %fusion.81 = f32[3,32,64,128]{3,2,1,0:T(8,128)} fusion(f32[3,32,64,128]{3,2,1,0:T(8,128)} %get-tuple-element.337, s32[]{:T(128)S(6)} %copy.55, bf16[32,8,128,128]{3,2,1,0:T(8,128)(2,1)} %bitcast.139, pred[32,8]{1,0:T(8,128)(4,1)S(1)} %get-tuple-element.295, bf16[32,8,64,128]{3,2,1,0:T(8,128)(2,1)} %bitcast.140, pred[32,8]{1,0:T(8,128)(4,1)S(1)} %get-tuple-element.296), kind=kOutput, calls=%fused_computation.16.clone.1 | convolution fusion | flops 543162368 | bytes 13632004 | tf_op jit(solution)/shard_map/while/body/eval_jaxpr/rkzq,rkpq->rzp/dot_general | solution.py:112
  252.6 11.4 %fusion.44 = f32[96,64,128]{2,1,0:T(8,128)} fusion(f32[96,64,128]{2,1,0:T(8,128)} %param.13, f32[97,65,128]{2,1,0:T(8,128)} %copy-done.5, f32[97,65,128]{2,1,0:T(8,128)} %get-tuple-element.147, f32[97,65,128]{2,1,0:T(8,128)} %get-tuple-element.144, f32[3,32,64,128]{3,2,1,0:T(8,128)} %get-tuple-element.76, f32[96,64,127]{2,1,0:T(8,128)} %slice.153), kind=kLoop, calls=%fused_computation.65 | loop fusion | flops 7077888 | bytes 28286976 | tf_op jit(solution)/shard_map/max | solution.py:137
  (81 shorter events, 2.3 us)
Async XLA Ops:
  0.0 9.7 %copy-start.6 = (s32[3072,8]{0,1:T(8,128)S(1)}, s32[3072,8]{0,1:T(8,128)}, u32[]{:S(2)}) copy-start(s32[3072,8]{0,1:T(8,128)} %param.16) | copy-start | bytes 294916
  0.0 10.0 %copy-start = (s32[64]{0:T(128)S(1)}, s32[64]{0:T(128)}, u32[]{:S(2)}) copy-start(s32[64]{0:T(128)} %param.17) | copy-start | bytes 772
  1.9 143.3 %collective-permute-start = (f32[96,1,128]{2,1,0:T(1,128)}, f32[96,1,128]{2,1,0:T(1,128)S(1)}, u32[]{:S(2)}, u32[]{:S(2)}) collective-permute-start(f32[96,1,128]{2,1,0:T(1,128)} %get-tuple-element.151), channel_id=1, source_target_pairs={{0,32},{32,64},{64,96},{96,128},{128,160},{160,192},{192,224},{1,3... | collective-permute-start | bytes 147464 | tf_op jit(solution)/shard_map/ppermute | solution.py:22
  3.8 141.4 %collective-permute-start.1 = (f32[96,1,128]{2,1,0:T(1,128)}, f32[96,1,128]{2,1,0:T(1,128)S(1)}, u32[]{:S(2)}, u32[]{:S(2)}) collective-permute-start(f32[96,1,128]{2,1,0:T(1,128)} %get-tuple-element.152), channel_id=1, source_target_pairs={{32,0},{64,32},{96,64},{128,96},{160,128},{192,160},{224,192},{33,... | collective-permute-start | bytes 147464 | tf_op jit(solution)/shard_map/ppermute | solution.py:24
  15.6 5.0 %copy-start.9 = (s32[96,8]{0,1:T(8,128)S(1)}, s32[96,8]{0,1:T(8,128)}, u32[]{:S(2)}) copy-start(s32[96,8]{0,1:T(8,128)} %param.15) | copy-start | bytes 9220
  15.6 5.1 %copy-start.1 = (bf16[32,128,128]{2,1,0:T(8,128)(2,1)S(1)}, bf16[32,128,128]{2,1,0:T(8,128)(2,1)}, u32[]{:S(2)}) copy-start(bf16[32,128,128]{2,1,0:T(8,128)(2,1)} %param.14) | copy-start | bytes 3145732
  90.0 75.0 %all-to-all-start = ((f32[32,64,128]{2,1,0:T(8,128)}), f32[32,64,128]{2,1,0:T(8,128)S(1)}, u32[]{:S(2)}, u32[]{:S(2)}) async-start(f32[32,64,128]{2,1,0:T(8,128)} %fusion.46), calls=%async_computation | async-start | bytes 2097152 | tf_op jit(solution)/shard_map/all_to_all | solution.py:95
  146.0 5.3 %collective-permute-start.3 = (f32[1,66,128]{2,1,0:T(8,128)S(1)}, f32[1,66,128]{2,1,0:T(8,128)S(1)}, u32[]{:S(2)}, u32[]{:S(2)}) collective-permute-start(f32[1,66,128]{2,1,0:T(8,128)S(1)} %get-tuple-element.150), channel_id=1, source_target_pairs={{0,1},{1,2},{2,3},{3,4},{4,5},{5,6},{6,7},{7,8},{8,9},{9,10},{10,1... | collective-permute-start | bytes 101384 | tf_op jit(solution)/shard_map/ppermute | solution.py:22
  149.7 5.9 %collective-permute-start.2 = (f32[1,66,128]{2,1,0:T(8,128)S(1)}, f32[1,66,128]{2,1,0:T(8,128)S(1)}, u32[]{:S(2)}, u32[]{:S(2)}) collective-permute-start(f32[1,66,128]{2,1,0:T(8,128)S(1)} %get-tuple-element.149), channel_id=1, source_target_pairs={{1,0},{2,1},{3,2},{4,3},{5,4},{6,5},{7,6},{8,7},{9,8},{10,9},{11,1... | collective-permute-start | bytes 101384 | tf_op jit(solution)/shard_map/ppermute | solution.py:24
  153.6 1.9 copy-start.2
  153.6 4.2 %copy-start.3 = (f32[96,64,128]{2,1,0:T(8,128)S(1)}, f32[96,64,128]{2,1,0:T(8,128)}, u32[]{:S(2)}) copy-start(f32[96,64,128]{2,1,0:T(8,128)} %param.13) | copy-start | bytes 9437188
  154.6 2.5 copy-start.4
  157.8 7.4 %copy-start.7 = (f32[2,64,128]{2,1,0:T(8,128)S(1)}, f32[2,64,128]{2,1,0:T(8,128)}, u32[]{:S(2)}) copy-start(f32[2,64,128]{2,1,0:T(8,128)} %param.19) | copy-start | bytes 196612
  157.8 7.4 %copy-start.8 = (f32[2,64,128]{2,1,0:T(8,128)S(1)}, f32[2,64,128]{2,1,0:T(8,128)}, u32[]{:S(2)}) copy-start(f32[2,64,128]{2,1,0:T(8,128)} %param.18) | copy-start | bytes 196612
  166.8 28.1 %all-to-all-start.1 = ((bf16[32,64,128]{2,1,0:T(8,128)(2,1)}), bf16[32,64,128]{2,1,0:T(8,128)(2,1)S(1)}, u32[]{:S(2)}, u32[]{:S(2)}) async-start(bf16[32,64,128]{2,1,0:T(8,128)(2,1)} %broadcast_select_fusion), calls=%async_computation.1 | async-start | bytes 1048576 | tf_op jit(solution)/shard_map/all_to_all | solution.py:102
  186.1 1.8 copy-start.5
where the time goes:
time: 265 us; the launch traced here: 264 us
  local copies, waits for them, and re-layouts  85.3 us (32%)
  other arithmetic  76.7 us (29%)
  matrix products  62.2 us (23%)
  starting transfers between devices  33.1 us (12%)
  waiting for transfers between devices  5.96 us (2%)
    reduce_max x2, other arithmetic, per_device(): jnp.max(jnp.where(owned_here, every_slot % owned_count, 0), axis=1)  40.5 us
    gather x3, local copies, waits for them, and re-layouts, project(): stencil = jnp.take(footprints, offsets, axis=0)  25.8 us
    gather x3, local copies, waits for them, and re-layouts, backproject(): stencil = jnp.take(footprints, offsets, axis=0)  25.8 us
    dot_general x3, matrix products, backproject(): jnp.einsum('rkzq,rkpq->rzp', values, stencil, preferred_element_type=jnp....  21.9 us
    dot_general x3, matrix products, project(): lax.dot_general(selector, low, dims, preferred_element_type=jnp.float32)  13.6 us
    dot_general x3, matrix products, project(): lax.dot_general(selector, high, dims, preferred_element_type=jnp.float32)  13.4 us
    dot_general x3, matrix products, project(): jnp.einsum('rzp,rkpq->rkzq', pixels, stencil, preferred_element_type=jnp....  13.2 us
    max x1, other arithmetic, per_device(): return jnp.maximum(updated, 0.0)  11.4 us
  transfers between devices with their start and end apart: 6, of which 3 were waited for; matrix products, arithmetic and copies ran while one was open for 56% of the time, Pallas kernels for 0%

commit v1 on v0

v1 whole, which is shorter than its diff:
```python
import functools

import jax
import jax.numpy as jnp
from jax import lax
from jax.experimental import pallas as pl
from jax.experimental.pallas import tpu as pltpu
from jax.sharding import PartitionSpec as P

smoothing = 0.04
step_length = 2.0
variation_weight = 1.0
lanes = 128

F32 = jnp.float32
BF16 = jnp.bfloat16
VMEM = pl.BlockSpec(memory_space=pltpu.VMEM)
SMEM = pl.BlockSpec(memory_space=pltpu.SMEM)
ANY = pl.BlockSpec(memory_space=pl.ANY)


def iota(shape, dim):
    return lax.broadcasted_iota(jnp.int32, shape, dim)


def forward_kernel(
    touch, owned, ray_slot, blocks, foots, volume, prints,
    sent, table, counts, head, tail,
    rows_buf, prints_buf, grouped, sums, table_buf, sems, table_sem, prints_sem,
):
    row_count, slice_count, pixels = volume.shape
    foot_count = prints.shape[0]
    owners = sent.shape[0]
    crossings = blocks.shape[0]
    chunk_count = sems.shape[0]
    depth = slice_count // chunk_count
    copies = []
    for c in range(chunk_count):
        span = pl.ds(c * depth, depth)
        copies.append(
            pltpu.make_async_copy(
                volume.at[:, span, :],
                rows_buf.reshape(row_count, slice_count, pixels).at[:, span, :],
                sems.at[c],
            )
        )
        copies[c].start()
    prints_copy = pltpu.make_async_copy(prints, prints_buf, prints_sem)
    prints_copy.start()

    position = lax.axis_index("tile")
    offset = position * row_count
    limit = blocks.shape[1] - 2 * lanes
    base = jnp.minimum((offset // lanes) * lanes, limit)
    window = blocks[:, pl.ds(pl.multiple_of(base, lanes), 2 * lanes)]
    mine = pltpu.roll(window, 2 * lanes - (offset - base), 1)[:, :lanes]
    slot = jnp.zeros_like(mine)
    for b in range(ray_slot.shape[0]):
        slot = jnp.where(mine == b, ray_slot[b], slot)
    valid = iota((crossings, lanes), 1) < row_count
    owner = jnp.where(valid, slot // owned, -1)
    label = iota((owners, lanes), 0)
    present = jnp.zeros((owners, lanes), F32)
    for k in range(crossings):
        present = jnp.where(owner[k : k + 1] == label, 1.0, present)
    present = jnp.broadcast_to(jnp.max(present, axis=1, keepdims=True), (owners, lanes))
    lower = (iota((owners, owners), 1) < iota((owners, owners), 0)).astype(BF16)
    rank = jnp.dot(lower, present.astype(BF16), preferred_element_type=F32)
    column = iota((owners, lanes), 1)
    rank_row = jnp.sum(jnp.where(label < column, present, 0.0), axis=0, keepdims=True)
    present_row = jnp.sum(jnp.where(label == column, present, 0.0), axis=0, keepdims=True)
    row = jnp.where(present_row > 0.5, rank_row, -1.0).astype(jnp.int32)
    table_buf[...] = jnp.broadcast_to(row, table_buf.shape)
    table_copy = pltpu.make_async_copy(table_buf, table, table_sem)
    table_copy.start()

    code_row = iota((foot_count * touch, lanes), 0)
    total = jnp.zeros((foot_count * touch, lanes), F32)
    foots_here = jnp.concatenate(
        [foots[...], jnp.zeros((crossings, lanes - row_count), jnp.int32)], axis=1
    )
    for k in range(crossings):
        place = jnp.sum(
            jnp.where(owner[k : k + 1] == label, rank, 0.0), axis=0, keepdims=True
        ).astype(jnp.int32)
        code = jnp.where(valid[k : k + 1], foots_here[k : k + 1] * touch + place, -1)
        total = total + jnp.where(code_row == code, 1.0, 0.0)
    counts[...] = total.astype(BF16)

    for c in range(chunk_count):
        copies[c].wait()

        @pl.loop(0, depth // 2)
        def _(i, c=c):
            z = c * depth + 2 * i
            pair = jnp.concatenate(
                [
                    rows_buf[pl.ds(z, row_count, stride=slice_count), :],
                    rows_buf[pl.ds(z + 1, row_count, stride=slice_count), :],
                ],
                axis=1,
            ).astype(BF16)
            group = jnp.dot(counts[:, :row_count], pair, preferred_element_type=F32).astype(BF16)
            for half in range(2):
                for f in range(foot_count):
                    grouped[
                        pl.ds(pl.multiple_of((z + half) * touch, touch), touch),
                        f * pixels : (f + 1) * pixels,
                    ] = group[f * touch : (f + 1) * touch, half * pixels : (half + 1) * pixels]

    head[...] = rows_buf[pl.ds(0, row_count, stride=slice_count), :]
    tail[...] = rows_buf[pl.ds(slice_count - 1, row_count, stride=slice_count), :]
    prints_copy.wait()
    step = 256

    @pl.loop(0, slice_count * touch // step)
    def _(m):
        span = pl.ds(pl.multiple_of(m * step, step), step)
        sums[span, :] = jnp.dot(
            grouped[span, :],
            prints_buf[...].reshape(foot_count * pixels, -1),
            preferred_element_type=F32,
        )

    table_copy.wait()
    for t in range(owners):
        place = table[0, t]
        block = sums[pl.ds(jnp.maximum(place, 0), slice_count, stride=touch), :]
        sent[t] = jnp.where(place >= 0, block, 0.0).astype(BF16)


def forward(touch, owned, owners, ray_slot, blocks, foots, volume, prints):
    rows, slices, pixels = volume.shape
    foot_count, _, rays = prints.shape
    chunks = 4
    return pl.pallas_call(
        functools.partial(forward_kernel, touch, owned),
        out_shape=(
            jax.ShapeDtypeStruct((owners, slices, rays), BF16),
            jax.ShapeDtypeStruct((8, lanes), jnp.int32),
            jax.ShapeDtypeStruct((foot_count * touch, lanes), BF16),
            jax.ShapeDtypeStruct((rows, pixels), F32),
            jax.ShapeDtypeStruct((rows, pixels), F32),
        ),
        in_specs=[SMEM, VMEM, VMEM, ANY, ANY],
        out_specs=(VMEM, SMEM, VMEM, VMEM, VMEM),
        scratch_shapes=[
            pltpu.VMEM((rows * slices, pixels), F32),
            pltpu.VMEM(prints.shape, BF16),
            pltpu.VMEM((slices * touch, foot_count * pixels), BF16),
            pltpu.VMEM((slices * touch, rays), F32),
            pltpu.VMEM((8, lanes), jnp.int32),
            pltpu.SemaphoreType.DMA((chunks,)),
            pltpu.SemaphoreType.DMA,
            pltpu.SemaphoreType.DMA,
        ],
        name="forward",
    )(ray_slot, blocks, foots, volume, prints)


def middle_kernel(
    owned, ray_slot, blocks, volume, before_slice, after_slice, before_row, after_row, counts,
    prints,
    base, turned, counts_turned, picks,
    slice_flux,
):
    rows, slices, pixels = volume.shape
    position = lax.axis_index("tile")
    layer = lax.axis_index("slab")
    last_position = lax.axis_size("tile") - 1
    last_layer = lax.axis_size("slab") - 1
    lane = iota((1, pixels), 1)
    inner = lane < pixels - 1
    first = lane == 0

    def col_grad(x):
        return jnp.where(inner, pltpu.roll(x, pixels - 1, 1) - x, 0.0)

    def scale(a, b, c):
        return lax.rsqrt(a * a + b * b + c * c + smoothing)

    low = before_slice[...]
    low_next = jnp.concatenate([low[1:], after_row[0:1]], axis=0)
    grad_rows = low_next - low
    row_id = iota((rows, 1), 0)
    grad_rows = jnp.where((row_id == rows - 1) & (position == last_position), 0.0, grad_rows)
    grad_slices = volume.reshape(rows * slices, pixels)[pl.ds(0, rows, stride=slices), :] - low
    flux = grad_slices * scale(grad_rows, grad_slices, col_grad(low))
    slice_flux[...] = jnp.where(layer == 0, 0.0, flux)

    z_id = iota((slices, 1), 0)
    top = z_id == slices - 1
    bottom = z_id == 0
    top_edge = top & (layer == last_layer)

    def fluxes(here, next_row, beyond, last):
        up = pltpu.roll(here, slices - 1, 0)
        up = jnp.where(top, beyond, up)
        grad_slices = jnp.where(top_edge, 0.0, up - here)
        grad_rows = jnp.where(last, 0.0, next_row - here)
        grad_cols = col_grad(here)
        inverse = scale(grad_rows, grad_slices, grad_cols)
        return grad_rows * inverse, grad_slices * inverse, grad_cols * inverse

    start, _, _ = fluxes(
        before_row[1 : slices + 1], volume[0], before_row[slices + 1 : slices + 2], False
    )
    start = jnp.where(position == 0, 0.0, start)

    def one(r, here, next_row, previous, last):
        flux_rows, flux_slices, flux_cols = fluxes(
            here, next_row, after_slice[pl.ds(r, 1), :], last
        )
        below = pltpu.roll(flux_slices, 1, 0)
        below = jnp.where(bottom, slice_flux[pl.ds(r, 1), :], below)
        left = jnp.where(first, 0.0, pltpu.roll(flux_cols, 1, 1))
        variation = (previous - flux_rows) + (below - flux_slices) + (left - flux_cols)
        base[r] = here - (step_length * variation_weight) * variation
        return flux_rows

    final = lax.fori_loop(
        0, rows - 1, lambda r, previous: one(r, volume[r], volume[r + 1], previous, False), start
    )
    one(rows - 1, volume[rows - 1], after_row[1 : slices + 1], final, position == last_position)

    @pl.loop(0, prints.shape[0])
    def _(f):
        turned[f] = prints[f].astype(F32).T.astype(BF16)

    counts_turned[...] = counts[...].astype(F32).T[:rows].astype(BF16)

    owners = picks.shape[0]
    width = blocks.shape[1]
    second = jnp.int32(0)
    for b in range(ray_slot.shape[0]):
        second = jnp.where(ray_slot[b] == position * owned + 1, b, second)
    hit = jnp.max(jnp.where(blocks[...] == second, 1.0, 0.0), axis=0, keepdims=True)
    member = (iota((owners, width), 1) // rows == iota((owners, width), 0)).astype(BF16)
    count = lax.dot_general(
        member,
        jnp.broadcast_to(hit, (lanes, width)).astype(BF16),
        (((1,), (1,)), ((), ())),
        preferred_element_type=F32,
    )
    picks[...] = jnp.where(count > 0.5, 1.0, 0.0)


def middle(owned, owners, ray_slot, blocks, volume, halos, counts, prints):
    rows, slices, pixels = volume.shape
    return pl.pallas_call(
        functools.partial(middle_kernel, owned),
        out_shape=(
            jax.ShapeDtypeStruct(volume.shape, F32),
            jax.ShapeDtypeStruct((prints.shape[0], prints.shape[2], prints.shape[1]), BF16),
            jax.ShapeDtypeStruct((rows, counts.shape[0]), BF16),
            jax.ShapeDtypeStruct((owners, lanes), F32),
        ),
        in_specs=[SMEM] + [VMEM] * 8,
        out_specs=(VMEM,) * 4,
        scratch_shapes=[pltpu.VMEM((rows, pixels), F32)],
        name="middle",
    )(ray_slot, blocks, volume, *halos, counts, prints)


def residual_kernel(arrived, picks, measured, weights, returned, second):
    owners = arrived.shape[0]
    sums = [jnp.zeros(measured.shape[1:], F32) for _ in range(2)]
    for j in range(owners):
        part = arrived[j].astype(F32)
        chosen = picks[j : j + 1, :] > 0.5
        sums[0] = sums[0] + jnp.where(chosen, 0.0, part)
        sums[1] = sums[1] + jnp.where(chosen, part, 0.0)
    out = [(weights[i] * (sums[i] - measured[i])).astype(BF16).astype(F32) for i in range(2)]
    for j in range(owners):
        returned[j] = jnp.where(picks[j : j + 1, :] > 0.5, out[1], out[0]).astype(BF16)


def residual(arrived, picks, measured, weights):
    return pl.pallas_call(
        residual_kernel,
        out_shape=jax.ShapeDtypeStruct(arrived.shape, BF16),
        in_specs=[VMEM] * 4,
        out_specs=VMEM,
        scratch_shapes=[pltpu.VMEM((8, lanes), F32)],
        name="residual",
    )(arrived, picks, measured, weights)


def backward_kernel(
    touch, table, returned, turned, counts_turned, base, out, gathered, spread, out_buf, sems
):
    rows, slices, pixels = base.shape
    owners = returned.shape[0]
    foot_count = turned.shape[0]
    codes = foot_count * touch
    gathered[...] = jnp.zeros_like(gathered)
    for t in range(owners):
        place = table[0, t]

        @pl.when(place >= 0)
        def _(t=t, place=place):
            gathered[pl.ds(place, slices, stride=touch), :] = returned[t].astype(F32)

    step = 256
    deep = step // touch

    @pl.loop(0, slices * touch // step)
    def _(m):
        part = gathered[pl.ds(pl.multiple_of(m * step, step), step), :].astype(BF16)
        for f in range(0, foot_count, 2):
            wide = jnp.concatenate([turned[f], turned[f + 1]], axis=1)
            value = jnp.dot(part, wide, preferred_element_type=F32).astype(BF16)
            for i in range(deep):
                for g in range(2):
                    row = (m * (deep // 2) + i // 2) * codes + (f + g) * touch
                    spread[
                        pl.ds(pl.multiple_of(row, touch), touch),
                        (i % 2) * pixels : (i % 2 + 1) * pixels,
                    ] = value[i * touch : (i + 1) * touch, g * pixels : (g + 1) * pixels]

    base_flat = base.reshape(rows * slices, pixels)
    chunk_count = sems.shape[0]
    depth = slices // chunk_count
    copies = []
    for c in range(chunk_count):

        @pl.loop(0, depth // 2)
        def _(i, c=c):
            z = c * depth + 2 * i
            row = (c * (depth // 2) + i) * codes
            grad = jnp.dot(
                counts_turned[...],
                spread[pl.ds(pl.multiple_of(row, codes), codes), :],
                preferred_element_type=F32,
            )
            for g in range(2):
                span = pl.ds(z + g, rows, stride=slices)
                out_buf[span, :] = jnp.maximum(
                    base_flat[span, :] - step_length * grad[:, g * pixels : (g + 1) * pixels], 0.0
                )

        span = pl.ds(c * depth, depth)
        copies.append(
            pltpu.make_async_copy(
                out_buf.reshape(rows, slices, pixels).at[:, span, :],
                out.at[:, span, :],
                sems.at[c],
            )
        )
        copies[c].start()
    for copy in copies:
        copy.wait()


def backward(touch, table, returned, turned, counts_turned, base):
    rows, slices, pixels = base.shape
    codes = turned.shape[0] * touch
    chunks = 4
    return pl.pallas_call(
        functools.partial(backward_kernel, touch),
        out_shape=jax.ShapeDtypeStruct(base.shape, F32),
        in_specs=[SMEM] + [VMEM] * 4,
        out_specs=ANY,
        scratch_shapes=[
            pltpu.VMEM((slices * touch, pixels), F32),
            pltpu.VMEM((slices // 2 * codes, 2 * pixels), BF16),
            pltpu.VMEM((rows * slices, pixels), F32),
            pltpu.SemaphoreType.DMA((chunks,)),
        ],
        name="backward",
    )(table, returned, turned, counts_turned, base)


def shifted(x, axis, forward_way):
    count = lax.axis_size(axis)
    if forward_way:
        pairs = [(i, i + 1) for i in range(count - 1)]
    else:
        pairs = [(i + 1, i) for i in range(count - 1)]
    return lax.ppermute(x, axis, pairs)


def per_device(volume, footprints, foot_index, ray_block, ray_slot, measured, weights):
    row_count, slice_count, pixels = volume.shape
    owners = lax.axis_size("tile")
    owned = measured.shape[0]
    touch = owners // 2
    blocks = ray_block.T
    sent, table, counts, head, tail = forward(
        touch, owned, owners, ray_slot, blocks, foot_index.T, volume, footprints
    )
    before_slice = shifted(tail, "slab", True)
    after_slice = shifted(head, "slab", False)
    arrived = lax.all_to_all(sent, "tile", split_axis=0, concat_axis=0, tiled=True)

    def edge(r):
        return jnp.concatenate(
            [before_slice[r : r + 1], volume[r], after_slice[r : r + 1]], axis=0
        )

    before_row = shifted(edge(row_count - 1), "tile", True)
    after_row = shifted(edge(0), "tile", False)
    base, turned, counts_turned, picks = middle(
        owned, owners, ray_slot, blocks, volume,
        (before_slice, after_slice, before_row, after_row), counts, footprints,
    )
    answer = residual(arrived, picks, measured, weights)
    returned = lax.all_to_all(answer, "tile", split_axis=0, concat_axis=0, tiled=True)
    return backward(touch, table, returned, turned, counts_turned, base)


def solution(mesh):
    in_specs = (
        P("tile", "slab", None),
        P(),
        P("tile", None),
        P(),
        P(),
        P("tile", "slab", None),
        P("tile", "slab", None),
    )
    out_specs = P("tile", "slab", None)
    return jax.shard_map(
        per_device, mesh=mesh, in_specs=in_specs, out_specs=out_specs, check_vma=False
    )
```

time: 265 us -> 115 us (0.43)
  local copies, waits for them, and re-layouts: 85.3 us -> 2.19 us
  other arithmetic: 76.7 us -> 0.02 us
  matrix products: 62.2 us -> 0 us
  Pallas kernels: 0 us -> 54.5 us
  blocking collectives: 0 us -> 30.1 us
  starting transfers between devices: 33.1 us -> 21.9 us
    gather x19 -> x0, local copies, waits for them, and re-layouts: 75 us -> none  [the longest x3 25.8 us: project(): stencil = jnp.take(footprints, offsets, axis=0)]
    dot_general x12 -> x0, matrix products: 62.2 us -> none  [the longest x3 21.9 us: backproject(): jnp.einsum('rkzq,rkpq->rzp', values, stencil, preferred_element_type=jnp....]
    pallas_call x0 -> x4, Pallas kernels: none -> 54.5 us  [the longest x1 23.2 us: middle(): pl.pallas_call(functools.partial(middle_kernel, owned), out_shape=(jax.Sh...]
    reduce_max x2 -> x0, other arithmetic: 40.5 us -> none  [per_device(): jnp.max(jnp.where(owned_here, every_slot % owned_count, 0), axis=1)]
    all_to_all x0 -> x1, blocking collectives: none -> 30.1 us  [per_device(): lax.all_to_all(answer, 'tile', split_axis=0, concat_axis=0, tiled=True)]
    select_n x14 -> x0, other arithmetic: 17.6 us -> none  [the longest x1 8.03 us: per_device(): flux_slices = jnp.where(inside, flux_slices, 0.0)]
    max x1 -> x0, other arithmetic: 11.4 us -> none  [per_device(): return jnp.maximum(updated, 0.0)]
    all_to_all x2 -> x1, starting transfers between devices: 22.6 us -> 11.3 us  [per_device(): lax.all_to_all(sent, 'tile', split_axis=0, concat_axis=0, tiled=True)]
  transfers between devices with their start and end apart: 6 -> 5, of which waited for: 3 -> 3; matrix products, arithmetic and copies ran while one was open for 56% -> 1% of each run, Pallas kernels for 0% -> 20%
where the time goes in v1:
time: 115 us
  Pallas kernels  54.5 us (47%)
  blocking collectives  30.1 us (26%)
  starting transfers between devices  21.9 us (19%)
  waiting for transfers between devices  5.79 us (5%)
  local copies, waits for them, and re-layouts  2.19 us (2%)
    all_to_all x1, blocking collectives, per_device(): lax.all_to_all(answer, 'tile', split_axis=0, concat_axis=0, tiled=True)  30.1 us
    pallas_call x1, Pallas kernels, middle(): pl.pallas_call(functools.partial(middle_kernel, owned), out_shape=(jax.Sh...  23.2 us
    pallas_call x1, Pallas kernels, forward(): pl.pallas_call(functools.partial(forward_kernel, touch, owned), out_shape...  15.1 us
    pallas_call x1, Pallas kernels, backward(): pl.pallas_call(functools.partial(backward_kernel, touch), out_shape=jax.S...  14.1 us
    all_to_all x1, starting transfers between devices, per_device(): lax.all_to_all(sent, 'tile', split_axis=0, concat_axis=0, tiled=True)  11.3 us
    ppermute x4, starting transfers between devices, shifted(): return lax.ppermute(x, axis, pairs)  10.5 us
    ppermute x4, waiting for transfers between devices, shifted(): return lax.ppermute(x, axis, pairs)  5.79 us
  transfers between devices with their start and end apart: 5, of which 3 were waited for; matrix products, arithmetic and copies ran while one was open for 1% of the time, Pallas kernels for 20%

profile of v1, /device:TPU:8, one launch (start us, length us, event | category | flops | bytes accessed | tf_op | source)
XLA Modules:
  0.0 114.5 jit_solution(14327354024757370574)
XLA Ops:
  0.0 15.1 %forward.1 = (bf16[32,64,128]{2,1,0:T(8,128)(2,1)}, s32[8,128]{1,0:T(8,128)}, bf16[512,128]{1,0:T(8,128)(2,1)}, f32[96,128]{1,0:T(8,128)}, f32[96,128]{1,0:T(8,128)}) custom-call(s32[64]{0:T(128)} %ray_slot.3, s32[8,3072]{1,0:T(8,128)} %bitcast.6, s32[8,96]{1,0:T(8,128)} %bitcast.8, f32[96,64,128]{2,1,0:T(8,128)} %volume.3, bf16[32,128,128]{2,1,0:T(8,128)(2,1)} %prints.3), custom_call_target="tpu_custom_call" | custom-call | tf_op jit(solution)/shard_map/forward/pallas_call | solution.py:136
  15.1 11.3 %all-to-all-start = ((bf16[32,64,128]{2,1,0:T(8,128)(2,1)}), bf16[32,64,128]{2,1,0:T(8,128)(2,1)S(1)}, u32[]{:S(2)}, u32[]{:S(2)}) async-start(bf16[32,64,128]{2,1,0:T(8,128)(2,1)} %get-tuple-element.15), calls=%async_computation | async-start | bytes 1048576 | tf_op jit(solution)/shard_map/all_to_all | solution.py:394
  26.4 1.9 %collective-permute-start = (f32[96,128]{1,0:T(8,128)}, f32[96,128]{1,0:T(8,128)S(1)}, u32[]{:S(2)}, u32[]{:S(2)}) collective-permute-start(f32[96,128]{1,0:T(8,128)} %get-tuple-element.16), channel_id=1, source_target_pairs={{0,32},{32,64},{64,96},{96,128},{128,160},{160,192},{192,224},{1,3... | collective-permute-start | bytes 147464 | tf_op jit(solution)/shard_map/ppermute | solution.py:380
  28.3 3.6 %collective-permute-start.1 = (f32[96,128]{1,0:T(8,128)}, f32[96,128]{1,0:T(8,128)S(1)}, u32[]{:S(2)}, u32[]{:S(2)}) collective-permute-start(f32[96,128]{1,0:T(8,128)} %get-tuple-element.17), channel_id=1, source_target_pairs={{32,0},{64,32},{96,64},{128,96},{160,128},{192,160},{224,192},{33,... | collective-permute-start | bytes 147464 | tf_op jit(solution)/shard_map/ppermute | solution.py:380
  32.0 0.8 slice_bitcast_fusion
  32.8 0.0 collective-permute-done.before_slice
  32.8 0.0 copy-start.1
  32.8 1.2 %collective-permute-done.1.after_slice = f32[96,128]{1,0:T(8,128)S(1)} collective-permute-done((f32[96,128]{1,0:T(8,128)}, f32[96,128]{1,0:T(8,128)S(1)}, u32[]{:S(2)}, u32[]{:S(2)}) %collective-permute-start.1) | collective-permute-done | bytes 49184 | tf_op jit(solution)/shard_map/ppermute | solution.py:380
  34.0 0.0 copy-start.2
  34.0 3.7 %collective-permute-start.2 = (f32[66,128]{1,0:T(8,128)S(1)}, f32[66,128]{1,0:T(8,128)S(1)}, u32[]{:S(2)}, u32[]{:S(2)}) collective-permute-start(f32[66,128]{1,0:T(8,128)S(1)} %pad_maximum_fusion), channel_id=1, source_target_pairs={{0,1},{1,2},{2,3},{3,4},{4,5},{5,6},{6,7},{7,8},{8,9},{9,10},{10,1... | collective-permute-start | bytes 101384 | tf_op jit(solution)/shard_map/ppermute | solution.py:380
  37.8 1.3 %collective-permute-start.3 = (f32[66,128]{1,0:T(8,128)S(1)}, f32[66,128]{1,0:T(8,128)S(1)}, u32[]{:S(2)}, u32[]{:S(2)}) collective-permute-start(f32[66,128]{1,0:T(8,128)S(1)} %pad_maximum_fusion.1), channel_id=1, source_target_pairs={{1,0},{2,1},{3,2},{4,3},{5,4},{6,5},{7,6},{8,7},{9,8},{10,9},{11,1... | collective-permute-start | bytes 101384 | tf_op jit(solution)/shard_map/ppermute | solution.py:380
  39.1 0.3 collective-permute-done.2.before_row
  39.4 0.0 copy-start.3
  39.4 4.3 %collective-permute-done.3.after_row = f32[66,128]{1,0:T(8,128)S(1)} collective-permute-done((f32[66,128]{1,0:T(8,128)S(1)}, f32[66,128]{1,0:T(8,128)S(1)}, u32[]{:S(2)}, u32[]{:S(2)}) %collective-permute-start.3) | collective-permute-done | bytes 33824 | tf_op jit(solution)/shard_map/ppermute | solution.py:380
  43.6 0.0 copy-start.4
  43.6 0.0 copy-done.1
  43.6 0.0 copy-done.2
  43.6 0.0 copy-done.3
  43.6 0.6 copy-done.4
  44.2 23.2 %middle.1 = (f32[96,64,128]{2,1,0:T(8,128)}, bf16[32,128,128]{2,1,0:T(8,128)(2,1)}, bf16[96,512]{1,0:T(8,128)(2,1)}, f32[32,128]{1,0:T(8,128)}) custom-call(s32[64]{0:T(128)} %ray_slot.3, s32[8,3072]{1,0:T(8,128)} %bitcast.7, f32[96,64,128]{2,1,0:T(8,128)} %volume.3, f32[96,128]{1,0:T(8,128)} %copy-done.1, f32[96,128]{1,0:T(8,128)} %copy-done.2, ...), custom_call_target="tpu_custom_call" | custom-call | tf_op jit(solution)/shard_map/middle/pallas_call | solution.py:250
  67.4 0.0 all-to-all-done.arrived
  67.4 0.0 copy-start
  67.5 0.8 copy-done
  68.2 2.1 %residual.1 = bf16[32,64,128]{2,1,0:T(8,128)(2,1)} custom-call(bf16[32,64,128]{2,1,0:T(8,128)(2,1)} %copy-done, f32[32,128]{1,0:T(8,128)} %get-tuple-element.19.picks, f32[2,64,128]{2,1,0:T(8,128)} %measured.1, f32[2,64,128]{2,1,0:T(8,128)} %weights.1), custom_call_target="tpu_custom_call" | custom-call | tf_op jit(solution)/shard_map/residual/pallas_call | solution.py:279
  70.4 30.1 %all_to_all.10.returned = bf16[32,64,128]{2,1,0:T(8,128)(2,1)} all-to-all(bf16[32,64,128]{2,1,0:T(8,128)(2,1)} %residual.1), channel_id=1, replica_groups=mesh['slab'=8,'tile'=32] {'tile'}, dimensions={0} | all-to-all | bytes 1048576 | tf_op jit(solution)/shard_map/all_to_all | solution.py:408
  100.4 14.1 %backward.1 = f32[96,64,128]{2,1,0:T(8,128)} custom-call(s32[8,128]{1,0:T(8,128)} %get-tuple-element.14.table, bf16[32,64,128]{2,1,0:T(8,128)(2,1)} %all_to_all.10.returned, bf16[32,128,128]{2,1,0:T(8,128)(2,1)} %get-tuple-element.20.turned, bf16[96,512]{1,0:T(8,128)(2,1)} %get-tuple-element.21.counts_turned, f32[96,64,128]{2,1,0:T(8,128)} %get-tuple-element.22.base), custom_call_target="tpu_custom_call" | custom-call | tf_op jit(solution)/shard_map/backward/pallas_call | solution.py:359
  (4 shorter events, 0.0 us)
Async XLA Ops:
  15.1 52.4 %all-to-all-start = ((bf16[32,64,128]{2,1,0:T(8,128)(2,1)}), bf16[32,64,128]{2,1,0:T(8,128)(2,1)S(1)}, u32[]{:S(2)}, u32[]{:S(2)}) async-start(bf16[32,64,128]{2,1,0:T(8,128)(2,1)} %get-tuple-element.15), calls=%async_computation | async-start | bytes 1048576 | tf_op jit(solution)/shard_map/all_to_all | solution.py:394
  26.4 6.4 %collective-permute-start = (f32[96,128]{1,0:T(8,128)}, f32[96,128]{1,0:T(8,128)S(1)}, u32[]{:S(2)}, u32[]{:S(2)}) collective-permute-start(f32[96,128]{1,0:T(8,128)} %get-tuple-element.16), channel_id=1, source_target_pairs={{0,32},{32,64},{64,96},{96,128},{128,160},{160,192},{192,224},{1,3... | collective-permute-start | bytes 147464 | tf_op jit(solution)/shard_map/ppermute | solution.py:380
  28.3 5.7 %collective-permute-start.1 = (f32[96,128]{1,0:T(8,128)}, f32[96,128]{1,0:T(8,128)S(1)}, u32[]{:S(2)}, u32[]{:S(2)}) collective-permute-start(f32[96,128]{1,0:T(8,128)} %get-tuple-element.17), channel_id=1, source_target_pairs={{32,0},{64,32},{96,64},{128,96},{160,128},{192,160},{224,192},{33,... | collective-permute-start | bytes 147464 | tf_op jit(solution)/shard_map/ppermute | solution.py:380
  32.8 10.9 %copy-start.1 = (f32[96,128]{1,0:T(8,128)}, f32[96,128]{1,0:T(8,128)S(1)}, u32[]{:S(2)}) copy-start(f32[96,128]{1,0:T(8,128)S(1)} %collective-permute-done.before_slice) | copy-start | bytes 147460
  34.0 9.6 %copy-start.2 = (f32[96,128]{1,0:T(8,128)}, f32[96,128]{1,0:T(8,128)S(1)}, u32[]{:S(2)}) copy-start(f32[96,128]{1,0:T(8,128)S(1)} %collective-permute-done.1.after_slice) | copy-start | bytes 147460
  34.0 5.3 %collective-permute-start.2 = (f32[66,128]{1,0:T(8,128)S(1)}, f32[66,128]{1,0:T(8,128)S(1)}, u32[]{:S(2)}, u32[]{:S(2)}) collective-permute-start(f32[66,128]{1,0:T(8,128)S(1)} %pad_maximum_fusion), channel_id=1, source_target_pairs={{0,1},{1,2},{2,3},{3,4},{4,5},{5,6},{6,7},{7,8},{8,9},{9,10},{10,1... | collective-permute-start | bytes 101384 | tf_op jit(solution)/shard_map/ppermute | solution.py:380
  37.8 5.9 %collective-permute-start.3 = (f32[66,128]{1,0:T(8,128)S(1)}, f32[66,128]{1,0:T(8,128)S(1)}, u32[]{:S(2)}, u32[]{:S(2)}) collective-permute-start(f32[66,128]{1,0:T(8,128)S(1)} %pad_maximum_fusion.1), channel_id=1, source_target_pairs={{1,0},{2,1},{3,2},{4,3},{5,4},{6,5},{7,6},{8,7},{9,8},{10,9},{11,1... | collective-permute-start | bytes 101384 | tf_op jit(solution)/shard_map/ppermute | solution.py:380
  39.4 4.3 %copy-start.3 = (f32[66,128]{1,0:T(8,128)}, f32[66,128]{1,0:T(8,128)S(1)}, u32[]{:S(2)}) copy-start(f32[66,128]{1,0:T(8,128)S(1)} %collective-permute-done.2.before_row) | copy-start | bytes 101380
  43.6 0.6 copy-start.4
  67.4 0.8 copy-start

commit v2 on v1

v2 whole, which is shorter than its diff:
```python
import functools

import jax
import jax.numpy as jnp
from jax import lax
from jax.experimental import pallas as pl
from jax.experimental.pallas import tpu as pltpu
from jax.sharding import PartitionSpec as P

smoothing = 0.04
step_length = 2.0
variation_weight = 1.0
lanes = 128

F32 = jnp.float32
BF16 = jnp.bfloat16
VMEM = pl.BlockSpec(memory_space=pltpu.VMEM)
SMEM = pl.BlockSpec(memory_space=pltpu.SMEM)
HBM = pl.BlockSpec(memory_space=pltpu.HBM)


def in_hbm(*arrays):
    return [pltpu.with_memory_space_constraint(x, pltpu.HBM) for x in arrays]


def iota(shape, dim):
    return lax.broadcasted_iota(jnp.int32, shape, dim)


def forward_kernel(
    touch, owned, ray_slot, blocks, foots, volume, prints,
    sent, table, counts, head, tail,
    window, foots_buf, slot_buf, by_slice, prints_buf, grouped, sums, compact, table_buf,
    sems, small_sems, table_sem, prints_sem,
):
    row_count, slice_count, pixels = volume.shape
    foot_count = prints.shape[0]
    owners = sent.shape[0]
    crossings = blocks.shape[0]

    def slice_copy(z):
        return pltpu.make_async_copy(volume.at[:, z, :], by_slice.at[z], sems.at[z])

    position = lax.axis_index("tile")
    offset = position * row_count
    limit = blocks.shape[1] - 2 * lanes
    base = jnp.minimum((offset // lanes) * lanes, limit)
    small = [
        pltpu.make_async_copy(source, target, small_sems.at[i])
        for i, (source, target) in enumerate(
            [
                (blocks.at[:, pl.ds(pl.multiple_of(base, lanes), 2 * lanes)], window),
                (foots, foots_buf),
                (ray_slot, slot_buf),
            ]
        )
    ]
    for copy in small:
        copy.start()
    for z in range(slice_count):
        slice_copy(z).start()
    prints_copy = pltpu.make_async_copy(prints, prints_buf, prints_sem)
    prints_copy.start()

    for copy in small:
        copy.wait()
    mine = pltpu.roll(window[...], 2 * lanes - (offset - base), 1)[:, :lanes]
    slot = jnp.zeros_like(mine)
    for b in range(ray_slot.shape[0]):
        slot = jnp.where(mine == b, slot_buf[b], slot)
    valid = iota((crossings, lanes), 1) < row_count
    owner = jnp.where(valid, slot // owned, -1)
    label = iota((owners, lanes), 0)
    present = jnp.zeros((owners, lanes), F32)
    for k in range(crossings):
        present = jnp.where(owner[k : k + 1] == label, 1.0, present)
    present = jnp.broadcast_to(jnp.max(present, axis=1, keepdims=True), (owners, lanes))
    lower = (iota((owners, owners), 1) < iota((owners, owners), 0)).astype(BF16)
    rank = jnp.dot(lower, present.astype(BF16), preferred_element_type=F32)
    column = iota((owners, lanes), 1)
    rank_row = jnp.sum(jnp.where(label < column, present, 0.0), axis=0, keepdims=True)
    present_row = jnp.sum(jnp.where(label == column, present, 0.0), axis=0, keepdims=True)
    rank_row = jnp.where(present_row > 0.5, rank_row, -1.0).astype(jnp.int32)
    match = jnp.where((rank.astype(jnp.int32) == column) & (present > 0.5), label + 1, 0)
    owner_row = jnp.sum(match, axis=0, keepdims=True) - 1
    table_buf[...] = jnp.where(iota(table_buf.shape, 0) == 0, rank_row, owner_row)
    table_copy = pltpu.make_async_copy(table_buf, table, table_sem)
    table_copy.start()

    foots_here = jnp.concatenate(
        [foots_buf[...], jnp.zeros((crossings, lanes - row_count), jnp.int32)], axis=1
    )
    codes = []
    for k in range(crossings):
        place = jnp.sum(
            jnp.where(owner[k : k + 1] == label, rank, 0.0), axis=0, keepdims=True
        ).astype(jnp.int32)
        codes.append(jnp.where(valid[k : k + 1], foots_here[k : k + 1] * touch + place, -1))
    part = 4 * touch
    for first in range(0, foot_count * touch, part):
        code_row = iota((part, lanes), 0) + first
        total = jnp.zeros((part, lanes), F32)
        for code in codes:
            total = total + jnp.where(code_row == code, 1.0, 0.0)
        counts[first : first + part] = total.astype(BF16)

    group_size = 4

    @pl.loop(0, slice_count // group_size)
    def _(i):
        for j in range(group_size):
            slice_copy(i * group_size + j).wait()
        for j in range(0, group_size, 2):
            z = i * group_size + j
            pair = jnp.concatenate([by_slice[z], by_slice[z + 1]], axis=1).astype(BF16)
            group = jnp.dot(counts[:, :row_count], pair, preferred_element_type=F32).astype(BF16)
            for half in range(2):
                for f in range(foot_count):
                    grouped[
                        f // 2,
                        pl.ds(pl.multiple_of((z + half) * touch, touch), touch),
                        (f % 2) * pixels : (f % 2 + 1) * pixels,
                    ] = group[f * touch : (f + 1) * touch, half * pixels : (half + 1) * pixels]

    head[...] = by_slice[0]
    tail[...] = by_slice[slice_count - 1]
    prints_copy.wait()
    sums[...] = jnp.zeros_like(sums)

    @pl.loop(0, foot_count // 4)
    def _(g):
        block = 256
        for m in range(0, slice_count * touch, block):
            span = slice(m, m + block)
            total = sums[span]
            for h in range(2):
                weight = prints_buf[pl.ds(4 * g + 2 * h, 2)].reshape(2 * pixels, -1)
                total = total + jnp.dot(
                    grouped[2 * g + h, span], weight, preferred_element_type=F32
                )
            sums[span] = total

    compact[...] = jnp.swapaxes(sums[...].reshape(slice_count, touch, -1), 0, 1).astype(BF16)
    table_copy.wait()
    for t in range(owners):
        place = table[0, t]
        block = compact[jnp.maximum(place, 0)]
        sent[t] = jnp.where(place >= 0, block, jnp.zeros_like(block))


def forward(touch, owned, owners, ray_slot, blocks, foots, volume, prints):
    rows, slices, pixels = volume.shape
    foot_count, _, rays = prints.shape
    return pl.pallas_call(
        functools.partial(forward_kernel, touch, owned),
        out_shape=(
            jax.ShapeDtypeStruct((owners, slices, rays), BF16),
            jax.ShapeDtypeStruct((8, lanes), jnp.int32),
            jax.ShapeDtypeStruct((foot_count * touch, lanes), BF16),
            jax.ShapeDtypeStruct((rows, pixels), F32),
            jax.ShapeDtypeStruct((rows, pixels), F32),
        ),
        in_specs=[HBM] * 5,
        out_specs=(VMEM, SMEM, VMEM, VMEM, VMEM),
        scratch_shapes=[
            pltpu.VMEM((blocks.shape[0], 2 * lanes), jnp.int32),
            pltpu.VMEM(foots.shape, jnp.int32),
            pltpu.SMEM(ray_slot.shape, jnp.int32),
            pltpu.VMEM((slices, rows, pixels), F32),
            pltpu.VMEM(prints.shape, BF16),
            pltpu.VMEM((foot_count // 2, slices * touch, 2 * pixels), BF16),
            pltpu.VMEM((slices * touch, rays), F32),
            pltpu.VMEM((touch, slices, rays), BF16),
            pltpu.VMEM((8, lanes), jnp.int32),
            pltpu.SemaphoreType.DMA((slices,)),
            pltpu.SemaphoreType.DMA((3,)),
            pltpu.SemaphoreType.DMA,
            pltpu.SemaphoreType.DMA,
        ],
        compiler_params=pltpu.CompilerParams(vmem_limit_bytes=24 << 20),
        name="forward",
    )(*in_hbm(ray_slot, blocks, foots, volume, prints))


def tables_kernel(owned, ray_slot, blocks, counts, counts_turned, picks):
    position = lax.axis_index("tile")
    rows = counts_turned.shape[0]

    counts_turned[...] = counts[...].astype(F32).T[:rows].astype(BF16)

    owners = picks.shape[0]
    width = blocks.shape[1]
    second = jnp.int32(0)
    for b in range(ray_slot.shape[0]):
        second = jnp.where(ray_slot[b] == position * owned + 1, b, second)
    hit = jnp.max(jnp.where(blocks[...] == second, 1.0, 0.0), axis=0, keepdims=True)
    start = iota((owners, width), 0) * rows
    at = iota((owners, width), 1)
    member = ((at >= start) & (at < start + rows)).astype(BF16)
    count = lax.dot_general(
        member,
        jnp.broadcast_to(hit, (lanes, width)).astype(BF16),
        (((1,), (1,)), ((), ())),
        preferred_element_type=F32,
    )
    picks[...] = jnp.where(count > 0.5, 1.0, 0.0)


def tables(owned, owners, rows, ray_slot, blocks, counts):
    return pl.pallas_call(
        functools.partial(tables_kernel, owned),
        out_shape=(
            jax.ShapeDtypeStruct((rows, counts.shape[0]), BF16),
            jax.ShapeDtypeStruct((owners, lanes), F32),
        ),
        in_specs=[SMEM] + [VMEM] * 2,
        out_specs=(VMEM,) * 2,
        compiler_params=pltpu.CompilerParams(vmem_limit_bytes=8 << 20),
        name="tables",
    )(ray_slot, blocks, counts)


def variation_kernel(
    volume, before_slice, after_slice, before_row, after_row, first_row,
    base, by_slice, row_flux, sems,
):
    slices, rows, pixels = base.shape

    def slice_copy(z):
        return pltpu.make_async_copy(volume.at[:, z, :], by_slice.at[z], sems.at[z])

    for z in range(slices):
        slice_copy(z).start()
    position = lax.axis_index("tile")
    layer = lax.axis_index("slab")
    last_position = lax.axis_size("tile") - 1
    last_layer = lax.axis_size("slab") - 1
    lane = iota((1, pixels), 1)
    inner = lane < pixels - 1
    first = lane == 0

    def col_grad(x):
        return jnp.where(inner, pltpu.roll(x, pixels - 1, 1) - x, 0.0)

    def scale(a, b, c):
        return lax.rsqrt(a * a + b * b + c * c + smoothing)

    low = before_row[1 : slices + 1]
    z_id = iota((slices, 1), 0)
    grad_slices = before_row[2 : slices + 2] - low
    grad_slices = jnp.where((z_id == slices - 1) & (layer == last_layer), 0.0, grad_slices)
    grad_rows = first_row[...] - low
    flux = grad_rows * scale(grad_rows, grad_slices, col_grad(low))
    row_flux[...] = jnp.where(position == 0, 0.0, flux)

    row_id = iota((rows, 1), 0)
    top = row_id == rows - 1
    bottom = row_id == 0
    keep = jnp.where(top & (position == last_position), 0.0, 1.0)

    def fluxes(here, next_slice, beyond, last):
        up = jnp.where(top, beyond, pltpu.roll(here, rows - 1, 0))
        grad_rows = (up - here) * keep
        grad_slices = jnp.where(last, 0.0, next_slice - here)
        grad_cols = col_grad(here)
        inverse = scale(grad_rows, grad_slices, grad_cols)
        return grad_rows * inverse, grad_slices * inverse, grad_cols * inverse

    slice_copy(0).wait()
    _, start, _ = fluxes(before_slice[...], by_slice[0], after_row[0:1], False)
    start = jnp.where(layer == 0, 0.0, start)

    def one(z, here, next_slice, previous, last):
        flux_rows, flux_slices, flux_cols = fluxes(
            here, next_slice, after_row[pl.ds(z + 1, 1), :], last
        )
        below = jnp.where(bottom, row_flux[pl.ds(z, 1), :], pltpu.roll(flux_rows, 1, 0))
        left = jnp.where(first, 0.0, pltpu.roll(flux_cols, 1, 1))
        variation = (previous - flux_slices) + (below - flux_rows) + (left - flux_cols)
        base[z] = here - (step_length * variation_weight) * variation
        return flux_slices

    def step(z, previous):
        slice_copy(z + 1).wait()
        return one(z, by_slice[z], by_slice[z + 1], previous, False)

    final = lax.fori_loop(0, slices - 1, step, start)
    one(slices - 1, by_slice[slices - 1], after_slice[...], final, layer == last_layer)


def variation(volume, *halos):
    rows, slices, pixels = volume.shape
    return pl.pallas_call(
        variation_kernel,
        out_shape=jax.ShapeDtypeStruct((slices, rows, pixels), F32),
        in_specs=[HBM] + [VMEM] * 5,
        out_specs=VMEM,
        scratch_shapes=[
            pltpu.VMEM((slices, rows, pixels), F32),
            pltpu.VMEM((slices, pixels), F32),
            pltpu.SemaphoreType.DMA((slices,)),
        ],
        compiler_params=pltpu.CompilerParams(vmem_limit_bytes=8 << 20),
        name="variation",
    )(*in_hbm(volume), *halos)


def residual_kernel(arrived, picks, measured, weights, returned):
    owners = arrived.shape[0]
    sums = [jnp.zeros(measured.shape[1:], F32) for _ in range(2)]
    for j in range(owners):
        part = arrived[j].astype(F32)
        chosen = picks[j : j + 1, :] > 0.5
        sums[0] = sums[0] + jnp.where(chosen, 0.0, part)
        sums[1] = sums[1] + jnp.where(chosen, part, 0.0)
    out = [(weights[i] * (sums[i] - measured[i])).astype(BF16).astype(F32) for i in range(2)]
    for j in range(owners):
        returned[j] = jnp.where(picks[j : j + 1, :] > 0.5, out[1], out[0]).astype(BF16)


def residual(arrived, picks, measured, weights):
    return pl.pallas_call(
        residual_kernel,
        out_shape=jax.ShapeDtypeStruct(arrived.shape, BF16),
        in_specs=[VMEM] * 4,
        out_specs=VMEM,
        compiler_params=pltpu.CompilerParams(vmem_limit_bytes=4 << 20),
        name="residual",
    )(arrived, picks, measured, weights)


def backward_kernel(
    touch, table, returned, prints, counts_turned, base,
    out, gathered, mixed, spread, out_buf, sems,
):
    slices, rows, pixels = base.shape
    foot_count, _, rays = prints.shape
    codes = foot_count * touch
    for s in range(touch):
        owner = table[1, s]
        block = returned[jnp.maximum(owner, 0)].astype(F32)
        gathered[s] = jnp.where(owner >= 0, block, 0.0)
    mixed[...] = jnp.swapaxes(gathered[...], 0, 1).reshape(slices * touch, rays).astype(BF16)
    deep = 16

    @pl.loop(0, foot_count // 4)
    def _(g):
        for f in range(0, 4, 2):
            wide = prints[pl.ds(4 * g + f, 2)].reshape(2 * pixels, rays)
            for z in range(0, slices, deep):
                value = lax.dot_general(
                    mixed[z * touch : (z + deep) * touch, :],
                    wide,
                    (((1,), (1,)), ((), ())),
                    preferred_element_type=F32,
                ).astype(BF16)
                for i in range(deep):
                    for h in range(2):
                        row = (4 * g + f + h) * touch
                        spread[
                            (z + i) // 2,
                            pl.ds(pl.multiple_of(row, touch), touch),
                            (i % 2) * pixels : (i % 2 + 1) * pixels,
                        ] = value[i * touch : (i + 1) * touch, h * pixels : (h + 1) * pixels]

    def slice_copy(z):
        return pltpu.make_async_copy(out_buf.at[z], out.at[:, z, :], sems.at[z])

    group_size = 4

    @pl.loop(0, slices // group_size)
    def _(i):
        for j in range(0, group_size, 2):
            z = i * group_size + j
            grad = jnp.dot(
                counts_turned[...],
                spread[i * (group_size // 2) + j // 2],
                preferred_element_type=F32,
            )
            for g in range(2):
                out_buf[z + g] = jnp.maximum(
                    base[z + g] - step_length * grad[:, g * pixels : (g + 1) * pixels], 0.0
                )
        for j in range(group_size):
            slice_copy(i * group_size + j).start()

    @pl.loop(0, slices)
    def _(z):
        slice_copy(z).wait()


def backward(touch, table, returned, prints, counts_turned, base):
    slices, rows, pixels = base.shape
    codes = prints.shape[0] * touch
    return pl.pallas_call(
        functools.partial(backward_kernel, touch),
        out_shape=jax.ShapeDtypeStruct((rows, slices, pixels), F32),
        in_specs=[SMEM] + [VMEM] * 4,
        out_specs=HBM,
        scratch_shapes=[
            pltpu.VMEM((touch, slices, prints.shape[2]), F32),
            pltpu.VMEM((slices * touch, prints.shape[2]), BF16),
            pltpu.VMEM((slices // 2, codes, 2 * pixels), BF16),
            pltpu.VMEM((slices, rows, pixels), F32),
            pltpu.SemaphoreType.DMA((slices,)),
        ],
        compiler_params=pltpu.CompilerParams(vmem_limit_bytes=24 << 20),
        name="backward",
    )(table, returned, prints, counts_turned, base)


def shifted(x, axis, forward_way):
    count = lax.axis_size(axis)
    if forward_way:
        pairs = [(i, i + 1) for i in range(count - 1)]
    else:
        pairs = [(i + 1, i) for i in range(count - 1)]
    return lax.ppermute(x, axis, pairs)


def per_device(volume, footprints, foot_index, ray_block, ray_slot, measured, weights):
    row_count, slice_count, pixels = volume.shape
    owners = lax.axis_size("tile")
    owned = measured.shape[0]
    touch = owners // 2
    blocks = ray_block.T
    sent, table, counts, head, tail = forward(
        touch, owned, owners, ray_slot, blocks, foot_index.T, volume, footprints
    )
    before_slice = shifted(tail, "slab", True)
    after_slice = shifted(head, "slab", False)
    arrived = lax.all_to_all(sent, "tile", split_axis=0, concat_axis=0, tiled=True)
    counts_turned, picks = tables(owned, owners, row_count, ray_slot, blocks, counts)

    def edge(r):
        return jnp.concatenate(
            [before_slice[r : r + 1], volume[r], after_slice[r : r + 1]], axis=0
        )

    first_edge, last_edge = edge(0), edge(row_count - 1)
    before_row = shifted(last_edge, "tile", True)
    after_row = shifted(first_edge, "tile", False)
    arrived, before_row, after_row = lax.optimization_barrier((arrived, before_row, after_row))
    answer = residual(arrived, picks, measured, weights)
    returned = lax.all_to_all(answer, "tile", split_axis=0, concat_axis=0, tiled=True)
    halos, _ = lax.optimization_barrier(
        ((before_slice, after_slice, before_row, after_row, volume[0]), answer)
    )
    base = variation(volume, *halos)
    return backward(touch, table, returned, footprints, counts_turned, base)


def solution(mesh):
    in_specs = (
        P("tile", "slab", None),
        P(),
        P("tile", None),
        P(),
        P(),
        P("tile", "slab", None),
        P("tile", "slab", None),
    )
    out_specs = P("tile", "slab", None)
    return jax.shard_map(
        per_device, mesh=mesh, in_specs=in_specs, out_specs=out_specs, check_vma=False
    )
```

time: 115 us -> 84.2 us (0.73)
  blocking collectives: 30.1 us -> 0 us
  Pallas kernels: 54.5 us -> 37.2 us
  starting transfers between devices: 21.9 us -> 33.5 us
  waiting for transfers between devices: 5.79 us -> 10.8 us
    all_to_all x1 -> x0, blocking collectives: 30.1 us -> none  [per_device(): lax.all_to_all(answer, 'tile', split_axis=0, concat_axis=0, tiled=True)]
    all_to_all x0 -> x1, starting transfers between devices: none -> 10.8 us  [per_device(): lax.all_to_all(answer, 'tile', split_axis=0, concat_axis=0, tiled=True)]
    pallas_call x1 -> x2, Pallas kernels: 23.2 us -> 13.2 us  [the longest x1 12.3 us: variation(): pl.pallas_call(variation_kernel, out_shape=jax.ShapeDtypeStruct((slices,...]
    all_to_all x0 -> x1, waiting for transfers between devices: none -> 6.2 us  [per_device(): lax.all_to_all(answer, 'tile', split_axis=0, concat_axis=0, tiled=True)]
    pallas_call x1, Pallas kernels: 14.1 us -> 9.75 us  [backward(): pl.pallas_call(functools.partial(backward_kernel, touch), out_shape=jax.S...]
    ppermute x4, waiting for transfers between devices: 5.79 us -> 1.56 us  [shifted(): return lax.ppermute(x, axis, pairs)]
    all_to_all x1, waiting for transfers between devices: 0.01 us -> 3.02 us  [per_device(): lax.all_to_all(sent, 'tile', split_axis=0, concat_axis=0, tiled=True)]
    pallas_call x1, Pallas kernels: 15.1 us -> 13.2 us  [forward(): pl.pallas_call(functools.partial(forward_kernel, touch, owned), out_shape...]
  transfers between devices with their start and end apart: 5 -> 6, of which waited for: 3 -> 4; matrix products, arithmetic and copies ran while one was open for 1% -> 1% of each run, Pallas kernels for 20% -> 16%
where the time goes in v2:
time: 84.2 us; the launch traced here: 83.6 us
  Pallas kernels  37.2 us (44%)
  starting transfers between devices  33.5 us (40%)
  waiting for transfers between devices  10.8 us (13%)
  local copies, waits for them, and re-layouts  2.03 us (2%)
    pallas_call x1, Pallas kernels, forward(): pl.pallas_call(functools.partial(forward_kernel, touch, owned), out_shape...  13.2 us
    pallas_call x1, Pallas kernels, variation(): pl.pallas_call(variation_kernel, out_shape=jax.ShapeDtypeStruct((slices,...  12.3 us
    ppermute x4, starting transfers between devices, shifted(): return lax.ppermute(x, axis, pairs)  11.4 us
    all_to_all x1, starting transfers between devices, per_device(): lax.all_to_all(sent, 'tile', split_axis=0, concat_axis=0, tiled=True)  11.3 us
    all_to_all x1, starting transfers between devices, per_device(): lax.all_to_all(answer, 'tile', split_axis=0, concat_axis=0, tiled=True)  10.8 us
    pallas_call x1, Pallas kernels, backward(): pl.pallas_call(functools.partial(backward_kernel, touch), out_shape=jax.S...  9.75 us
    all_to_all x1, waiting for transfers between devices, per_device(): lax.all_to_all(answer, 'tile', split_axis=0, concat_axis=0, tiled=True)  6.2 us
    all_to_all x1, waiting for transfers between devices, per_device(): lax.all_to_all(sent, 'tile', split_axis=0, concat_axis=0, tiled=True)  3.02 us
  transfers between devices with their start and end apart: 6, of which 4 were waited for; matrix products, arithmetic and copies ran while one was open for 1% of the time, Pallas kernels for 16%

profile of v2, /device:TPU:8, one launch (start us, length us, event | category | flops | bytes accessed | tf_op | source)
XLA Modules:
  0.0 83.6 jit_solution(6072206332969222544)
XLA Ops:
  0.0 0.0 copy-start.4
  0.0 0.0 copy-start.1
  0.0 0.0 copy-start.3
  0.0 0.0 copy-start.2
  0.0 13.2 %forward.1 = (bf16[32,64,128]{2,1,0:T(8,128)(2,1)}, s32[8,128]{1,0:T(8,128)S(1)}, bf16[512,128]{1,0:T(8,128)(2,1)S(1)}, f32[96,128]{1,0:T(8,128)S(1)}, f32[96,128]{1,0:T(8,128)S(1)}) custom-call(s32[64]{0:T(128)} %ray_slot.3, s32[8,3072]{1,0:T(8,128)} %bitcast.6, s32[8,96]{1,0:T(8,128)} %bitcast.8, f32[96,64,128]{2,1,0:T(8,128)} %volume.3, ...), custom_call_target="tpu_custom_call" | custom-call | tf_op jit(solution)/shard_map/forward/pallas_call | solution.py:154
  13.2 11.3 %all-to-all-start = ((bf16[32,64,128]{2,1,0:T(8,128)(2,1)}), bf16[32,64,128]{2,1,0:T(8,128)(2,1)S(1)}, u32[]{:S(2)}, u32[]{:S(2)}) async-start(bf16[32,64,128]{2,1,0:T(8,128)(2,1)} %get-tuple-element.21), calls=%async_computation | async-start | bytes 1048576 | tf_op jit(solution)/shard_map/all_to_all | solution.py:432
  24.5 1.9 %collective-permute-start = (f32[96,128]{1,0:T(8,128)S(1)}, f32[96,128]{1,0:T(8,128)S(1)}, u32[]{:S(2)}, u32[]{:S(2)}) collective-permute-start(f32[96,128]{1,0:T(8,128)S(1)} %get-tuple-element.22), channel_id=1, source_target_pairs={{0,32},{32,64},{64,96},{96,128},{128,160},{160,192},{192,224},{1,3... | collective-permute-start | bytes 147464 | tf_op jit(solution)/shard_map/ppermute | solution.py:418
  26.5 3.6 %collective-permute-start.1 = (f32[96,128]{1,0:T(8,128)S(1)}, f32[96,128]{1,0:T(8,128)S(1)}, u32[]{:S(2)}, u32[]{:S(2)}) collective-permute-start(f32[96,128]{1,0:T(8,128)S(1)} %get-tuple-element.23), channel_id=1, source_target_pairs={{32,0},{64,32},{96,64},{128,96},{160,128},{192,160},{224,192},{33,... | collective-permute-start | bytes 147464 | tf_op jit(solution)/shard_map/ppermute | solution.py:418
  30.1 0.8 slice_bitcast_fusion
  30.9 0.0 collective-permute-done.before_slice
  30.9 0.9 %collective-permute-done.1.after_slice = f32[96,128]{1,0:T(8,128)S(1)} collective-permute-done((f32[96,128]{1,0:T(8,128)S(1)}, f32[96,128]{1,0:T(8,128)S(1)}, u32[]{:S(2)}, u32[]{:S(2)}) %collective-permute-start.1) | collective-permute-done | bytes 49184 | tf_op jit(solution)/shard_map/ppermute | solution.py:418
  31.8 1.3 %collective-permute-start.3 = (f32[66,128]{1,0:T(8,128)S(1)}, f32[66,128]{1,0:T(8,128)S(1)}, u32[]{:S(2)}, u32[]{:S(2)}) collective-permute-start(f32[66,128]{1,0:T(8,128)S(1)} %pad_maximum_fusion.1), channel_id=1, source_target_pairs={{1,0},{2,1},{3,2},{4,3},{5,4},{6,5},{7,6},{8,7},{9,8},{10,9},{11,1... | collective-permute-start | bytes 101384 | tf_op jit(solution)/shard_map/ppermute | solution.py:418
  33.2 4.5 %collective-permute-start.2 = (f32[66,128]{1,0:T(8,128)S(1)}, f32[66,128]{1,0:T(8,128)S(1)}, u32[]{:S(2)}, u32[]{:S(2)}) collective-permute-start(f32[66,128]{1,0:T(8,128)S(1)} %pad_maximum_fusion), channel_id=1, source_target_pairs={{0,1},{1,2},{2,3},{3,4},{4,5},{5,6},{6,7},{7,8},{8,9},{9,10},{10,1... | collective-permute-start | bytes 101384 | tf_op jit(solution)/shard_map/ppermute | solution.py:418
  37.7 0.0 copy-done.4
  37.7 0.0 copy-done.1
  37.7 1.0 %tables.1 = (bf16[96,512]{1,0:T(8,128)(2,1)S(1)}, f32[32,128]{1,0:T(8,128)S(1)}) custom-call(s32[64]{0:T(128)S(1)} %copy-done.4, s32[8,3072]{1,0:T(8,128)S(1)} %bitcast.7, bf16[512,128]{1,0:T(8,128)(2,1)S(1)} %get-tuple-element.25.counts), custom_call_target="tpu_custom_call" | custom-call | tf_op jit(solution)/shard_map/tables/pallas_call | solution.py:210
  38.7 0.0 collective-permute-done.3.after_row
  38.7 0.6 collective-permute-done.2.before_row
  39.3 3.0 %all-to-all-done.arrived = bf16[32,64,128]{2,1,0:T(8,128)(2,1)S(1)} async-done(((bf16[32,64,128]{2,1,0:T(8,128)(2,1)}), bf16[32,64,128]{2,1,0:T(8,128)(2,1)S(1)}, u32[]{:S(2)}, u32[]{:S(2)}) %all-to-all-start) | async-done | bytes 524320 | tf_op jit(solution)/shard_map/all_to_all | solution.py:432
  42.4 0.0 copy-done.3
  42.4 0.0 copy-done.2
  42.4 1.1 %residual.1 = bf16[32,64,128]{2,1,0:T(8,128)(2,1)} custom-call(bf16[32,64,128]{2,1,0:T(8,128)(2,1)S(1)} %all-to-all-done.arrived, f32[32,128]{1,0:T(8,128)S(1)} %get-tuple-element.26.picks, f32[2,64,128]{2,1,0:T(8,128)S(1)} %copy-done.2, f32[2,64,128]{2,1,0:T(8,128)S(1)} %copy-done.3), custom_call_target="tpu_custom_call" | custom-call | tf_op jit(solution)/shard_map/residual/pallas_call | solution.py:322
  43.4 10.8 %all-to-all-start.1 = ((bf16[32,64,128]{2,1,0:T(8,128)(2,1)}), bf16[32,64,128]{2,1,0:T(8,128)(2,1)}, u32[]{:S(2)}, u32[]{:S(2)}) async-start(bf16[32,64,128]{2,1,0:T(8,128)(2,1)} %residual.1), calls=%async_computation.1 | async-start | bytes 1048576 | tf_op jit(solution)/shard_map/all_to_all | solution.py:445
  54.2 12.3 %variation.1.base = f32[64,96,128]{2,1,0:T(8,128)S(1)} custom-call(f32[96,64,128]{2,1,0:T(8,128)} %volume.3, f32[96,128]{1,0:T(8,128)S(1)} %collective-permute-done.before_slice, f32[96,128]{1,0:T(8,128)S(1)} %collective-permute-done.1.after_slice, f32[66,128]{1,0:T(8,128)S(1)} %collective-permute-done.2.before_row, ...), custom_call_target="tpu_custom_call" | custom-call | tf_op jit(solution)/shard_map/variation/pallas_call | solution.py:293
  66.5 6.2 %all-to-all-done.1.returned = bf16[32,64,128]{2,1,0:T(8,128)(2,1)} async-done(((bf16[32,64,128]{2,1,0:T(8,128)(2,1)}), bf16[32,64,128]{2,1,0:T(8,128)(2,1)}, u32[]{:S(2)}, u32[]{:S(2)}) %all-to-all-start.1) | async-done | bytes 524320 | tf_op jit(solution)/shard_map/all_to_all | solution.py:445
  72.7 0.0 copy-start
  72.7 1.2 %copy-done = bf16[32,128,128]{2,1,0:T(8,128)(2,1)S(1)} copy-done((bf16[32,128,128]{2,1,0:T(8,128)(2,1)S(1)}, bf16[32,128,128]{2,1,0:T(8,128)(2,1)}, u32[]{:S(2)}) %copy-start) | copy-done | bytes 1048600
  73.9 9.7 %backward.1 = f32[96,64,128]{2,1,0:T(8,128)} custom-call(s32[8,128]{1,0:T(8,128)S(1)} %get-tuple-element.20.table, bf16[32,64,128]{2,1,0:T(8,128)(2,1)} %all-to-all-done.1.returned, bf16[32,128,128]{2,1,0:T(8,128)(2,1)S(1)} %copy-done, bf16[96,512]{1,0:T(8,128)(2,1)S(1)} %get-tuple-element.27.counts_turned, f32[64,96,128]{2,1,0:T(8,128)S(1)} %variation.1.base), custom_call_target="tpu_custom_call" | custom-call | tf_op jit(solution)/shard_map/backward/pallas_call | solution.py:395
  (4 shorter events, 0.0 us)
Async XLA Ops:
  0.0 37.7 %copy-start.4 = (s32[64]{0:T(128)S(1)}, s32[64]{0:T(128)}, u32[]{:S(2)}) copy-start(s32[64]{0:T(128)} %ray_slot.3) | copy-start | bytes 772
  0.0 37.7 %copy-start.1 = (s32[3072,8]{0,1:T(8,128)S(1)}, s32[3072,8]{0,1:T(8,128)}, u32[]{:S(2)}) copy-start(s32[3072,8]{0,1:T(8,128)} %param.10) | copy-start | bytes 294916
  0.0 42.4 %copy-start.3 = (f32[2,64,128]{2,1,0:T(8,128)S(1)}, f32[2,64,128]{2,1,0:T(8,128)}, u32[]{:S(2)}) copy-start(f32[2,64,128]{2,1,0:T(8,128)} %weights.1) | copy-start | bytes 196612
  0.0 42.4 %copy-start.2 = (f32[2,64,128]{2,1,0:T(8,128)S(1)}, f32[2,64,128]{2,1,0:T(8,128)}, u32[]{:S(2)}) copy-start(f32[2,64,128]{2,1,0:T(8,128)} %measured.1) | copy-start | bytes 196612
  13.2 29.2 %all-to-all-start = ((bf16[32,64,128]{2,1,0:T(8,128)(2,1)}), bf16[32,64,128]{2,1,0:T(8,128)(2,1)S(1)}, u32[]{:S(2)}, u32[]{:S(2)}) async-start(bf16[32,64,128]{2,1,0:T(8,128)(2,1)} %get-tuple-element.21), calls=%async_computation | async-start | bytes 1048576 | tf_op jit(solution)/shard_map/all_to_all | solution.py:432
  24.5 6.4 %collective-permute-start = (f32[96,128]{1,0:T(8,128)S(1)}, f32[96,128]{1,0:T(8,128)S(1)}, u32[]{:S(2)}, u32[]{:S(2)}) collective-permute-start(f32[96,128]{1,0:T(8,128)S(1)} %get-tuple-element.22), channel_id=1, source_target_pairs={{0,32},{32,64},{64,96},{96,128},{128,160},{160,192},{192,224},{1,3... | collective-permute-start | bytes 147464 | tf_op jit(solution)/shard_map/ppermute | solution.py:418
  26.5 5.4 %collective-permute-start.1 = (f32[96,128]{1,0:T(8,128)S(1)}, f32[96,128]{1,0:T(8,128)S(1)}, u32[]{:S(2)}, u32[]{:S(2)}) collective-permute-start(f32[96,128]{1,0:T(8,128)S(1)} %get-tuple-element.23), channel_id=1, source_target_pairs={{32,0},{64,32},{96,64},{128,96},{160,128},{192,160},{224,192},{33,... | collective-permute-start | bytes 147464 | tf_op jit(solution)/shard_map/ppermute | solution.py:418
  31.8 6.9 %collective-permute-start.3 = (f32[66,128]{1,0:T(8,128)S(1)}, f32[66,128]{1,0:T(8,128)S(1)}, u32[]{:S(2)}, u32[]{:S(2)}) collective-permute-start(f32[66,128]{1,0:T(8,128)S(1)} %pad_maximum_fusion.1), channel_id=1, source_target_pairs={{1,0},{2,1},{3,2},{4,3},{5,4},{6,5},{7,6},{8,7},{9,8},{10,9},{11,1... | collective-permute-start | bytes 101384 | tf_op jit(solution)/shard_map/ppermute | solution.py:418
  33.2 6.2 %collective-permute-start.2 = (f32[66,128]{1,0:T(8,128)S(1)}, f32[66,128]{1,0:T(8,128)S(1)}, u32[]{:S(2)}, u32[]{:S(2)}) collective-permute-start(f32[66,128]{1,0:T(8,128)S(1)} %pad_maximum_fusion), channel_id=1, source_target_pairs={{0,1},{1,2},{2,3},{3,4},{4,5},{5,6},{6,7},{7,8},{8,9},{9,10},{10,1... | collective-permute-start | bytes 101384 | tf_op jit(solution)/shard_map/ppermute | solution.py:418
  43.4 29.2 %all-to-all-start.1 = ((bf16[32,64,128]{2,1,0:T(8,128)(2,1)}), bf16[32,64,128]{2,1,0:T(8,128)(2,1)}, u32[]{:S(2)}, u32[]{:S(2)}) async-start(bf16[32,64,128]{2,1,0:T(8,128)(2,1)} %residual.1), calls=%async_computation.1 | async-start | bytes 1048576 | tf_op jit(solution)/shard_map/all_to_all | solution.py:445
  72.7 1.2 %copy-start = (bf16[32,128,128]{2,1,0:T(8,128)(2,1)S(1)}, bf16[32,128,128]{2,1,0:T(8,128)(2,1)}, u32[]{:S(2)}) copy-start(bf16[32,128,128]{2,1,0:T(8,128)(2,1)} %prints.3) | copy-start | bytes 3145732

commit v3 on v2

--- a/solution.py
+++ b/solution.py
@@ -6,6 +6,7 @@
 from jax.experimental import pallas as pl
 from jax.experimental.pallas import tpu as pltpu
 from jax.sharding import PartitionSpec as P
+
 
 smoothing = 0.04
 step_length = 2.0
@@ -104,7 +105,7 @@
             total = total + jnp.where(code_row == code, 1.0, 0.0)
         counts[first : first + part] = total.astype(BF16)
 
-    group_size = 4
+    group_size = 8
 
     @pl.loop(0, slice_count // group_size)
     def _(i):
@@ -127,16 +128,16 @@
     prints_copy.wait()
     sums[...] = jnp.zeros_like(sums)
 
-    @pl.loop(0, foot_count // 4)
+    @pl.loop(0, foot_count // 8)
     def _(g):
         block = 256
         for m in range(0, slice_count * touch, block):
             span = slice(m, m + block)
             total = sums[span]
-            for h in range(2):
-                weight = prints_buf[pl.ds(4 * g + 2 * h, 2)].reshape(2 * pixels, -1)
+            for h in range(4):
+                weight = prints_buf[pl.ds(8 * g + 2 * h, 2)].reshape(2 * pixels, -1)
                 total = total + jnp.dot(
-                    grouped[2 * g + h, span], weight, preferred_element_type=F32
+                    grouped[4 * g + h, span], weight, preferred_element_type=F32
                 )
             sums[span] = total
 
@@ -245,9 +246,10 @@
     def scale(a, b, c):
         return lax.rsqrt(a * a + b * b + c * c + smoothing)
 
-    low = before_row[1 : slices + 1]
+    low = before_row[...]
     z_id = iota((slices, 1), 0)
-    grad_slices = before_row[2 : slices + 2] - low
+    above = jnp.where(z_id == slices - 1, after_slice[0:1], pltpu.roll(low, slices - 1, 0))
+    grad_slices = above - low
     grad_slices = jnp.where((z_id == slices - 1) & (layer == last_layer), 0.0, grad_slices)
     grad_rows = first_row[...] - low
     flux = grad_rows * scale(grad_rows, grad_slices, col_grad(low))
@@ -267,12 +269,14 @@
         return grad_rows * inverse, grad_slices * inverse, grad_cols * inverse
 
     slice_copy(0).wait()
-    _, start, _ = fluxes(before_slice[...], by_slice[0], after_row[0:1], False)
+    _, start, _ = fluxes(
+        before_slice[1 : rows + 1], by_slice[0], before_slice[rows + 1 : rows + 2], False
+    )
     start = jnp.where(layer == 0, 0.0, start)
 
     def one(z, here, next_slice, previous, last):
         flux_rows, flux_slices, flux_cols = fluxes(
-            here, next_slice, after_row[pl.ds(z + 1, 1), :], last
+            here, next_slice, after_row[pl.ds(z, 1), :], last
         )
         below = jnp.where(bottom, row_flux[pl.ds(z, 1), :], pltpu.roll(flux_rows, 1, 0))
         left = jnp.where(first, 0.0, pltpu.roll(flux_cols, 1, 1))
@@ -285,7 +289,7 @@
         return one(z, by_slice[z], by_slice[z + 1], previous, False)
 
     final = lax.fori_loop(0, slices - 1, step, start)
-    one(slices - 1, by_slice[slices - 1], after_slice[...], final, layer == last_layer)
+    one(slices - 1, by_slice[slices - 1], after_slice[1 : rows + 1], final, layer == last_layer)
 
 
 def variation(volume, *halos):
@@ -331,11 +335,19 @@
 
 def backward_kernel(
     touch, table, returned, prints, counts_turned, base,
-    out, gathered, mixed, spread, out_buf, sems,
+    out, gathered, mixed, spread, out_buf, prints_buf, sems, prints_sems,
 ):
-    slices, rows, pixels = base.shape
+    slices, _, pixels = base.shape
     foot_count, _, rays = prints.shape
-    codes = foot_count * touch
+    parts = prints_sems.shape[0]
+    per_part = foot_count // parts
+
+    def prints_copy(g):
+        span = pl.ds(g * per_part, per_part)
+        return pltpu.make_async_copy(prints.at[span], prints_buf.at[span], prints_sems.at[g])
+
+    for g in range(parts):
+        prints_copy(g).start()
     for s in range(touch):
         owner = table[1, s]
         block = returned[jnp.maximum(owner, 0)].astype(F32)
@@ -343,10 +355,11 @@
     mixed[...] = jnp.swapaxes(gathered[...], 0, 1).reshape(slices * touch, rays).astype(BF16)
     deep = 16
 
-    @pl.loop(0, foot_count // 4)
+    @pl.loop(0, parts)
     def _(g):
-        for f in range(0, 4, 2):
-            wide = prints[pl.ds(4 * g + f, 2)].reshape(2 * pixels, rays)
+        prints_copy(g).wait()
+        for f in range(0, per_part, 2):
+            wide = prints_buf[pl.ds(per_part * g + f, 2)].reshape(2 * pixels, rays)
             for z in range(0, slices, deep):
                 value = lax.dot_general(
                     mixed[z * touch : (z + deep) * touch, :],
@@ -356,7 +369,7 @@
                 ).astype(BF16)
                 for i in range(deep):
                     for h in range(2):
-                        row = (4 * g + f + h) * touch
+                        row = (per_part * g + f + h) * touch
                         spread[
                             (z + i) // 2,
                             pl.ds(pl.multiple_of(row, touch), touch),
@@ -366,7 +379,7 @@
     def slice_copy(z):
         return pltpu.make_async_copy(out_buf.at[z], out.at[:, z, :], sems.at[z])
 
-    group_size = 4
+    group_size = 8
 
     @pl.loop(0, slices // group_size)
     def _(i):
@@ -395,18 +408,20 @@
     return pl.pallas_call(
         functools.partial(backward_kernel, touch),
         out_shape=jax.ShapeDtypeStruct((rows, slices, pixels), F32),
-        in_specs=[SMEM] + [VMEM] * 4,
+        in_specs=[SMEM, VMEM, HBM, VMEM, VMEM],
         out_specs=HBM,
         scratch_shapes=[
             pltpu.VMEM((touch, slices, prints.shape[2]), F32),
             pltpu.VMEM((slices * touch, prints.shape[2]), BF16),
             pltpu.VMEM((slices // 2, codes, 2 * pixels), BF16),
             pltpu.VMEM((slices, rows, pixels), F32),
+            pltpu.VMEM(prints.shape, BF16),
             pltpu.SemaphoreType.DMA((slices,)),
+            pltpu.SemaphoreType.DMA((4,)),
         ],
         compiler_params=pltpu.CompilerParams(vmem_limit_bytes=24 << 20),
         name="backward",
-    )(table, returned, prints, counts_turned, base)
+    )(table, returned, *in_hbm(prints), counts_turned, base)
 
 
 def shifted(x, axis, forward_way):
@@ -419,7 +434,7 @@
 
 
 def per_device(volume, footprints, foot_index, ray_block, ray_slot, measured, weights):
-    row_count, slice_count, pixels = volume.shape
+    row_count, slice_count, _ = volume.shape
     owners = lax.axis_size("tile")
     owned = measured.shape[0]
     touch = owners // 2
@@ -427,24 +442,23 @@
     sent, table, counts, head, tail = forward(
         touch, owned, owners, ray_slot, blocks, foot_index.T, volume, footprints
     )
-    before_slice = shifted(tail, "slab", True)
-    after_slice = shifted(head, "slab", False)
     arrived = lax.all_to_all(sent, "tile", split_axis=0, concat_axis=0, tiled=True)
+    first_row, last_row, _ = lax.optimization_barrier((volume[0], volume[row_count - 1], head))
+    before_row = shifted(last_row, "tile", True)
+    after_row = shifted(first_row, "tile", False)
     counts_turned, picks = tables(owned, owners, row_count, ray_slot, blocks, counts)
 
-    def edge(r):
-        return jnp.concatenate(
-            [before_slice[r : r + 1], volume[r], after_slice[r : r + 1]], axis=0
-        )
-
-    first_edge, last_edge = edge(0), edge(row_count - 1)
-    before_row = shifted(last_edge, "tile", True)
-    after_row = shifted(first_edge, "tile", False)
-    arrived, before_row, after_row = lax.optimization_barrier((arrived, before_row, after_row))
+    def edge(z, x):
+        return jnp.concatenate([before_row[z : z + 1], x, after_row[z : z + 1]], axis=0)
+
+    edges = (edge(slice_count - 1, tail), edge(0, head))
+    before_slice = shifted(edges[0], "slab", True)
+    after_slice = shifted(edges[1], "slab", False)
+    arrived, _ = lax.optimization_barrier((arrived, edges))
     answer = residual(arrived, picks, measured, weights)
     returned = lax.all_to_all(answer, "tile", split_axis=0, concat_axis=0, tiled=True)
     halos, _ = lax.optimization_barrier(
-        ((before_slice, after_slice, before_row, after_row, volume[0]), answer)
+        ((before_slice, after_slice, before_row, after_row, first_row), answer)
     )
     base = variation(volume, *halos)
     return backward(touch, table, returned, footprints, counts_turned, base)

time: 84.2 us -> 79 us (0.938)
  the two profiles are of different devices: /device:TPU:8 before, /device:TPU:1 now
where the time goes in v3:
time: 79 us; the launch traced here: 78.5 us
  Pallas kernels  34.7 us (44%)
  starting transfers between devices  28.8 us (36%)
  waiting for transfers between devices  14 us (18%)
  local copies, waits for them, and re-layouts  0.81 us (1%)
    pallas_call x1, Pallas kernels, variation(): pl.pallas_call(variation_kernel, out_shape=jax.ShapeDtypeStruct((slices,...  12.2 us
    all_to_all x1, starting transfers between devices, per_device(): lax.all_to_all(sent, 'tile', split_axis=0, concat_axis=0, tiled=True)  11.9 us
    pallas_call x1, Pallas kernels, forward(): pl.pallas_call(functools.partial(forward_kernel, touch, owned), out_shape...  11.6 us
    ppermute x4, starting transfers between devices, shifted(): return lax.ppermute(x, axis, pairs)  11.6 us
    pallas_call x1, Pallas kernels, backward(): pl.pallas_call(functools.partial(backward_kernel, touch), out_shape=jax.S...  8.8 us
    all_to_all x1, waiting for transfers between devices, per_device(): lax.all_to_all(sent, 'tile', split_axis=0, concat_axis=0, tiled=True)  7.01 us
    ppermute x4, waiting for transfers between devices, shifted(): return lax.ppermute(x, axis, pairs)  6.95 us
    all_to_all x1, starting transfers between devices, per_device(): lax.all_to_all(answer, 'tile', split_axis=0, concat_axis=0, tiled=True)  5.37 us
  transfers between devices with their start and end apart: 6, of which 3 were waited for; matrix products, arithmetic and copies ran while one was open for 1% of the time, Pallas kernels for 17%

profile of v3, /device:TPU:1, one launch (start us, length us, event | category | flops | bytes accessed | tf_op | source)
XLA Modules:
  0.0 78.5 jit_solution(3538802113363108344)
XLA Ops:
  0.0 0.0 copy-start.3
  0.0 0.0 copy-start
  0.0 0.0 copy-start.2
  0.0 0.0 copy-start.1
  0.0 11.6 %forward.1 = (bf16[32,64,128]{2,1,0:T(8,128)(2,1)}, s32[8,128]{1,0:T(8,128)S(1)}, bf16[512,128]{1,0:T(8,128)(2,1)S(1)}, f32[96,128]{1,0:T(8,128)S(1)}, f32[96,128]{1,0:T(8,128)S(1)}) custom-call(s32[64]{0:T(128)} %ray_slot.3, s32[8,3072]{1,0:T(8,128)} %bitcast.6, s32[8,96]{1,0:T(8,128)} %bitcast.8, f32[96,64,128]{2,1,0:T(8,128)} %volume.3, ...), custom_call_target="tpu_custom_call" | custom-call | tf_op jit(solution)/shard_map/forward/pallas_call | solution.py:155
  11.6 11.9 %all-to-all-start = ((bf16[32,64,128]{2,1,0:T(8,128)(2,1)}), bf16[32,64,128]{2,1,0:T(8,128)(2,1)S(1)}, u32[]{:S(2)}, u32[]{:S(2)}) async-start(bf16[32,64,128]{2,1,0:T(8,128)(2,1)} %get-tuple-element.21), calls=%async_computation | async-start | bytes 1048576 | tf_op jit(solution)/shard_map/all_to_all | solution.py:445
  23.5 0.8 slice_bitcast_fusion
  24.3 3.1 %collective-permute-start = (f32[64,128]{1,0:T(8,128)S(1)}, f32[64,128]{1,0:T(8,128)S(1)}, u32[]{:S(2)}, u32[]{:S(2)}) collective-permute-start(f32[64,128]{1,0:T(8,128)S(1)} %get-tuple-element.23), channel_id=1, source_target_pairs={{0,1},{1,2},{2,3},{3,4},{4,5},{5,6},{6,7},{7,8},{8,9},{9,10},{10,1... | collective-permute-start | bytes 98312 | tf_op jit(solution)/shard_map/ppermute | solution.py:433
  27.4 1.3 %collective-permute-start.1 = (f32[64,128]{1,0:T(8,128)S(1)}, f32[64,128]{1,0:T(8,128)S(1)}, u32[]{:S(2)}, u32[]{:S(2)}) collective-permute-start(f32[64,128]{1,0:T(8,128)S(1)} %get-tuple-element.34.first_row), channel_id=1, source_target_pairs={{1,0},{2,1},{3,2},{4,3},{5,4},{6,5},{7,6},{8,7},{9,8},{10,9},{11,1... | collective-permute-start | bytes 98312 | tf_op jit(solution)/shard_map/ppermute | solution.py:433
  28.7 0.0 copy-done.3
  28.7 0.0 copy-done
  28.8 1.0 %tables.1 = (bf16[96,512]{1,0:T(8,128)(2,1)S(1)}, f32[32,128]{1,0:T(8,128)S(1)}) custom-call(s32[64]{0:T(128)S(1)} %copy-done.3, s32[8,3072]{1,0:T(8,128)S(1)} %bitcast.7, bf16[512,128]{1,0:T(8,128)(2,1)S(1)} %get-tuple-element.27.counts), custom_call_target="tpu_custom_call" | custom-call | tf_op jit(solution)/shard_map/tables/pallas_call | solution.py:211
  29.7 0.0 collective-permute-done.before_row
  29.7 3.0 %collective-permute-done.1.after_row = f32[64,128]{1,0:T(8,128)S(1)} collective-permute-done((f32[64,128]{1,0:T(8,128)S(1)}, f32[64,128]{1,0:T(8,128)S(1)}, u32[]{:S(2)}, u32[]{:S(2)}) %collective-permute-start.1) | collective-permute-done | bytes 32800 | tf_op jit(solution)/shard_map/ppermute | solution.py:433
  32.8 7.0 %all-to-all-done.arrived = bf16[32,64,128]{2,1,0:T(8,128)(2,1)S(1)} async-done(((bf16[32,64,128]{2,1,0:T(8,128)(2,1)}), bf16[32,64,128]{2,1,0:T(8,128)(2,1)S(1)}, u32[]{:S(2)}, u32[]{:S(2)}) %all-to-all-start) | async-done | bytes 524320 | tf_op jit(solution)/shard_map/all_to_all | solution.py:445
  39.8 0.0 copy-done.2
  39.8 0.0 copy-done.1
  39.8 1.1 %residual.1 = bf16[32,64,128]{2,1,0:T(8,128)(2,1)} custom-call(bf16[32,64,128]{2,1,0:T(8,128)(2,1)S(1)} %all-to-all-done.arrived, f32[32,128]{1,0:T(8,128)S(1)} %get-tuple-element.28.picks, f32[2,64,128]{2,1,0:T(8,128)S(1)} %copy-done.1, f32[2,64,128]{2,1,0:T(8,128)S(1)} %copy-done.2), custom_call_target="tpu_custom_call" | custom-call | tf_op jit(solution)/shard_map/residual/pallas_call | solution.py:326
  40.9 5.4 %all-to-all-start.1 = ((bf16[32,64,128]{2,1,0:T(8,128)(2,1)}), bf16[32,64,128]{2,1,0:T(8,128)(2,1)}, u32[]{:S(2)}, u32[]{:S(2)}) async-start(bf16[32,64,128]{2,1,0:T(8,128)(2,1)} %residual.1), calls=%async_computation.1 | async-start | bytes 1048576 | tf_op jit(solution)/shard_map/all_to_all | solution.py:459
  46.3 5.3 %collective-permute-start.2 = (f32[98,128]{1,0:T(8,128)S(1)}, f32[98,128]{1,0:T(8,128)S(1)}, u32[]{:S(2)}, u32[]{:S(2)}) collective-permute-start(f32[98,128]{1,0:T(8,128)S(1)} %pad_maximum_fusion), channel_id=1, source_target_pairs={{0,32},{32,64},{64,96},{96,128},{128,160},{160,192},{192,224},{1,3... | collective-permute-start | bytes 150536 | tf_op jit(solution)/shard_map/ppermute | solution.py:433
  51.5 1.9 %collective-permute-start.3 = (f32[98,128]{1,0:T(8,128)S(1)}, f32[98,128]{1,0:T(8,128)S(1)}, u32[]{:S(2)}, u32[]{:S(2)}) collective-permute-start(f32[98,128]{1,0:T(8,128)S(1)} %pad_maximum_fusion.1), channel_id=1, source_target_pairs={{32,0},{64,32},{96,64},{128,96},{160,128},{192,160},{224,192},{33,... | collective-permute-start | bytes 150536 | tf_op jit(solution)/shard_map/ppermute | solution.py:433
  53.5 0.0 collective-permute-done.2.before_slice
  53.5 3.9 %collective-permute-done.3.after_slice = f32[98,128]{1,0:T(8,128)S(1)} collective-permute-done((f32[98,128]{1,0:T(8,128)S(1)}, f32[98,128]{1,0:T(8,128)S(1)}, u32[]{:S(2)}, u32[]{:S(2)}) %collective-permute-start.3) | collective-permute-done | bytes 50208 | tf_op jit(solution)/shard_map/ppermute | solution.py:433
  57.4 12.2 %variation.1.base = f32[64,96,128]{2,1,0:T(8,128)S(1)} custom-call(f32[96,64,128]{2,1,0:T(8,128)} %volume.3, f32[98,128]{1,0:T(8,128)S(1)} %collective-permute-done.2.before_slice, f32[98,128]{1,0:T(8,128)S(1)} %collective-permute-done.3.after_slice, f32[64,128]{1,0:T(8,128)S(1)} %collective-permute-done.before_row, ...), custom_call_target="tpu_custom_call" | custom-call | tf_op jit(solution)/shard_map/variation/pallas_call | solution.py:297
  69.6 0.0 all-to-all-done.1.returned
  69.6 8.8 %backward.1 = f32[96,64,128]{2,1,0:T(8,128)} custom-call(s32[8,128]{1,0:T(8,128)S(1)} %get-tuple-element.20.table, bf16[32,64,128]{2,1,0:T(8,128)(2,1)} %all-to-all-done.1.returned, bf16[32,128,128]{2,1,0:T(8,128)(2,1)} %prints.3, bf16[96,512]{1,0:T(8,128)(2,1)S(1)} %get-tuple-element.29.counts_turned, f32[64,96,128]{2,1,0:T(8,128)S(1)} %variation.1.base), custom_call_target="tpu_custom_call" | custom-call | tf_op jit(solution)/shard_map/backward/pallas_call | solution.py:408
  (4 shorter events, 0.0 us)
Async XLA Ops:
  0.0 28.7 %copy-start.3 = (s32[64]{0:T(128)S(1)}, s32[64]{0:T(128)}, u32[]{:S(2)}) copy-start(s32[64]{0:T(128)} %ray_slot.3) | copy-start | bytes 772
  0.0 28.7 %copy-start = (s32[3072,8]{0,1:T(8,128)S(1)}, s32[3072,8]{0,1:T(8,128)}, u32[]{:S(2)}) copy-start(s32[3072,8]{0,1:T(8,128)} %param.10) | copy-start | bytes 294916
  0.0 39.8 %copy-start.2 = (f32[2,64,128]{2,1,0:T(8,128)S(1)}, f32[2,64,128]{2,1,0:T(8,128)}, u32[]{:S(2)}) copy-start(f32[2,64,128]{2,1,0:T(8,128)} %weights.1) | copy-start | bytes 196612
  0.0 39.8 %copy-start.1 = (f32[2,64,128]{2,1,0:T(8,128)S(1)}, f32[2,64,128]{2,1,0:T(8,128)}, u32[]{:S(2)}) copy-start(f32[2,64,128]{2,1,0:T(8,128)} %measured.1) | copy-start | bytes 196612
  11.6 28.2 %all-to-all-start = ((bf16[32,64,128]{2,1,0:T(8,128)(2,1)}), bf16[32,64,128]{2,1,0:T(8,128)(2,1)S(1)}, u32[]{:S(2)}, u32[]{:S(2)}) async-start(bf16[32,64,128]{2,1,0:T(8,128)(2,1)} %get-tuple-element.21), calls=%async_computation | async-start | bytes 1048576 | tf_op jit(solution)/shard_map/all_to_all | solution.py:445
  24.3 5.4 %collective-permute-start = (f32[64,128]{1,0:T(8,128)S(1)}, f32[64,128]{1,0:T(8,128)S(1)}, u32[]{:S(2)}, u32[]{:S(2)}) collective-permute-start(f32[64,128]{1,0:T(8,128)S(1)} %get-tuple-element.23), channel_id=1, source_target_pairs={{0,1},{1,2},{2,3},{3,4},{4,5},{5,6},{6,7},{7,8},{8,9},{9,10},{10,1... | collective-permute-start | bytes 98312 | tf_op jit(solution)/shard_map/ppermute | solution.py:433
  27.4 5.3 %collective-permute-start.1 = (f32[64,128]{1,0:T(8,128)S(1)}, f32[64,128]{1,0:T(8,128)S(1)}, u32[]{:S(2)}, u32[]{:S(2)}) collective-permute-start(f32[64,128]{1,0:T(8,128)S(1)} %get-tuple-element.34.first_row), channel_id=1, source_target_pairs={{1,0},{2,1},{3,2},{4,3},{5,4},{6,5},{7,6},{8,7},{9,8},{10,9},{11,1... | collective-permute-start | bytes 98312 | tf_op jit(solution)/shard_map/ppermute | solution.py:433
  40.9 28.8 %all-to-all-start.1 = ((bf16[32,64,128]{2,1,0:T(8,128)(2,1)}), bf16[32,64,128]{2,1,0:T(8,128)(2,1)}, u32[]{:S(2)}, u32[]{:S(2)}) async-start(bf16[32,64,128]{2,1,0:T(8,128)(2,1)} %residual.1), calls=%async_computation.1 | async-start | bytes 1048576 | tf_op jit(solution)/shard_map/all_to_all | solution.py:459
  46.3 7.2 %collective-permute-start.2 = (f32[98,128]{1,0:T(8,128)S(1)}, f32[98,128]{1,0:T(8,128)S(1)}, u32[]{:S(2)}, u32[]{:S(2)}) collective-permute-start(f32[98,128]{1,0:T(8,128)S(1)} %pad_maximum_fusion), channel_id=1, source_target_pairs={{0,32},{32,64},{64,96},{96,128},{128,160},{160,192},{192,224},{1,3... | collective-permute-start | bytes 150536 | tf_op jit(solution)/shard_map/ppermute | solution.py:433
  51.5 5.9 %collective-permute-start.3 = (f32[98,128]{1,0:T(8,128)S(1)}, f32[98,128]{1,0:T(8,128)S(1)}, u32[]{:S(2)}, u32[]{:S(2)}) collective-permute-start(f32[98,128]{1,0:T(8,128)S(1)} %pad_maximum_fusion.1), channel_id=1, source_target_pairs={{32,0},{64,32},{96,64},{128,96},{160,128},{192,160},{224,192},{33,... | collective-permute-start | bytes 150536 | tf_op jit(solution)/shard_map/ppermute | solution.py:433

commit v4 on v3

--- a/solution.py
+++ b/solution.py
@@ -30,17 +30,18 @@
 
 def forward_kernel(
     touch, owned, ray_slot, blocks, foots, volume, prints,
-    sent, table, counts, head, tail,
+    sent, table, counts, head, tail, first_row, last_row,
     window, foots_buf, slot_buf, by_slice, prints_buf, grouped, sums, compact, table_buf,
     sems, small_sems, table_sem, prints_sem,
 ):
-    row_count, slice_count, pixels = volume.shape
+    row_count, slice_count, _ = volume.shape
     foot_count = prints.shape[0]
     owners = sent.shape[0]
     crossings = blocks.shape[0]
 
-    def slice_copy(z):
-        return pltpu.make_async_copy(volume.at[:, z, :], by_slice.at[z], sems.at[z])
+    half = slice_count // 2
+    groups = sems.shape[0]
+    group_size = half // groups
 
     position = lax.axis_index("tile")
     offset = position * row_count
@@ -53,17 +54,22 @@
                 (blocks.at[:, pl.ds(pl.multiple_of(base, lanes), 2 * lanes)], window),
                 (foots, foots_buf),
                 (ray_slot, slot_buf),
+                (volume.at[0], first_row),
+                (volume.at[row_count - 1], last_row),
             ]
         )
     ]
     for copy in small:
         copy.start()
-    for z in range(slice_count):
-        slice_copy(z).start()
+    for z in range(half):
+        for z in (z, z + half):
+            pltpu.make_async_copy(
+                volume.at[:, z, :], by_slice.at[z], sems.at[z % half // group_size]
+            ).start()
     prints_copy = pltpu.make_async_copy(prints, prints_buf, prints_sem)
     prints_copy.start()
 
-    for copy in small:
+    for copy in small[:3]:
         copy.wait()
     mine = pltpu.roll(window[...], 2 * lanes - (offset - base), 1)[:, :lanes]
     slot = jnp.zeros_like(mine)
@@ -97,51 +103,60 @@
             jnp.where(owner[k : k + 1] == label, rank, 0.0), axis=0, keepdims=True
         ).astype(jnp.int32)
         codes.append(jnp.where(valid[k : k + 1], foots_here[k : k + 1] * touch + place, -1))
-    part = 4 * touch
-    for first in range(0, foot_count * touch, part):
-        code_row = iota((part, lanes), 0) + first
-        total = jnp.zeros((part, lanes), F32)
+    step = 4
+    for f in range(0, foot_count, step):
+        code_row = iota((step * touch, lanes), 0) + f * touch
+        total = jnp.zeros((step * touch, lanes), F32)
         for code in codes:
             total = total + jnp.where(code_row == code, 1.0, 0.0)
-        counts[first : first + part] = total.astype(BF16)
-
-    group_size = 8
-
-    @pl.loop(0, slice_count // group_size)
+        counts[f * touch : (f + step) * touch] = total.astype(BF16)
+
+    @pl.loop(0, groups)
     def _(i):
+        both = by_slice.at[pl.ds(0, 2 * group_size)]
+        pltpu.make_async_copy(both, both, sems.at[i]).wait()
         for j in range(group_size):
-            slice_copy(i * group_size + j).wait()
-        for j in range(0, group_size, 2):
             z = i * group_size + j
-            pair = jnp.concatenate([by_slice[z], by_slice[z + 1]], axis=1).astype(BF16)
-            group = jnp.dot(counts[:, :row_count], pair, preferred_element_type=F32).astype(BF16)
-            for half in range(2):
-                for f in range(foot_count):
-                    grouped[
-                        f // 2,
-                        pl.ds(pl.multiple_of((z + half) * touch, touch), touch),
-                        (f % 2) * pixels : (f % 2 + 1) * pixels,
-                    ] = group[f * touch : (f + 1) * touch, half * pixels : (half + 1) * pixels]
+            pair = jnp.concatenate([by_slice[z], by_slice[z + half]], axis=1).astype(BF16)
+            for first in range(0, foot_count, step):
+                group = jnp.dot(
+                    counts[first * touch : (first + step) * touch, :row_count],
+                    pair,
+                    preferred_element_type=F32,
+                ).astype(BF16)
+                for f in range(step):
+                    grouped[first + f, pl.ds(pl.multiple_of(z * touch, touch), touch), :] = group[
+                        f * touch : (f + 1) * touch
+                    ]
 
     head[...] = by_slice[0]
     tail[...] = by_slice[slice_count - 1]
     prints_copy.wait()
     sums[...] = jnp.zeros_like(sums)
-
-    @pl.loop(0, foot_count // 8)
+    deep = 16
+    block = 256
+    zero = jnp.zeros(prints.shape[1:], BF16)
+
+    @pl.loop(0, foot_count // deep)
     def _(g):
-        block = 256
-        for m in range(0, slice_count * touch, block):
-            span = slice(m, m + block)
-            total = sums[span]
-            for h in range(4):
-                weight = prints_buf[pl.ds(8 * g + 2 * h, 2)].reshape(2 * pixels, -1)
-                total = total + jnp.dot(
-                    grouped[4 * g + h, span], weight, preferred_element_type=F32
-                )
-            sums[span] = total
+        weights = []
+        for h in range(deep):
+            weight = prints_buf[g * deep + h]
+            weights.append(jnp.concatenate([weight, zero], axis=1))
+            weights.append(jnp.concatenate([zero, weight], axis=1))
+        weights = jnp.concatenate(weights, axis=0)
+        for m in range(0, half * touch, block):
+            left = [grouped[g * deep + h, m : m + block, :] for h in range(deep)]
+            both = jnp.dot(
+                jnp.concatenate(left, axis=1), weights, preferred_element_type=F32
+            )
+            rays = both.shape[1] // 2
+            sums[m : m + block] += both[:, :rays]
+            sums[half * touch + m : half * touch + m + block] += both[:, rays:]
 
     compact[...] = jnp.swapaxes(sums[...].reshape(slice_count, touch, -1), 0, 1).astype(BF16)
+    for copy in small[3:]:
+        copy.wait()
     table_copy.wait()
     for t in range(owners):
         place = table[0, t]
@@ -160,21 +175,23 @@
             jax.ShapeDtypeStruct((foot_count * touch, lanes), BF16),
             jax.ShapeDtypeStruct((rows, pixels), F32),
             jax.ShapeDtypeStruct((rows, pixels), F32),
+            jax.ShapeDtypeStruct((slices, pixels), F32),
+            jax.ShapeDtypeStruct((slices, pixels), F32),
         ),
         in_specs=[HBM] * 5,
-        out_specs=(VMEM, SMEM, VMEM, VMEM, VMEM),
+        out_specs=(VMEM, SMEM) + (VMEM,) * 5,
         scratch_shapes=[
             pltpu.VMEM((blocks.shape[0], 2 * lanes), jnp.int32),
             pltpu.VMEM(foots.shape, jnp.int32),
             pltpu.SMEM(ray_slot.shape, jnp.int32),
             pltpu.VMEM((slices, rows, pixels), F32),
             pltpu.VMEM(prints.shape, BF16),
-            pltpu.VMEM((foot_count // 2, slices * touch, 2 * pixels), BF16),
+            pltpu.VMEM((foot_count, slices // 2 * touch, 2 * pixels), BF16),
             pltpu.VMEM((slices * touch, rays), F32),
             pltpu.VMEM((touch, slices, rays), BF16),
             pltpu.VMEM((8, lanes), jnp.int32),
-            pltpu.SemaphoreType.DMA((slices,)),
-            pltpu.SemaphoreType.DMA((3,)),
+            pltpu.SemaphoreType.DMA((4,)),
+            pltpu.SemaphoreType.DMA((5,)),
             pltpu.SemaphoreType.DMA,
             pltpu.SemaphoreType.DMA,
         ],
@@ -227,11 +244,15 @@
 ):
     slices, rows, pixels = base.shape
 
-    def slice_copy(z):
-        return pltpu.make_async_copy(volume.at[:, z, :], by_slice.at[z], sems.at[z])
-
+    groups = sems.shape[0]
+    size = slices // groups
     for z in range(slices):
-        slice_copy(z).start()
+        pltpu.make_async_copy(volume.at[:, z, :], by_slice.at[z], sems.at[z // size]).start()
+
+    def wait_group(i):
+        span = by_slice.at[pl.ds(i * size, size)]
+        pltpu.make_async_copy(span, span, sems.at[i]).wait()
+
     position = lax.axis_index("tile")
     layer = lax.axis_index("slab")
     last_position = lax.axis_size("tile") - 1
@@ -268,7 +289,7 @@
         inverse = scale(grad_rows, grad_slices, grad_cols)
         return grad_rows * inverse, grad_slices * inverse, grad_cols * inverse
 
-    slice_copy(0).wait()
+    wait_group(0)
     _, start, _ = fluxes(
         before_slice[1 : rows + 1], by_slice[0], before_slice[rows + 1 : rows + 2], False
     )
@@ -285,7 +306,10 @@
         return flux_slices
 
     def step(z, previous):
-        slice_copy(z + 1).wait()
+        @pl.when((z + 1) % size == 0)
+        def _():
+            wait_group((z + 1) // size)
+
         return one(z, by_slice[z], by_slice[z + 1], previous, False)
 
     final = lax.fori_loop(0, slices - 1, step, start)
@@ -302,7 +326,7 @@
         scratch_shapes=[
             pltpu.VMEM((slices, rows, pixels), F32),
             pltpu.VMEM((slices, pixels), F32),
-            pltpu.SemaphoreType.DMA((slices,)),
+            pltpu.SemaphoreType.DMA((8,)),
         ],
         compiler_params=pltpu.CompilerParams(vmem_limit_bytes=8 << 20),
         name="variation",
@@ -353,53 +377,56 @@
         block = returned[jnp.maximum(owner, 0)].astype(F32)
         gathered[s] = jnp.where(owner >= 0, block, 0.0)
     mixed[...] = jnp.swapaxes(gathered[...], 0, 1).reshape(slices * touch, rays).astype(BF16)
-    deep = 16
+    half = slices // 2
+    block = 256
+    zero = jnp.zeros(prints.shape[1:], BF16)
 
     @pl.loop(0, parts)
     def _(g):
         prints_copy(g).wait()
-        for f in range(0, per_part, 2):
-            wide = prints_buf[pl.ds(per_part * g + f, 2)].reshape(2 * pixels, rays)
-            for z in range(0, slices, deep):
+        for f in range(per_part):
+            weight = prints_buf[per_part * g + f]
+            weights = jnp.concatenate(
+                [
+                    jnp.concatenate([weight, zero], axis=1),
+                    jnp.concatenate([zero, weight], axis=1),
+                ],
+                axis=0,
+            )
+            for m in range(0, half * touch, block):
+                left = jnp.concatenate(
+                    [mixed[m : m + block], mixed[half * touch + m : half * touch + m + block]], axis=1
+                )
                 value = lax.dot_general(
-                    mixed[z * touch : (z + deep) * touch, :],
-                    wide,
-                    (((1,), (1,)), ((), ())),
-                    preferred_element_type=F32,
+                    left, weights, (((1,), (1,)), ((), ())), preferred_element_type=F32
                 ).astype(BF16)
-                for i in range(deep):
-                    for h in range(2):
-                        row = (per_part * g + f + h) * touch
-                        spread[
-                            (z + i) // 2,
-                            pl.ds(pl.multiple_of(row, touch), touch),
-                            (i % 2) * pixels : (i % 2 + 1) * pixels,
-                        ] = value[i * touch : (i + 1) * touch, h * pixels : (h + 1) * pixels]
-
-    def slice_copy(z):
-        return pltpu.make_async_copy(out_buf.at[z], out.at[:, z, :], sems.at[z])
-
-    group_size = 8
-
-    @pl.loop(0, slices // group_size)
+                for i in range(block // touch):
+                    row = pl.multiple_of((per_part * g + f) * touch, touch)
+                    spread[m // touch + i, pl.ds(row, touch), :] = value[
+                        i * touch : (i + 1) * touch
+                    ]
+
+    groups = sems.shape[0]
+    group_size = half // groups
+
+    @pl.loop(0, groups)
     def _(i):
-        for j in range(0, group_size, 2):
+        for j in range(group_size):
             z = i * group_size + j
-            grad = jnp.dot(
-                counts_turned[...],
-                spread[i * (group_size // 2) + j // 2],
-                preferred_element_type=F32,
-            )
+            grad = jnp.dot(counts_turned[...], spread[z], preferred_element_type=F32)
             for g in range(2):
-                out_buf[z + g] = jnp.maximum(
-                    base[z + g] - step_length * grad[:, g * pixels : (g + 1) * pixels], 0.0
+                at = z + g * half
+                out_buf[at] = jnp.maximum(
+                    base[at] - step_length * grad[:, g * pixels : (g + 1) * pixels], 0.0
                 )
         for j in range(group_size):
-            slice_copy(i * group_size + j).start()
-
-    @pl.loop(0, slices)
-    def _(z):
-        slice_copy(z).wait()
+            for g in range(2):
+                at = i * group_size + j + g * half
+                pltpu.make_async_copy(out_buf.at[at], out.at[:, at, :], sems.at[i]).start()
+
+    for i in range(groups):
+        both = out_buf.at[pl.ds(0, 2 * group_size)]
+        pltpu.make_async_copy(both, both, sems.at[i]).wait()
 
 
 def backward(touch, table, returned, prints, counts_turned, base):
@@ -416,7 +443,7 @@
             pltpu.VMEM((slices // 2, codes, 2 * pixels), BF16),
             pltpu.VMEM((slices, rows, pixels), F32),
             pltpu.VMEM(prints.shape, BF16),
-            pltpu.SemaphoreType.DMA((slices,)),
+            pltpu.SemaphoreType.DMA((4,)),
             pltpu.SemaphoreType.DMA((4,)),
         ],
         compiler_params=pltpu.CompilerParams(vmem_limit_bytes=24 << 20),
@@ -439,11 +466,10 @@
     owned = measured.shape[0]
     touch = owners // 2
     blocks = ray_block.T
-    sent, table, counts, head, tail = forward(
+    sent, table, counts, head, tail, first_row, last_row = forward(
         touch, owned, owners, ray_slot, blocks, foot_index.T, volume, footprints
     )
     arrived = lax.all_to_all(sent, "tile", split_axis=0, concat_axis=0, tiled=True)
-    first_row, last_row, _ = lax.optimization_barrier((volume[0], volume[row_count - 1], head))
     before_row = shifted(last_row, "tile", True)
     after_row = shifted(first_row, "tile", False)
     counts_turned, picks = tables(owned, owners, row_count, ray_slot, blocks, counts)

time: 79 us -> 75.3 us (0.953)
  Pallas kernels: 34.7 us -> 31.1 us
  waiting for transfers between devices: 14 us -> 14.8 us
  local copies, waits for them, and re-layouts: 0.81 us -> 0.02 us
    pallas_call x1, Pallas kernels: 11.6 us -> 9.25 us  [forward(): pl.pallas_call(functools.partial(forward_kernel, touch, owned), out_shape...]
    pallas_call x1, Pallas kernels: 8.8 us -> 7.86 us  [backward(): pl.pallas_call(functools.partial(backward_kernel, touch), out_shape=jax.S...]
  transfers between devices with their start and end apart: 6 -> 6, of which waited for: 3 -> 3; matrix products, arithmetic and copies ran while one was open for 1% -> 0% of each run, Pallas kernels for 17% -> 17%
where the time goes in v4:
time: 75.3 us; the launch traced here: 74.9 us
  Pallas kernels  31.1 us (41%)
  starting transfers between devices  28.8 us (38%)
  waiting for transfers between devices  14.8 us (20%)
    pallas_call x1, Pallas kernels, variation(): pl.pallas_call(variation_kernel, out_shape=jax.ShapeDtypeStruct((slices,...  12 us
    all_to_all x1, starting transfers between devices, per_device(): lax.all_to_all(sent, 'tile', split_axis=0, concat_axis=0, tiled=True)  11.9 us
    ppermute x4, starting transfers between devices, shifted(): return lax.ppermute(x, axis, pairs)  11.6 us
    pallas_call x1, Pallas kernels, forward(): pl.pallas_call(functools.partial(forward_kernel, touch, owned), out_shape...  9.25 us
    pallas_call x1, Pallas kernels, backward(): pl.pallas_call(functools.partial(backward_kernel, touch), out_shape=jax.S...  7.86 us
    ppermute x4, waiting for transfers between devices, shifted(): return lax.ppermute(x, axis, pairs)  7.61 us
    all_to_all x1, waiting for transfers between devices, per_device(): lax.all_to_all(sent, 'tile', split_axis=0, concat_axis=0, tiled=True)  7.15 us
    all_to_all x1, starting transfers between devices, per_device(): lax.all_to_all(answer, 'tile', split_axis=0, concat_axis=0, tiled=True)  5.35 us
  transfers between devices with their start and end apart: 6, of which 3 were waited for; matrix products, arithmetic and copies ran while one was open for 0% of the time, Pallas kernels for 17%

profile of v4, /device:TPU:1, one launch (start us, length us, event | category | flops | bytes accessed | tf_op | source)
XLA Modules:
  0.0 74.9 jit_solution(17069671298322101589)
XLA Ops:
  0.0 0.0 copy-start.3
  0.0 0.0 copy-start
  0.0 0.0 copy-start.2
  0.0 0.0 copy-start.1
  0.0 9.2 %forward.1 = (bf16[32,64,128]{2,1,0:T(8,128)(2,1)}, s32[8,128]{1,0:T(8,128)S(1)}, bf16[512,128]{1,0:T(8,128)(2,1)S(1)}, f32[96,128]{1,0:T(8,128)S(1)}, f32[96,12...) custom-call(s32[64]{0:T(128)} %ray_slot.3, s32[8,3072]{1,0:T(8,128)} %bitcast.2, s32[8,96]{1,0:T(8,128)} %bitcast.4, ...), custom_call_target="tpu_custom_call" | custom-call | tf_op jit(solution)/shard_map/forward/pallas_call | solution.py:170
  9.3 11.9 %all-to-all-start = ((bf16[32,64,128]{2,1,0:T(8,128)(2,1)}), bf16[32,64,128]{2,1,0:T(8,128)(2,1)S(1)}, u32[]{:S(2)}, u32[]{:S(2)}) async-start(bf16[32,64,128]{2,1,0:T(8,128)(2,1)} %get-tuple-element.21), calls=%async_computation | async-start | bytes 1048576 | tf_op jit(solution)/shard_map/all_to_all | solution.py:472
  21.1 3.1 %collective-permute-start = (f32[64,128]{1,0:T(8,128)S(1)}, f32[64,128]{1,0:T(8,128)S(1)}, u32[]{:S(2)}, u32[]{:S(2)}) collective-permute-start(f32[64,128]{1,0:T(8,128)S(1)} %get-tuple-element.22), channel_id=1, source_target_pairs={{0,1},{1,2},{2,3},{3,4},{4,5},{5,6},{6,7},{7,8},{8,9},{9,10},{10,1... | collective-permute-start | bytes 98312 | tf_op jit(solution)/shard_map/ppermute | solution.py:460
  24.3 1.3 %collective-permute-start.1 = (f32[64,128]{1,0:T(8,128)S(1)}, f32[64,128]{1,0:T(8,128)S(1)}, u32[]{:S(2)}, u32[]{:S(2)}) collective-permute-start(f32[64,128]{1,0:T(8,128)S(1)} %get-tuple-element.34.first_row), channel_id=1, source_target_pairs={{1,0},{2,1},{3,2},{4,3},{5,4},{6,5},{7,6},{8,7},{9,8},{10,9},{11,1... | collective-permute-start | bytes 98312 | tf_op jit(solution)/shard_map/ppermute | solution.py:460
  25.6 0.0 copy-done.3
  25.6 0.0 copy-done
  25.6 1.0 %tables.1 = (bf16[96,512]{1,0:T(8,128)(2,1)S(1)}, f32[32,128]{1,0:T(8,128)S(1)}) custom-call(s32[64]{0:T(128)S(1)} %copy-done.3, s32[8,3072]{1,0:T(8,128)S(1)} %bitcast.3, bf16[512,128]{1,0:T(8,128)(2,1)S(1)} %get-tuple-element.27.counts), custom_call_target="tpu_custom_call" | custom-call | tf_op jit(solution)/shard_map/tables/pallas_call | solution.py:228
  26.6 0.0 collective-permute-done.before_row
  26.6 3.7 %collective-permute-done.1.after_row = f32[64,128]{1,0:T(8,128)S(1)} collective-permute-done((f32[64,128]{1,0:T(8,128)S(1)}, f32[64,128]{1,0:T(8,128)S(1)}, u32[]{:S(2)}, u32[]{:S(2)}) %collective-permute-start.1) | collective-permute-done | bytes 32800 | tf_op jit(solution)/shard_map/ppermute | solution.py:460
  30.3 7.1 %all-to-all-done.arrived = bf16[32,64,128]{2,1,0:T(8,128)(2,1)S(1)} async-done(((bf16[32,64,128]{2,1,0:T(8,128)(2,1)}), bf16[32,64,128]{2,1,0:T(8,128)(2,1)S(1)}, u32[]{:S(2)}, u32[]{:S(2)}) %all-to-all-start) | async-done | bytes 524320 | tf_op jit(solution)/shard_map/all_to_all | solution.py:472
  37.5 0.0 copy-done.2
  37.5 0.0 copy-done.1
  37.5 1.1 %residual.1 = bf16[32,64,128]{2,1,0:T(8,128)(2,1)} custom-call(bf16[32,64,128]{2,1,0:T(8,128)(2,1)S(1)} %all-to-all-done.arrived, f32[32,128]{1,0:T(8,128)S(1)} %get-tuple-element.28.picks, f32[2,64,128]{2,1,0:T(8,128)S(1)} %copy-done.1, f32[2,64,128]{2,1,0:T(8,128)S(1)} %copy-done.2), custom_call_target="tpu_custom_call" | custom-call | tf_op jit(solution)/shard_map/residual/pallas_call | solution.py:350
  38.5 5.4 %all-to-all-start.1 = ((bf16[32,64,128]{2,1,0:T(8,128)(2,1)}), bf16[32,64,128]{2,1,0:T(8,128)(2,1)}, u32[]{:S(2)}, u32[]{:S(2)}) async-start(bf16[32,64,128]{2,1,0:T(8,128)(2,1)} %residual.1), calls=%async_computation.1 | async-start | bytes 1048576 | tf_op jit(solution)/shard_map/all_to_all | solution.py:485
  43.9 5.3 %collective-permute-start.2 = (f32[98,128]{1,0:T(8,128)S(1)}, f32[98,128]{1,0:T(8,128)S(1)}, u32[]{:S(2)}, u32[]{:S(2)}) collective-permute-start(f32[98,128]{1,0:T(8,128)S(1)} %pad_maximum_fusion), channel_id=1, source_target_pairs={{0,32},{32,64},{64,96},{96,128},{128,160},{160,192},{192,224},{1,3... | collective-permute-start | bytes 150536 | tf_op jit(solution)/shard_map/ppermute | solution.py:460
  49.2 1.9 %collective-permute-start.3 = (f32[98,128]{1,0:T(8,128)S(1)}, f32[98,128]{1,0:T(8,128)S(1)}, u32[]{:S(2)}, u32[]{:S(2)}) collective-permute-start(f32[98,128]{1,0:T(8,128)S(1)} %pad_maximum_fusion.1), channel_id=1, source_target_pairs={{32,0},{64,32},{96,64},{128,96},{160,128},{192,160},{224,192},{33,... | collective-permute-start | bytes 150536 | tf_op jit(solution)/shard_map/ppermute | solution.py:460
  51.1 0.0 collective-permute-done.2.before_slice
  51.1 3.9 %collective-permute-done.3.after_slice = f32[98,128]{1,0:T(8,128)S(1)} collective-permute-done((f32[98,128]{1,0:T(8,128)S(1)}, f32[98,128]{1,0:T(8,128)S(1)}, u32[]{:S(2)}, u32[]{:S(2)}) %collective-permute-start.3) | collective-permute-done | bytes 50208 | tf_op jit(solution)/shard_map/ppermute | solution.py:460
  55.0 12.0 %variation.1.base = f32[64,96,128]{2,1,0:T(8,128)S(1)} custom-call(f32[96,64,128]{2,1,0:T(8,128)} %volume.3, f32[98,128]{1,0:T(8,128)S(1)} %collective-permute-done.2.before_slice, f32[98,128]{1,0:T(8,128)S(1)} %collective-permute-done.3.after_slice, f32[64,128]{1,0:T(8,128)S(1)} %collective-permute-done.before_row, ...), custom_call_target="tpu_custom_call" | custom-call | tf_op jit(solution)/shard_map/variation/pallas_call | solution.py:321
  67.0 0.0 all-to-all-done.1.returned
  67.0 7.9 %backward.1 = f32[96,64,128]{2,1,0:T(8,128)} custom-call(s32[8,128]{1,0:T(8,128)S(1)} %get-tuple-element.20.table, bf16[32,64,128]{2,1,0:T(8,128)(2,1)} %all-to-all-done.1.returned, bf16[32,128,128]{2,1,0:T(8,128)(2,1)} %prints.3, bf16[96,512]{1,0:T(8,128)(2,1)S(1)} %get-tuple-element.29.counts_turned, f32[64,96,128]{2,1,0:T(8,128)S(1)} %variation.1.base), custom_call_target="tpu_custom_call" | custom-call | tf_op jit(solution)/shard_map/backward/pallas_call | solution.py:435
  (4 shorter events, 0.0 us)
Async XLA Ops:
  0.0 25.6 %copy-start.3 = (s32[64]{0:T(128)S(1)}, s32[64]{0:T(128)}, u32[]{:S(2)}) copy-start(s32[64]{0:T(128)} %ray_slot.3) | copy-start | bytes 772
  0.0 25.6 %copy-start = (s32[3072,8]{0,1:T(8,128)S(1)}, s32[3072,8]{0,1:T(8,128)}, u32[]{:S(2)}) copy-start(s32[3072,8]{0,1:T(8,128)} %param.10) | copy-start | bytes 294916
  0.0 37.5 %copy-start.2 = (f32[2,64,128]{2,1,0:T(8,128)S(1)}, f32[2,64,128]{2,1,0:T(8,128)}, u32[]{:S(2)}) copy-start(f32[2,64,128]{2,1,0:T(8,128)} %weights.1) | copy-start | bytes 196612
  0.0 37.5 %copy-start.1 = (f32[2,64,128]{2,1,0:T(8,128)S(1)}, f32[2,64,128]{2,1,0:T(8,128)}, u32[]{:S(2)}) copy-start(f32[2,64,128]{2,1,0:T(8,128)} %measured.1) | copy-start | bytes 196612
  9.3 28.2 %all-to-all-start = ((bf16[32,64,128]{2,1,0:T(8,128)(2,1)}), bf16[32,64,128]{2,1,0:T(8,128)(2,1)S(1)}, u32[]{:S(2)}, u32[]{:S(2)}) async-start(bf16[32,64,128]{2,1,0:T(8,128)(2,1)} %get-tuple-element.21), calls=%async_computation | async-start | bytes 1048576 | tf_op jit(solution)/shard_map/all_to_all | solution.py:472
  21.1 5.4 %collective-permute-start = (f32[64,128]{1,0:T(8,128)S(1)}, f32[64,128]{1,0:T(8,128)S(1)}, u32[]{:S(2)}, u32[]{:S(2)}) collective-permute-start(f32[64,128]{1,0:T(8,128)S(1)} %get-tuple-element.22), channel_id=1, source_target_pairs={{0,1},{1,2},{2,3},{3,4},{4,5},{5,6},{6,7},{7,8},{8,9},{9,10},{10,1... | collective-permute-start | bytes 98312 | tf_op jit(solution)/shard_map/ppermute | solution.py:460
  24.3 6.0 %collective-permute-start.1 = (f32[64,128]{1,0:T(8,128)S(1)}, f32[64,128]{1,0:T(8,128)S(1)}, u32[]{:S(2)}, u32[]{:S(2)}) collective-permute-start(f32[64,128]{1,0:T(8,128)S(1)} %get-tuple-element.34.first_row), channel_id=1, source_target_pairs={{1,0},{2,1},{3,2},{4,3},{5,4},{6,5},{7,6},{8,7},{9,8},{10,9},{11,1... | collective-permute-start | bytes 98312 | tf_op jit(solution)/shard_map/ppermute | solution.py:460
  38.5 28.5 %all-to-all-start.1 = ((bf16[32,64,128]{2,1,0:T(8,128)(2,1)}), bf16[32,64,128]{2,1,0:T(8,128)(2,1)}, u32[]{:S(2)}, u32[]{:S(2)}) async-start(bf16[32,64,128]{2,1,0:T(8,128)(2,1)} %residual.1), calls=%async_computation.1 | async-start | bytes 1048576 | tf_op jit(solution)/shard_map/all_to_all | solution.py:485
  43.9 7.2 %collective-permute-start.2 = (f32[98,128]{1,0:T(8,128)S(1)}, f32[98,128]{1,0:T(8,128)S(1)}, u32[]{:S(2)}, u32[]{:S(2)}) collective-permute-start(f32[98,128]{1,0:T(8,128)S(1)} %pad_maximum_fusion), channel_id=1, source_target_pairs={{0,32},{32,64},{64,96},{96,128},{128,160},{160,192},{192,224},{1,3... | collective-permute-start | bytes 150536 | tf_op jit(solution)/shard_map/ppermute | solution.py:460
  49.2 5.9 %collective-permute-start.3 = (f32[98,128]{1,0:T(8,128)S(1)}, f32[98,128]{1,0:T(8,128)S(1)}, u32[]{:S(2)}, u32[]{:S(2)}) collective-permute-start(f32[98,128]{1,0:T(8,128)S(1)} %pad_maximum_fusion.1), channel_id=1, source_target_pairs={{32,0},{64,32},{96,64},{128,96},{160,128},{192,160},{224,192},{33,... | collective-permute-start | bytes 150536 | tf_op jit(solution)/shard_map/ppermute | solution.py:460

commit v5 on v4

--- a/solution.py
+++ b/solution.py
@@ -97,19 +97,23 @@
     foots_here = jnp.concatenate(
         [foots_buf[...], jnp.zeros((crossings, lanes - row_count), jnp.int32)], axis=1
     )
-    codes = []
+    step = 4
+    hits, feet = [], []
+    rank_id = iota((touch, lanes), 0)
     for k in range(crossings):
         place = jnp.sum(
             jnp.where(owner[k : k + 1] == label, rank, 0.0), axis=0, keepdims=True
         ).astype(jnp.int32)
-        codes.append(jnp.where(valid[k : k + 1], foots_here[k : k + 1] * touch + place, -1))
-    step = 4
-    for f in range(0, foot_count, step):
-        code_row = iota((step * touch, lanes), 0) + f * touch
-        total = jnp.zeros((step * touch, lanes), F32)
-        for code in codes:
-            total = total + jnp.where(code_row == code, 1.0, 0.0)
-        counts[f * touch : (f + step) * touch] = total.astype(BF16)
+        hits.append(jnp.where((rank_id == place) & valid[k : k + 1], 1.0, 0.0).astype(BF16))
+        feet.append(
+            jnp.broadcast_to(foots_here[k : k + 1].astype(F32), (touch, lanes)).astype(BF16)
+        )
+    none = jnp.zeros((touch, lanes), BF16)
+    for f in range(foot_count):
+        terms = [jnp.where(foot == f, hit, none) for foot, hit in zip(feet, hits)]
+        while len(terms) > 1:
+            terms = [x + y for x, y in zip(terms[::2], terms[1::2])]
+        counts[f * touch : (f + 1) * touch] = terms[0]
 
     @pl.loop(0, groups)
     def _(i):

time: 75.3 us -> 75.2 us (level)
  no operation moved by 1% of the time
where the time goes in v5:
time: 75.2 us; the launch traced here: 74.8 us
  Pallas kernels  31 us (41%)
  starting transfers between devices  28.8 us (38%)
  waiting for transfers between devices  14.7 us (20%)
    pallas_call x1, Pallas kernels, variation(): pl.pallas_call(variation_kernel, out_shape=jax.ShapeDtypeStruct((slices,...  12 us
    all_to_all x1, starting transfers between devices, per_device(): lax.all_to_all(sent, 'tile', split_axis=0, concat_axis=0, tiled=True)  11.9 us
    ppermute x4, starting transfers between devices, shifted(): return lax.ppermute(x, axis, pairs)  11.6 us
    pallas_call x1, Pallas kernels, forward(): pl.pallas_call(functools.partial(forward_kernel, touch, owned), out_shape...  9.11 us
    pallas_call x1, Pallas kernels, backward(): pl.pallas_call(functools.partial(backward_kernel, touch), out_shape=jax.S...  7.86 us
    ppermute x4, waiting for transfers between devices, shifted(): return lax.ppermute(x, axis, pairs)  7.61 us
    all_to_all x1, waiting for transfers between devices, per_device(): lax.all_to_all(sent, 'tile', split_axis=0, concat_axis=0, tiled=True)  7.12 us
    all_to_all x1, starting transfers between devices, per_device(): lax.all_to_all(answer, 'tile', split_axis=0, concat_axis=0, tiled=True)  5.38 us
  transfers between devices with their start and end apart: 6, of which 3 were waited for; matrix products, arithmetic and copies ran while one was open for 0% of the time, Pallas kernels for 17%

profile of v5, /device:TPU:1, one launch (start us, length us, event | category | flops | bytes accessed | tf_op | source)
XLA Modules:
  0.0 74.8 jit_solution(5081966865244984162)
XLA Ops:
  0.0 0.0 copy-start.3
  0.0 0.0 copy-start
  0.0 0.0 copy-start.2
  0.0 0.0 copy-start.1
  0.0 9.1 %forward.1 = (bf16[32,64,128]{2,1,0:T(8,128)(2,1)}, s32[8,128]{1,0:T(8,128)S(1)}, bf16[512,128]{1,0:T(8,128)(2,1)S(1)}, f32[96,128]{1,0:T(8,128)S(1)}, f32[96,12...) custom-call(s32[64]{0:T(128)} %ray_slot.3, s32[8,3072]{1,0:T(8,128)} %bitcast.2, s32[8,96]{1,0:T(8,128)} %bitcast.4, ...), custom_call_target="tpu_custom_call" | custom-call | tf_op jit(solution)/shard_map/forward/pallas_call | solution.py:174
  9.1 11.9 %all-to-all-start = ((bf16[32,64,128]{2,1,0:T(8,128)(2,1)}), bf16[32,64,128]{2,1,0:T(8,128)(2,1)S(1)}, u32[]{:S(2)}, u32[]{:S(2)}) async-start(bf16[32,64,128]{2,1,0:T(8,128)(2,1)} %get-tuple-element.21), calls=%async_computation | async-start | bytes 1048576 | tf_op jit(solution)/shard_map/all_to_all | solution.py:476
  21.0 3.1 %collective-permute-start = (f32[64,128]{1,0:T(8,128)S(1)}, f32[64,128]{1,0:T(8,128)S(1)}, u32[]{:S(2)}, u32[]{:S(2)}) collective-permute-start(f32[64,128]{1,0:T(8,128)S(1)} %get-tuple-element.22), channel_id=1, source_target_pairs={{0,1},{1,2},{2,3},{3,4},{4,5},{5,6},{6,7},{7,8},{8,9},{9,10},{10,1... | collective-permute-start | bytes 98312 | tf_op jit(solution)/shard_map/ppermute | solution.py:464
  24.2 1.3 %collective-permute-start.1 = (f32[64,128]{1,0:T(8,128)S(1)}, f32[64,128]{1,0:T(8,128)S(1)}, u32[]{:S(2)}, u32[]{:S(2)}) collective-permute-start(f32[64,128]{1,0:T(8,128)S(1)} %get-tuple-element.34.first_row), channel_id=1, source_target_pairs={{1,0},{2,1},{3,2},{4,3},{5,4},{6,5},{7,6},{8,7},{9,8},{10,9},{11,1... | collective-permute-start | bytes 98312 | tf_op jit(solution)/shard_map/ppermute | solution.py:464
  25.5 0.0 copy-done.3
  25.5 0.0 copy-done
  25.5 1.0 %tables.1 = (bf16[96,512]{1,0:T(8,128)(2,1)S(1)}, f32[32,128]{1,0:T(8,128)S(1)}) custom-call(s32[64]{0:T(128)S(1)} %copy-done.3, s32[8,3072]{1,0:T(8,128)S(1)} %bitcast.3, bf16[512,128]{1,0:T(8,128)(2,1)S(1)} %get-tuple-element.27.counts), custom_call_target="tpu_custom_call" | custom-call | tf_op jit(solution)/shard_map/tables/pallas_call | solution.py:232
  26.4 0.0 collective-permute-done.before_row
  26.5 3.7 %collective-permute-done.1.after_row = f32[64,128]{1,0:T(8,128)S(1)} collective-permute-done((f32[64,128]{1,0:T(8,128)S(1)}, f32[64,128]{1,0:T(8,128)S(1)}, u32[]{:S(2)}, u32[]{:S(2)}) %collective-permute-start.1) | collective-permute-done | bytes 32800 | tf_op jit(solution)/shard_map/ppermute | solution.py:464
  30.2 7.1 %all-to-all-done.arrived = bf16[32,64,128]{2,1,0:T(8,128)(2,1)S(1)} async-done(((bf16[32,64,128]{2,1,0:T(8,128)(2,1)}), bf16[32,64,128]{2,1,0:T(8,128)(2,1)S(1)}, u32[]{:S(2)}, u32[]{:S(2)}) %all-to-all-start) | async-done | bytes 524320 | tf_op jit(solution)/shard_map/all_to_all | solution.py:476
  37.3 0.0 copy-done.2
  37.3 0.0 copy-done.1
  37.3 1.1 %residual.1 = bf16[32,64,128]{2,1,0:T(8,128)(2,1)} custom-call(bf16[32,64,128]{2,1,0:T(8,128)(2,1)S(1)} %all-to-all-done.arrived, f32[32,128]{1,0:T(8,128)S(1)} %get-tuple-element.28.picks, f32[2,64,128]{2,1,0:T(8,128)S(1)} %copy-done.1, f32[2,64,128]{2,1,0:T(8,128)S(1)} %copy-done.2), custom_call_target="tpu_custom_call" | custom-call | tf_op jit(solution)/shard_map/residual/pallas_call | solution.py:354
  38.4 5.4 %all-to-all-start.1 = ((bf16[32,64,128]{2,1,0:T(8,128)(2,1)}), bf16[32,64,128]{2,1,0:T(8,128)(2,1)}, u32[]{:S(2)}, u32[]{:S(2)}) async-start(bf16[32,64,128]{2,1,0:T(8,128)(2,1)} %residual.1), calls=%async_computation.1 | async-start | bytes 1048576 | tf_op jit(solution)/shard_map/all_to_all | solution.py:489
  43.8 5.3 %collective-permute-start.2 = (f32[98,128]{1,0:T(8,128)S(1)}, f32[98,128]{1,0:T(8,128)S(1)}, u32[]{:S(2)}, u32[]{:S(2)}) collective-permute-start(f32[98,128]{1,0:T(8,128)S(1)} %pad_maximum_fusion), channel_id=1, source_target_pairs={{0,32},{32,64},{64,96},{96,128},{128,160},{160,192},{192,224},{1,3... | collective-permute-start | bytes 150536 | tf_op jit(solution)/shard_map/ppermute | solution.py:464
  49.0 1.9 %collective-permute-start.3 = (f32[98,128]{1,0:T(8,128)S(1)}, f32[98,128]{1,0:T(8,128)S(1)}, u32[]{:S(2)}, u32[]{:S(2)}) collective-permute-start(f32[98,128]{1,0:T(8,128)S(1)} %pad_maximum_fusion.1), channel_id=1, source_target_pairs={{32,0},{64,32},{96,64},{128,96},{160,128},{192,160},{224,192},{33,... | collective-permute-start | bytes 150536 | tf_op jit(solution)/shard_map/ppermute | solution.py:464
  50.9 0.0 collective-permute-done.2.before_slice
  51.0 3.9 %collective-permute-done.3.after_slice = f32[98,128]{1,0:T(8,128)S(1)} collective-permute-done((f32[98,128]{1,0:T(8,128)S(1)}, f32[98,128]{1,0:T(8,128)S(1)}, u32[]{:S(2)}, u32[]{:S(2)}) %collective-permute-start.3) | collective-permute-done | bytes 50208 | tf_op jit(solution)/shard_map/ppermute | solution.py:464
  54.9 12.0 %variation.1.base = f32[64,96,128]{2,1,0:T(8,128)S(1)} custom-call(f32[96,64,128]{2,1,0:T(8,128)} %volume.3, f32[98,128]{1,0:T(8,128)S(1)} %collective-permute-done.2.before_slice, f32[98,128]{1,0:T(8,128)S(1)} %collective-permute-done.3.after_slice, f32[64,128]{1,0:T(8,128)S(1)} %collective-permute-done.before_row, ...), custom_call_target="tpu_custom_call" | custom-call | tf_op jit(solution)/shard_map/variation/pallas_call | solution.py:325
  66.9 0.0 all-to-all-done.1.returned
  66.9 7.9 %backward.1 = f32[96,64,128]{2,1,0:T(8,128)} custom-call(s32[8,128]{1,0:T(8,128)S(1)} %get-tuple-element.20.table, bf16[32,64,128]{2,1,0:T(8,128)(2,1)} %all-to-all-done.1.returned, bf16[32,128,128]{2,1,0:T(8,128)(2,1)} %prints.3, bf16[96,512]{1,0:T(8,128)(2,1)S(1)} %get-tuple-element.29.counts_turned, f32[64,96,128]{2,1,0:T(8,128)S(1)} %variation.1.base), custom_call_target="tpu_custom_call" | custom-call | tf_op jit(solution)/shard_map/backward/pallas_call | solution.py:439
  (4 shorter events, 0.0 us)
Async XLA Ops:
  0.0 25.5 %copy-start.3 = (s32[64]{0:T(128)S(1)}, s32[64]{0:T(128)}, u32[]{:S(2)}) copy-start(s32[64]{0:T(128)} %ray_slot.3) | copy-start | bytes 772
  0.0 25.5 %copy-start = (s32[3072,8]{0,1:T(8,128)S(1)}, s32[3072,8]{0,1:T(8,128)}, u32[]{:S(2)}) copy-start(s32[3072,8]{0,1:T(8,128)} %param.10) | copy-start | bytes 294916
  0.0 37.3 %copy-start.2 = (f32[2,64,128]{2,1,0:T(8,128)S(1)}, f32[2,64,128]{2,1,0:T(8,128)}, u32[]{:S(2)}) copy-start(f32[2,64,128]{2,1,0:T(8,128)} %weights.1) | copy-start | bytes 196612
  0.0 37.3 %copy-start.1 = (f32[2,64,128]{2,1,0:T(8,128)S(1)}, f32[2,64,128]{2,1,0:T(8,128)}, u32[]{:S(2)}) copy-start(f32[2,64,128]{2,1,0:T(8,128)} %measured.1) | copy-start | bytes 196612
  9.1 28.2 %all-to-all-start = ((bf16[32,64,128]{2,1,0:T(8,128)(2,1)}), bf16[32,64,128]{2,1,0:T(8,128)(2,1)S(1)}, u32[]{:S(2)}, u32[]{:S(2)}) async-start(bf16[32,64,128]{2,1,0:T(8,128)(2,1)} %get-tuple-element.21), calls=%async_computation | async-start | bytes 1048576 | tf_op jit(solution)/shard_map/all_to_all | solution.py:476
  21.0 5.4 %collective-permute-start = (f32[64,128]{1,0:T(8,128)S(1)}, f32[64,128]{1,0:T(8,128)S(1)}, u32[]{:S(2)}, u32[]{:S(2)}) collective-permute-start(f32[64,128]{1,0:T(8,128)S(1)} %get-tuple-element.22), channel_id=1, source_target_pairs={{0,1},{1,2},{2,3},{3,4},{4,5},{5,6},{6,7},{7,8},{8,9},{9,10},{10,1... | collective-permute-start | bytes 98312 | tf_op jit(solution)/shard_map/ppermute | solution.py:464
  24.2 6.0 %collective-permute-start.1 = (f32[64,128]{1,0:T(8,128)S(1)}, f32[64,128]{1,0:T(8,128)S(1)}, u32[]{:S(2)}, u32[]{:S(2)}) collective-permute-start(f32[64,128]{1,0:T(8,128)S(1)} %get-tuple-element.34.first_row), channel_id=1, source_target_pairs={{1,0},{2,1},{3,2},{4,3},{5,4},{6,5},{7,6},{8,7},{9,8},{10,9},{11,1... | collective-permute-start | bytes 98312 | tf_op jit(solution)/shard_map/ppermute | solution.py:464
  38.4 28.5 %all-to-all-start.1 = ((bf16[32,64,128]{2,1,0:T(8,128)(2,1)}), bf16[32,64,128]{2,1,0:T(8,128)(2,1)}, u32[]{:S(2)}, u32[]{:S(2)}) async-start(bf16[32,64,128]{2,1,0:T(8,128)(2,1)} %residual.1), calls=%async_computation.1 | async-start | bytes 1048576 | tf_op jit(solution)/shard_map/all_to_all | solution.py:489
  43.8 7.2 %collective-permute-start.2 = (f32[98,128]{1,0:T(8,128)S(1)}, f32[98,128]{1,0:T(8,128)S(1)}, u32[]{:S(2)}, u32[]{:S(2)}) collective-permute-start(f32[98,128]{1,0:T(8,128)S(1)} %pad_maximum_fusion), channel_id=1, source_target_pairs={{0,32},{32,64},{64,96},{96,128},{128,160},{160,192},{192,224},{1,3... | collective-permute-start | bytes 150536 | tf_op jit(solution)/shard_map/ppermute | solution.py:464
  49.0 5.9 %collective-permute-start.3 = (f32[98,128]{1,0:T(8,128)S(1)}, f32[98,128]{1,0:T(8,128)S(1)}, u32[]{:S(2)}, u32[]{:S(2)}) collective-permute-start(f32[98,128]{1,0:T(8,128)S(1)} %pad_maximum_fusion.1), channel_id=1, source_target_pairs={{32,0},{64,32},{96,64},{128,96},{160,128},{192,160},{224,192},{33,... | collective-permute-start | bytes 150536 | tf_op jit(solution)/shard_map/ppermute | solution.py:464

commit v6 on v5

--- a/solution.py
+++ b/solution.py
@@ -242,28 +242,33 @@
     )(ray_slot, blocks, counts)
 
 
-def variation_kernel(
-    volume, before_slice, after_slice, before_row, after_row, first_row,
-    base, by_slice, row_flux, sems,
-):
-    slices, rows, pixels = base.shape
-
-    groups = sems.shape[0]
-    size = slices // groups
-    for z in range(slices):
-        pltpu.make_async_copy(volume.at[:, z, :], by_slice.at[z], sems.at[z // size]).start()
-
-    def wait_group(i):
-        span = by_slice.at[pl.ds(i * size, size)]
-        pltpu.make_async_copy(span, span, sems.at[i]).wait()
-
+def variation_kernel(spans, refs, base, rows_buf, out_buf, slice_flux, in_sems, out_sems):
+    volume, before_slice, after_slice = refs[:3]
+    before_row, after_row = refs[3:5] if len(refs) > 3 else (None, None)
+    rows, slices, pixels = volume.shape
     position = lax.axis_index("tile")
     layer = lax.axis_index("slab")
     last_position = lax.axis_size("tile") - 1
     last_layer = lax.axis_size("slab") - 1
+
+    pieces = []
+    for first, end in spans:
+        pieces += [(r, min(r + 16, end)) for r in range(first, end, 16)]
+    seen = set()
+    loads = []
+    for first, end in pieces:
+        need = [r for r in range(max(first - 1, 0), min(end + 1, rows)) if r not in seen]
+        seen |= set(need)
+        span = pl.ds(need[0], len(need))
+        copy = pltpu.make_async_copy(
+            volume.at[span], rows_buf.at[span], in_sems.at[len(loads)]
+        )
+        copy.start()
+        loads.append(copy)
+
     lane = iota((1, pixels), 1)
     inner = lane < pixels - 1
-    first = lane == 0
+    left_edge = lane == 0
 
     def col_grad(x):
         return jnp.where(inner, pltpu.roll(x, pixels - 1, 1) - x, 0.0)
@@ -271,70 +276,116 @@
     def scale(a, b, c):
         return lax.rsqrt(a * a + b * b + c * c + smoothing)
 
-    low = before_row[...]
     z_id = iota((slices, 1), 0)
-    above = jnp.where(z_id == slices - 1, after_slice[0:1], pltpu.roll(low, slices - 1, 0))
-    grad_slices = above - low
-    grad_slices = jnp.where((z_id == slices - 1) & (layer == last_layer), 0.0, grad_slices)
-    grad_rows = first_row[...] - low
-    flux = grad_rows * scale(grad_rows, grad_slices, col_grad(low))
-    row_flux[...] = jnp.where(position == 0, 0.0, flux)
-
-    row_id = iota((rows, 1), 0)
-    top = row_id == rows - 1
-    bottom = row_id == 0
-    keep = jnp.where(top & (position == last_position), 0.0, 1.0)
-
-    def fluxes(here, next_slice, beyond, last):
-        up = jnp.where(top, beyond, pltpu.roll(here, rows - 1, 0))
-        grad_rows = (up - here) * keep
-        grad_slices = jnp.where(last, 0.0, next_slice - here)
+    top = z_id == slices - 1
+    bottom = z_id == 0
+    keep = jnp.where(top & (layer == last_layer), 0.0, 1.0)
+
+    def fluxes(here, next_row, beyond, last=False):
+        up = jnp.where(top, beyond, pltpu.roll(here, slices - 1, 0))
+        grad_slices = (up - here) * keep
+        grad_rows = jnp.where(last, 0.0, next_row - here)
         grad_cols = col_grad(here)
         inverse = scale(grad_rows, grad_slices, grad_cols)
         return grad_rows * inverse, grad_slices * inverse, grad_cols * inverse
 
-    wait_group(0)
-    _, start, _ = fluxes(
-        before_slice[1 : rows + 1], by_slice[0], before_slice[rows + 1 : rows + 2], False
-    )
-    start = jnp.where(layer == 0, 0.0, start)
-
-    def one(z, here, next_slice, previous, last):
-        flux_rows, flux_slices, flux_cols = fluxes(
-            here, next_slice, after_row[pl.ds(z, 1), :], last
+    stores = []
+    held = None
+    for i, (first, end) in enumerate(pieces):
+        loads[i].wait()
+        count = end - first
+        low = before_slice[first:end]
+        if end < rows:
+            low_next = jnp.concatenate([low[1:], before_slice[end : end + 1]], axis=0)
+        else:
+            low_next = jnp.concatenate([low[1:], after_row[0:1]], axis=0)
+        grad_rows = low_next - low
+        if end == rows:
+            final = (iota((count, 1), 0) == count - 1) & (position == last_position)
+            grad_rows = jnp.where(final, 0.0, grad_rows)
+        bottoms = jnp.concatenate([rows_buf[r, 0:1] for r in range(first, end)], axis=0)
+        grad_slices = bottoms - low
+        flux = grad_slices * scale(grad_rows, grad_slices, col_grad(low))
+        slice_flux[first:end] = jnp.where(layer == 0, 0.0, flux)
+
+        if held is None or pieces[i - 1][1] != first:
+            if first == 0:
+                held, _, _ = fluxes(
+                    before_row[1 : slices + 1], rows_buf[0], before_row[slices + 1 : slices + 2]
+                )
+                held = jnp.where(position == 0, 0.0, held)
+            else:
+                held, _, _ = fluxes(
+                    rows_buf[first - 1], rows_buf[first], after_slice[first - 1 : first]
+                )
+
+        def one(r, here, next_row, previous, last=False):
+            flux_rows, flux_slices, flux_cols = fluxes(
+                here, next_row, after_slice[pl.ds(r, 1), :], last
+            )
+            below = jnp.where(
+                bottom, slice_flux[pl.ds(r, 1), :], pltpu.roll(flux_slices, 1, 0)
+            )
+            left = jnp.where(left_edge, 0.0, pltpu.roll(flux_cols, 1, 1))
+            variation = (previous - flux_rows) + (below - flux_slices) + (left - flux_cols)
+            out_buf[r] = here - (step_length * variation_weight) * variation
+            return flux_rows
+
+        held = lax.fori_loop(
+            first,
+            min(end, rows - 1),
+            lambda r, previous: one(r, rows_buf[r], rows_buf[r + 1], previous),
+            held,
         )
-        below = jnp.where(bottom, row_flux[pl.ds(z, 1), :], pltpu.roll(flux_rows, 1, 0))
-        left = jnp.where(first, 0.0, pltpu.roll(flux_cols, 1, 1))
-        variation = (previous - flux_slices) + (below - flux_rows) + (left - flux_cols)
-        base[z] = here - (step_length * variation_weight) * variation
-        return flux_slices
-
-    def step(z, previous):
-        @pl.when((z + 1) % size == 0)
-        def _():
-            wait_group((z + 1) // size)
-
-        return one(z, by_slice[z], by_slice[z + 1], previous, False)
-
-    final = lax.fori_loop(0, slices - 1, step, start)
-    one(slices - 1, by_slice[slices - 1], after_slice[1 : rows + 1], final, layer == last_layer)
-
-
-def variation(volume, *halos):
-    rows, slices, pixels = volume.shape
+        if end == rows:
+            one(
+                rows - 1, rows_buf[rows - 1], after_row[1 : slices + 1], held,
+                position == last_position,
+            )
+        span = pl.ds(first, count)
+        copy = pltpu.make_async_copy(out_buf.at[span], base.at[span], out_sems.at[i])
+        copy.start()
+        stores.append(copy)
+    for copy in stores:
+        copy.wait()
+
+
+def variation_first_kernel(volume, before_slice, after_slice, base, *scratch):
+    spans = [(8, volume.shape[0] // 2 + 8)]
+    variation_kernel(spans, (volume, before_slice, after_slice), base, *scratch)
+
+
+def variation_rest_kernel(part, *refs):
+    rows = refs[0].shape[0]
+    spans = [(rows // 2 + 8, rows), (0, 8)]
+    variation_kernel(spans, refs[:5], *refs[5:])
+
+
+def variation_call(kernel, aliases, volume, begin, halos):
+    rows, _, pixels = volume.shape
     return pl.pallas_call(
-        variation_kernel,
-        out_shape=jax.ShapeDtypeStruct((slices, rows, pixels), F32),
-        in_specs=[HBM] + [VMEM] * 5,
-        out_specs=VMEM,
+        kernel,
+        out_shape=pltpu.HBM(volume.shape, F32),
+        in_specs=[HBM] * (len(begin) + 1) + [VMEM] * len(halos),
+        out_specs=HBM,
         scratch_shapes=[
-            pltpu.VMEM((slices, rows, pixels), F32),
-            pltpu.VMEM((slices, pixels), F32),
+            pltpu.VMEM(volume.shape, F32),
+            pltpu.VMEM(volume.shape, F32),
+            pltpu.VMEM((rows, pixels), F32),
+            pltpu.SemaphoreType.DMA((8,)),
             pltpu.SemaphoreType.DMA((8,)),
         ],
-        compiler_params=pltpu.CompilerParams(vmem_limit_bytes=8 << 20),
-        name="variation",
-    )(*in_hbm(volume), *halos)
+        input_output_aliases=aliases,
+        compiler_params=pltpu.CompilerParams(vmem_limit_bytes=16 << 20),
+    )(*in_hbm(*begin, volume), *halos)
+
+
+def variation_first(volume, *halos):
+    return variation_call(variation_first_kernel, {}, volume, (), halos)
+
+
+def variation_rest(part, volume, *halos):
+    return variation_call(variation_rest_kernel, {0: 0}, volume, (part,), halos)
 
 
 def residual_kernel(arrived, picks, measured, weights, returned):
@@ -363,9 +414,9 @@
 
 def backward_kernel(
     touch, table, returned, prints, counts_turned, base,
-    out, gathered, mixed, spread, out_buf, prints_buf, sems, prints_sems,
+    out, gathered, mixed, spread, base_buf, out_buf, prints_buf, sems, prints_sems, base_sems,
 ):
-    slices, _, pixels = base.shape
+    _, slices, pixels = base.shape
     foot_count, _, rays = prints.shape
     parts = prints_sems.shape[0]
     per_part = foot_count // parts
@@ -376,12 +427,19 @@
 
     for g in range(parts):
         prints_copy(g).start()
+    half = slices // 2
+    groups = sems.shape[0]
+    group_size = half // groups
+    for z in range(half):
+        for z in (z, z + half):
+            pltpu.make_async_copy(
+                base.at[:, z, :], base_buf.at[z], base_sems.at[z % half // group_size]
+            ).start()
     for s in range(touch):
         owner = table[1, s]
         block = returned[jnp.maximum(owner, 0)].astype(F32)
         gathered[s] = jnp.where(owner >= 0, block, 0.0)
     mixed[...] = jnp.swapaxes(gathered[...], 0, 1).reshape(slices * touch, rays).astype(BF16)
-    half = slices // 2
     block = 256
     zero = jnp.zeros(prints.shape[1:], BF16)
 
@@ -410,18 +468,17 @@
                         i * touch : (i + 1) * touch
                     ]
 
-    groups = sems.shape[0]
-    group_size = half // groups
-
     @pl.loop(0, groups)
     def _(i):
+        arrived = base_buf.at[pl.ds(0, 2 * group_size)]
+        pltpu.make_async_copy(arrived, arrived, base_sems.at[i]).wait()
         for j in range(group_size):
             z = i * group_size + j
             grad = jnp.dot(counts_turned[...], spread[z], preferred_element_type=F32)
             for g in range(2):
                 at = z + g * half
                 out_buf[at] = jnp.maximum(
-                    base[at] - step_length * grad[:, g * pixels : (g + 1) * pixels], 0.0
+                    base_buf[at] - step_length * grad[:, g * pixels : (g + 1) * pixels], 0.0
                 )
         for j in range(group_size):
             for g in range(2):
@@ -434,25 +491,27 @@
 
 
 def backward(touch, table, returned, prints, counts_turned, base):
-    slices, rows, pixels = base.shape
+    rows, slices, pixels = base.shape
     codes = prints.shape[0] * touch
     return pl.pallas_call(
         functools.partial(backward_kernel, touch),
         out_shape=jax.ShapeDtypeStruct((rows, slices, pixels), F32),
-        in_specs=[SMEM, VMEM, HBM, VMEM, VMEM],
+        in_specs=[SMEM, VMEM, HBM, VMEM, HBM],
         out_specs=HBM,
         scratch_shapes=[
             pltpu.VMEM((touch, slices, prints.shape[2]), F32),
             pltpu.VMEM((slices * touch, prints.shape[2]), BF16),
             pltpu.VMEM((slices // 2, codes, 2 * pixels), BF16),
             pltpu.VMEM((slices, rows, pixels), F32),
+            pltpu.VMEM((slices, rows, pixels), F32),
             pltpu.VMEM(prints.shape, BF16),
+            pltpu.SemaphoreType.DMA((4,)),
             pltpu.SemaphoreType.DMA((4,)),
             pltpu.SemaphoreType.DMA((4,)),
         ],
         compiler_params=pltpu.CompilerParams(vmem_limit_bytes=24 << 20),
         name="backward",
-    )(table, returned, *in_hbm(prints), counts_turned, base)
+    )(table, returned, *in_hbm(prints), counts_turned, *in_hbm(base))
 
 
 def shifted(x, axis, forward_way):
@@ -465,7 +524,7 @@
 
 
 def per_device(volume, footprints, foot_index, ray_block, ray_slot, measured, weights):
-    row_count, slice_count, _ = volume.shape
+    row_count, _, _ = volume.shape
     owners = lax.axis_size("tile")
     owned = measured.shape[0]
     touch = owners // 2
@@ -474,23 +533,27 @@
         touch, owned, owners, ray_slot, blocks, foot_index.T, volume, footprints
     )
     arrived = lax.all_to_all(sent, "tile", split_axis=0, concat_axis=0, tiled=True)
-    before_row = shifted(last_row, "tile", True)
-    after_row = shifted(first_row, "tile", False)
+    before_slice = shifted(tail, "slab", True)
+    after_slice = shifted(head, "slab", False)
     counts_turned, picks = tables(owned, owners, row_count, ray_slot, blocks, counts)
-
-    def edge(z, x):
-        return jnp.concatenate([before_row[z : z + 1], x, after_row[z : z + 1]], axis=0)
-
-    edges = (edge(slice_count - 1, tail), edge(0, head))
-    before_slice = shifted(edges[0], "slab", True)
-    after_slice = shifted(edges[1], "slab", False)
+    part = variation_first(volume, before_slice, after_slice)
+
+    def edge(r, x):
+        return jnp.concatenate(
+            [before_slice[r : r + 1], x, after_slice[r : r + 1]], axis=0
+        )
+
+    edges = (edge(row_count - 1, last_row), edge(0, first_row))
+    edges, part = lax.optimization_barrier((edges, part))
+    before_row = shifted(edges[0], "tile", True)
+    after_row = shifted(edges[1], "tile", False)
     arrived, _ = lax.optimization_barrier((arrived, edges))
     answer = residual(arrived, picks, measured, weights)
     returned = lax.all_to_all(answer, "tile", split_axis=0, concat_axis=0, tiled=True)
-    halos, _ = lax.optimization_barrier(
-        ((before_slice, after_slice, before_row, after_row, first_row), answer)
+    halos, part, _ = lax.optimization_barrier(
+        ((before_slice, after_slice, before_row, after_row), part, answer)
     )
-    base = variation(volume, *halos)
+    base = variation_rest(part, volume, *halos)
     return backward(touch, table, returned, footprints, counts_turned, base)
 
 

time: 75.2 us -> 83.9 us (1.12)
  the two profiles are of different devices: /device:TPU:1 before, /device:TPU:49 now
where the time goes in v6:
time: 83.9 us; the launch traced here: 83.4 us
  Pallas kernels  40 us (48%)
  starting transfers between devices  33.2 us (40%)
  waiting for transfers between devices  10.1 us (12%)
    pallas_call x2, Pallas kernels, variation_call(): pl.pallas_call(kernel, out_shape=pltpu.HBM(volume.shape, F32), in_specs=[...  20 us
    ppermute x4, starting transfers between devices, shifted(): return lax.ppermute(x, axis, pairs)  13.3 us
    all_to_all x1, starting transfers between devices, per_device(): lax.all_to_all(sent, 'tile', split_axis=0, concat_axis=0, tiled=True)  10.7 us
    ppermute x4, waiting for transfers between devices, shifted(): return lax.ppermute(x, axis, pairs)  10.1 us
    all_to_all x1, starting transfers between devices, per_device(): lax.all_to_all(answer, 'tile', split_axis=0, concat_axis=0, tiled=True)  9.21 us
    pallas_call x1, Pallas kernels, forward(): pl.pallas_call(functools.partial(forward_kernel, touch, owned), out_shape...  9.1 us
    pallas_call x1, Pallas kernels, backward(): pl.pallas_call(functools.partial(backward_kernel, touch), out_shape=jax.S...  8.84 us
  transfers between devices with their start and end apart: 6, of which 2 were waited for; matrix products, arithmetic and copies ran while one was open for 0% of the time, Pallas kernels for 25%

profile of v6, /device:TPU:49, one launch (start us, length us, event | category | flops | bytes accessed | tf_op | source)
XLA Modules:
  0.0 83.4 jit_solution(7168938166426060814)
XLA Ops:
  0.0 0.0 copy-start.3
  0.0 0.0 copy-start
  0.0 9.1 %forward.1 = (bf16[32,64,128]{2,1,0:T(8,128)(2,1)}, s32[8,128]{1,0:T(8,128)S(1)}, bf16[512,128]{1,0:T(8,128)(2,1)S(1)}, f32[96,128]{1,0:T(8,128)S(1)}, f32[96,12...) custom-call(s32[64]{0:T(128)} %ray_slot.3, s32[8,3072]{1,0:T(8,128)} %bitcast.2, s32[8,96]{1,0:T(8,128)} %bitcast.4, ...), custom_call_target="tpu_custom_call" | custom-call | tf_op jit(solution)/shard_map/forward/pallas_call | solution.py:174
  9.1 10.7 %all-to-all-start = ((bf16[32,64,128]{2,1,0:T(8,128)(2,1)}), bf16[32,64,128]{2,1,0:T(8,128)(2,1)S(1)}, u32[]{:S(2)}, u32[]{:S(2)}) async-start(bf16[32,64,128]{2,1,0:T(8,128)(2,1)} %get-tuple-element.24), calls=%async_computation | async-start | bytes 1048576 | tf_op jit(solution)/shard_map/all_to_all | solution.py:535
  19.8 4.0 %collective-permute-start = (f32[96,128]{1,0:T(8,128)S(1)}, f32[96,128]{1,0:T(8,128)S(1)}, u32[]{:S(2)}, u32[]{:S(2)}) collective-permute-start(f32[96,128]{1,0:T(8,128)S(1)} %get-tuple-element.25), channel_id=1, source_target_pairs={{0,32},{32,64},{64,96},{96,128},{128,160},{160,192},{192,224},{1,3... | collective-permute-start | bytes 147464 | tf_op jit(solution)/shard_map/ppermute | solution.py:523
  23.8 1.9 %collective-permute-start.1 = (f32[96,128]{1,0:T(8,128)S(1)}, f32[96,128]{1,0:T(8,128)S(1)}, u32[]{:S(2)}, u32[]{:S(2)}) collective-permute-start(f32[96,128]{1,0:T(8,128)S(1)} %get-tuple-element.27), channel_id=1, source_target_pairs={{32,0},{64,32},{96,64},{128,96},{160,128},{192,160},{224,192},{33,... | collective-permute-start | bytes 147464 | tf_op jit(solution)/shard_map/ppermute | solution.py:523
  25.7 0.0 copy-done.3
  25.7 0.0 copy-done
  25.7 1.0 %tables.1 = (bf16[96,512]{1,0:T(8,128)(2,1)S(1)}, f32[32,128]{1,0:T(8,128)S(1)}) custom-call(s32[64]{0:T(128)S(1)} %copy-done.3, s32[8,3072]{1,0:T(8,128)S(1)} %bitcast.3, bf16[512,128]{1,0:T(8,128)(2,1)S(1)} %get-tuple-element.32.counts), custom_call_target="tpu_custom_call" | custom-call | tf_op jit(solution)/shard_map/tables/pallas_call | solution.py:232
  26.7 0.0 copy-start.1
  26.7 0.0 copy-start.2
  26.7 0.0 collective-permute-done.before_slice.refs_1_
  26.7 2.8 %collective-permute-done.1.after_slice.refs_2_ = f32[96,128]{1,0:T(8,128)S(1)} collective-permute-done((f32[96,128]{1,0:T(8,128)S(1)}, f32[96,128]{1,0:T(8,128)S(1)}, u32[]{:S(2)}, u32[]{:S(2)}) %collective-permute-start.1) | collective-permute-done | bytes 49184 | tf_op jit(solution)/shard_map/ppermute | solution.py:523
  29.5 10.0 %shard_map.73.part = f32[96,64,128]{2,1,0:T(8,128)} custom-call(f32[96,64,128]{2,1,0:T(8,128)} %refs_0_.1, f32[96,128]{1,0:T(8,128)S(1)} %collective-permute-done.before_slice.refs_1_, f32[96,128]{1,0:T(8,128)S(1)} %collective-permute-done.1.after_slice.refs_2_), custom_call_target="tpu_custom_call" | custom-call | tf_op jit(solution)/shard_map/pallas_call | solution.py:366
  39.6 0.0 all-to-all-done.arrived
  39.6 0.0 copy-done.1
  39.6 0.0 copy-done.2
  39.6 1.1 %residual.1 = bf16[32,64,128]{2,1,0:T(8,128)(2,1)} custom-call(bf16[32,64,128]{2,1,0:T(8,128)(2,1)S(1)} %all-to-all-done.arrived, f32[32,128]{1,0:T(8,128)S(1)} %get-tuple-element.33.picks, f32[2,64,128]{2,1,0:T(8,128)S(1)} %copy-done.1, f32[2,64,128]{2,1,0:T(8,128)S(1)} %copy-done.2), custom_call_target="tpu_custom_call" | custom-call | tf_op jit(solution)/shard_map/residual/pallas_call | solution.py:405
  40.7 9.2 %all-to-all-start.1 = ((bf16[32,64,128]{2,1,0:T(8,128)(2,1)}), bf16[32,64,128]{2,1,0:T(8,128)(2,1)S(1)}, u32[]{:S(2)}, u32[]{:S(2)}) async-start(bf16[32,64,128]{2,1,0:T(8,128)(2,1)} %residual.1), calls=%async_computation.1 | async-start | bytes 1048576 | tf_op jit(solution)/shard_map/all_to_all | solution.py:552
  49.9 3.1 %collective-permute-start.2 = (f32[66,128]{1,0:T(8,128)S(1)}, f32[66,128]{1,0:T(8,128)S(1)}, u32[]{:S(2)}, u32[]{:S(2)}) collective-permute-start(f32[66,128]{1,0:T(8,128)S(1)} %get-tuple-element.29), channel_id=1, source_target_pairs={{0,1},{1,2},{2,3},{3,4},{4,5},{5,6},{6,7},{7,8},{8,9},{9,10},{10,1... | collective-permute-start | bytes 101384 | tf_op jit(solution)/shard_map/ppermute | solution.py:523
  53.0 4.3 %collective-permute-start.3 = (f32[66,128]{1,0:T(8,128)S(1)}, f32[66,128]{1,0:T(8,128)S(1)}, u32[]{:S(2)}, u32[]{:S(2)}) collective-permute-start(f32[66,128]{1,0:T(8,128)S(1)} %get-tuple-element.30), channel_id=1, source_target_pairs={{1,0},{2,1},{3,2},{4,3},{5,4},{6,5},{7,6},{8,7},{9,8},{10,9},{11,1... | collective-permute-start | bytes 101384 | tf_op jit(solution)/shard_map/ppermute | solution.py:523
  57.3 7.3 %collective-permute-done.2.refs_3_ = f32[66,128]{1,0:T(8,128)S(1)} collective-permute-done((f32[66,128]{1,0:T(8,128)S(1)}, f32[66,128]{1,0:T(8,128)S(1)}, u32[]{:S(2)}, u32[]{:S(2)}) %collective-permute-start.2) | collective-permute-done | bytes 33824 | tf_op jit(solution)/shard_map/ppermute | solution.py:523
  64.6 0.0 collective-permute-done.3.refs_4_
  64.6 10.0 %shard_map.74.base = f32[96,64,128]{2,1,0:T(8,128)} custom-call(f32[96,64,128]{2,1,0:T(8,128)} %shard_map.73.part, f32[96,64,128]{2,1,0:T(8,128)} %refs_0_.1, f32[96,128]{1,0:T(8,128)S(1)} %collective-permute-done.before_slice.refs_1_, f32[96,128]{1,0:T(8,128)S(1)} %collective-permute-done.1.after_slice.refs_2_, ...), custom_call_target="tpu_custom_call", output_to_operand_aliasing={{}: (0, {})} | custom-call | tf_op jit(solution)/shard_map/pallas_call | solution.py:366
  74.6 0.0 all-to-all-done.1.returned
  74.6 8.8 %backward.1 = f32[96,64,128]{2,1,0:T(8,128)} custom-call(s32[8,128]{1,0:T(8,128)S(1)} %get-tuple-element.23.table, bf16[32,64,128]{2,1,0:T(8,128)(2,1)S(1)} %all-to-all-done.1.returned, bf16[32,128,128]{2,1,0:T(8,128)(2,1)} %prints.3, bf16[96,512]{1,0:T(8,128)(2,1)S(1)} %get-tuple-element.34.counts_turned, f32[96,64,128]{2,1,0:T(8,128)} %shard_map.74.base), custom_call_target="tpu_custom_call" | custom-call | tf_op jit(solution)/shard_map/backward/pallas_call | solution.py:496
  (3 shorter events, 0.0 us)
Async XLA Ops:
  0.0 25.7 %copy-start.3 = (s32[64]{0:T(128)S(1)}, s32[64]{0:T(128)}, u32[]{:S(2)}) copy-start(s32[64]{0:T(128)} %ray_slot.3) | copy-start | bytes 772
  0.0 25.7 %copy-start = (s32[3072,8]{0,1:T(8,128)S(1)}, s32[3072,8]{0,1:T(8,128)}, u32[]{:S(2)}) copy-start(s32[3072,8]{0,1:T(8,128)} %param.10) | copy-start | bytes 294916
  9.1 30.5 %all-to-all-start = ((bf16[32,64,128]{2,1,0:T(8,128)(2,1)}), bf16[32,64,128]{2,1,0:T(8,128)(2,1)S(1)}, u32[]{:S(2)}, u32[]{:S(2)}) async-start(bf16[32,64,128]{2,1,0:T(8,128)(2,1)} %get-tuple-element.24), calls=%async_computation | async-start | bytes 1048576 | tf_op jit(solution)/shard_map/all_to_all | solution.py:535
  19.8 6.9 %collective-permute-start = (f32[96,128]{1,0:T(8,128)S(1)}, f32[96,128]{1,0:T(8,128)S(1)}, u32[]{:S(2)}, u32[]{:S(2)}) collective-permute-start(f32[96,128]{1,0:T(8,128)S(1)} %get-tuple-element.25), channel_id=1, source_target_pairs={{0,32},{32,64},{64,96},{96,128},{128,160},{160,192},{192,224},{1,3... | collective-permute-start | bytes 147464 | tf_op jit(solution)/shard_map/ppermute | solution.py:523
  23.8 5.7 %collective-permute-start.1 = (f32[96,128]{1,0:T(8,128)S(1)}, f32[96,128]{1,0:T(8,128)S(1)}, u32[]{:S(2)}, u32[]{:S(2)}) collective-permute-start(f32[96,128]{1,0:T(8,128)S(1)} %get-tuple-element.27), channel_id=1, source_target_pairs={{32,0},{64,32},{96,64},{128,96},{160,128},{192,160},{224,192},{33,... | collective-permute-start | bytes 147464 | tf_op jit(solution)/shard_map/ppermute | solution.py:523
  26.7 12.9 %copy-start.1 = (f32[2,64,128]{2,1,0:T(8,128)S(1)}, f32[2,64,128]{2,1,0:T(8,128)}, u32[]{:S(2)}) copy-start(f32[2,64,128]{2,1,0:T(8,128)} %measured.1) | copy-start | bytes 196612
  26.7 12.9 %copy-start.2 = (f32[2,64,128]{2,1,0:T(8,128)S(1)}, f32[2,64,128]{2,1,0:T(8,128)}, u32[]{:S(2)}) copy-start(f32[2,64,128]{2,1,0:T(8,128)} %weights.1) | copy-start | bytes 196612
  40.7 33.9 %all-to-all-start.1 = ((bf16[32,64,128]{2,1,0:T(8,128)(2,1)}), bf16[32,64,128]{2,1,0:T(8,128)(2,1)S(1)}, u32[]{:S(2)}, u32[]{:S(2)}) async-start(bf16[32,64,128]{2,1,0:T(8,128)(2,1)} %residual.1), calls=%async_computation.1 | async-start | bytes 1048576 | tf_op jit(solution)/shard_map/all_to_all | solution.py:552
  49.9 14.7 %collective-permute-start.2 = (f32[66,128]{1,0:T(8,128)S(1)}, f32[66,128]{1,0:T(8,128)S(1)}, u32[]{:S(2)}, u32[]{:S(2)}) collective-permute-start(f32[66,128]{1,0:T(8,128)S(1)} %get-tuple-element.29), channel_id=1, source_target_pairs={{0,1},{1,2},{2,3},{3,4},{4,5},{5,6},{6,7},{7,8},{8,9},{9,10},{10,1... | collective-permute-start | bytes 101384 | tf_op jit(solution)/shard_map/ppermute | solution.py:523
  53.0 11.6 %collective-permute-start.3 = (f32[66,128]{1,0:T(8,128)S(1)}, f32[66,128]{1,0:T(8,128)S(1)}, u32[]{:S(2)}, u32[]{:S(2)}) collective-permute-start(f32[66,128]{1,0:T(8,128)S(1)} %get-tuple-element.30), channel_id=1, source_target_pairs={{1,0},{2,1},{3,2},{4,3},{5,4},{6,5},{7,6},{8,7},{9,8},{10,9},{11,1... | collective-permute-start | bytes 101384 | tf_op jit(solution)/shard_map/ppermute | solution.py:523

commit v7 on v5

--- a/solution.py
+++ b/solution.py
@@ -271,10 +271,9 @@
     def scale(a, b, c):
         return lax.rsqrt(a * a + b * b + c * c + smoothing)
 
-    low = before_row[...]
+    low = before_row[1 : slices + 1]
     z_id = iota((slices, 1), 0)
-    above = jnp.where(z_id == slices - 1, after_slice[0:1], pltpu.roll(low, slices - 1, 0))
-    grad_slices = above - low
+    grad_slices = before_row[2 : slices + 2] - low
     grad_slices = jnp.where((z_id == slices - 1) & (layer == last_layer), 0.0, grad_slices)
     grad_rows = first_row[...] - low
     flux = grad_rows * scale(grad_rows, grad_slices, col_grad(low))
@@ -294,14 +293,12 @@
         return grad_rows * inverse, grad_slices * inverse, grad_cols * inverse
 
     wait_group(0)
-    _, start, _ = fluxes(
-        before_slice[1 : rows + 1], by_slice[0], before_slice[rows + 1 : rows + 2], False
-    )
+    _, start, _ = fluxes(before_slice[...], by_slice[0], after_row[0:1], False)
     start = jnp.where(layer == 0, 0.0, start)
 
     def one(z, here, next_slice, previous, last):
         flux_rows, flux_slices, flux_cols = fluxes(
-            here, next_slice, after_row[pl.ds(z, 1), :], last
+            here, next_slice, after_row[pl.ds(z + 1, 1), :], last
         )
         below = jnp.where(bottom, row_flux[pl.ds(z, 1), :], pltpu.roll(flux_rows, 1, 0))
         left = jnp.where(first, 0.0, pltpu.roll(flux_cols, 1, 1))
@@ -317,7 +314,7 @@
         return one(z, by_slice[z], by_slice[z + 1], previous, False)
 
     final = lax.fori_loop(0, slices - 1, step, start)
-    one(slices - 1, by_slice[slices - 1], after_slice[1 : rows + 1], final, layer == last_layer)
+    one(slices - 1, by_slice[slices - 1], after_slice[...], final, layer == last_layer)
 
 
 def variation(volume, *halos):
@@ -465,7 +462,7 @@
 
 
 def per_device(volume, footprints, foot_index, ray_block, ray_slot, measured, weights):
-    row_count, slice_count, _ = volume.shape
+    row_count, _, _ = volume.shape
     owners = lax.axis_size("tile")
     owned = measured.shape[0]
     touch = owners // 2
@@ -474,16 +471,18 @@
         touch, owned, owners, ray_slot, blocks, foot_index.T, volume, footprints
     )
     arrived = lax.all_to_all(sent, "tile", split_axis=0, concat_axis=0, tiled=True)
-    before_row = shifted(last_row, "tile", True)
-    after_row = shifted(first_row, "tile", False)
+    before_slice = shifted(tail, "slab", True)
+    after_slice = shifted(head, "slab", False)
     counts_turned, picks = tables(owned, owners, row_count, ray_slot, blocks, counts)
 
-    def edge(z, x):
-        return jnp.concatenate([before_row[z : z + 1], x, after_row[z : z + 1]], axis=0)
-
-    edges = (edge(slice_count - 1, tail), edge(0, head))
-    before_slice = shifted(edges[0], "slab", True)
-    after_slice = shifted(edges[1], "slab", False)
+    def edge(r, x):
+        return jnp.concatenate(
+            [before_slice[r : r + 1], x, after_slice[r : r + 1]], axis=0
+        )
+
+    edges = (edge(row_count - 1, last_row), edge(0, first_row))
+    before_row = shifted(edges[0], "tile", True)
+    after_row = shifted(edges[1], "tile", False)
     arrived, _ = lax.optimization_barrier((arrived, edges))
     answer = residual(arrived, picks, measured, weights)
     returned = lax.all_to_all(answer, "tile", split_axis=0, concat_axis=0, tiled=True)

time: 75.2 us -> 77.6 us (1.032)
  the two profiles are of different devices: /device:TPU:1 before, /device:TPU:56 now
where the time goes in v7:
time: 77.6 us; the launch traced here: 77.2 us
  Pallas kernels  31 us (40%)
  starting transfers between devices  28.5 us (37%)
  waiting for transfers between devices  17.5 us (23%)
    ppermute x4, starting transfers between devices, shifted(): return lax.ppermute(x, axis, pairs)  12.1 us
    pallas_call x1, Pallas kernels, variation(): pl.pallas_call(variation_kernel, out_shape=jax.ShapeDtypeStruct((slices,...  12 us
    all_to_all x1, starting transfers between devices, per_device(): lax.all_to_all(sent, 'tile', split_axis=0, concat_axis=0, tiled=True)  11.2 us
    all_to_all x1, waiting for transfers between devices, per_device(): lax.all_to_all(sent, 'tile', split_axis=0, concat_axis=0, tiled=True)  9.86 us
    pallas_call x1, Pallas kernels, forward(): pl.pallas_call(functools.partial(forward_kernel, touch, owned), out_shape...  9.14 us
    pallas_call x1, Pallas kernels, backward(): pl.pallas_call(functools.partial(backward_kernel, touch), out_shape=jax.S...  7.86 us
    ppermute x4, waiting for transfers between devices, shifted(): return lax.ppermute(x, axis, pairs)  7.62 us
    all_to_all x1, starting transfers between devices, per_device(): lax.all_to_all(answer, 'tile', split_axis=0, concat_axis=0, tiled=True)  5.26 us
  transfers between devices with their start and end apart: 6, of which 4 were waited for; matrix products, arithmetic and copies ran while one was open for 0% of the time, Pallas kernels for 17%

profile of v7, /device:TPU:56, one launch (start us, length us, event | category | flops | bytes accessed | tf_op | source)
XLA Modules:
  0.0 77.2 jit_solution(1924730981557175180)
XLA Ops:
  0.0 0.0 copy-start.3
  0.0 0.0 copy-start
  0.0 0.0 copy-start.2
  0.0 0.0 copy-start.1
  0.0 9.1 %forward.1 = (bf16[32,64,128]{2,1,0:T(8,128)(2,1)}, s32[8,128]{1,0:T(8,128)S(1)}, bf16[512,128]{1,0:T(8,128)(2,1)S(1)}, f32[96,128]{1,0:T(8,128)S(1)}, f32[96,12...) custom-call(s32[64]{0:T(128)} %ray_slot.3, s32[8,3072]{1,0:T(8,128)} %bitcast.2, s32[8,96]{1,0:T(8,128)} %bitcast.4, ...), custom_call_target="tpu_custom_call" | custom-call | tf_op jit(solution)/shard_map/forward/pallas_call | solution.py:174
  9.2 11.2 %all-to-all-start = ((bf16[32,64,128]{2,1,0:T(8,128)(2,1)}), bf16[32,64,128]{2,1,0:T(8,128)(2,1)S(1)}, u32[]{:S(2)}, u32[]{:S(2)}) async-start(bf16[32,64,128]{2,1,0:T(8,128)(2,1)} %get-tuple-element.21), calls=%async_computation | async-start | bytes 1048576 | tf_op jit(solution)/shard_map/all_to_all | solution.py:473
  20.3 1.9 %collective-permute-start = (f32[96,128]{1,0:T(8,128)S(1)}, f32[96,128]{1,0:T(8,128)S(1)}, u32[]{:S(2)}, u32[]{:S(2)}) collective-permute-start(f32[96,128]{1,0:T(8,128)S(1)} %get-tuple-element.22), channel_id=1, source_target_pairs={{0,32},{32,64},{64,96},{96,128},{128,160},{160,192},{192,224},{1,3... | collective-permute-start | bytes 147464 | tf_op jit(solution)/shard_map/ppermute | solution.py:461
  22.3 3.6 %collective-permute-start.1 = (f32[96,128]{1,0:T(8,128)S(1)}, f32[96,128]{1,0:T(8,128)S(1)}, u32[]{:S(2)}, u32[]{:S(2)}) collective-permute-start(f32[96,128]{1,0:T(8,128)S(1)} %get-tuple-element.24), channel_id=1, source_target_pairs={{32,0},{64,32},{96,64},{128,96},{160,128},{192,160},{224,192},{33,... | collective-permute-start | bytes 147464 | tf_op jit(solution)/shard_map/ppermute | solution.py:461
  25.9 0.0 copy-done.3
  25.9 0.0 copy-done
  25.9 1.0 %tables.1 = (bf16[96,512]{1,0:T(8,128)(2,1)S(1)}, f32[32,128]{1,0:T(8,128)S(1)}) custom-call(s32[64]{0:T(128)S(1)} %copy-done.3, s32[8,3072]{1,0:T(8,128)S(1)} %bitcast.3, bf16[512,128]{1,0:T(8,128)(2,1)S(1)} %get-tuple-element.27.counts), custom_call_target="tpu_custom_call" | custom-call | tf_op jit(solution)/shard_map/tables/pallas_call | solution.py:232
  26.9 0.0 collective-permute-done.before_slice
  26.9 0.7 collective-permute-done.1.after_slice
  27.7 9.9 %all-to-all-done.arrived = bf16[32,64,128]{2,1,0:T(8,128)(2,1)S(1)} async-done(((bf16[32,64,128]{2,1,0:T(8,128)(2,1)}), bf16[32,64,128]{2,1,0:T(8,128)(2,1)S(1)}, u32[]{:S(2)}, u32[]{:S(2)}) %all-to-all-start) | async-done | bytes 524320 | tf_op jit(solution)/shard_map/all_to_all | solution.py:473
  37.5 0.0 copy-done.2
  37.5 0.0 copy-done.1
  37.5 1.1 %residual.1 = bf16[32,64,128]{2,1,0:T(8,128)(2,1)} custom-call(bf16[32,64,128]{2,1,0:T(8,128)(2,1)S(1)} %all-to-all-done.arrived, f32[32,128]{1,0:T(8,128)S(1)} %get-tuple-element.28.picks, f32[2,64,128]{2,1,0:T(8,128)S(1)} %copy-done.1, f32[2,64,128]{2,1,0:T(8,128)S(1)} %copy-done.2), custom_call_target="tpu_custom_call" | custom-call | tf_op jit(solution)/shard_map/residual/pallas_call | solution.py:351
  38.6 5.3 %all-to-all-start.1 = ((bf16[32,64,128]{2,1,0:T(8,128)(2,1)}), bf16[32,64,128]{2,1,0:T(8,128)(2,1)}, u32[]{:S(2)}, u32[]{:S(2)}) async-start(bf16[32,64,128]{2,1,0:T(8,128)(2,1)} %residual.1), calls=%async_computation.1 | async-start | bytes 1048576 | tf_op jit(solution)/shard_map/all_to_all | solution.py:488
  43.9 4.6 %collective-permute-start.3 = (f32[66,128]{1,0:T(8,128)S(1)}, f32[66,128]{1,0:T(8,128)S(1)}, u32[]{:S(2)}, u32[]{:S(2)}) collective-permute-start(f32[66,128]{1,0:T(8,128)S(1)} %pad_maximum_fusion.1), channel_id=1, source_target_pairs={{1,0},{2,1},{3,2},{4,3},{5,4},{6,5},{7,6},{8,7},{9,8},{10,9},{11,1... | collective-permute-start | bytes 101384 | tf_op jit(solution)/shard_map/ppermute | solution.py:461
  48.5 1.9 %collective-permute-start.2 = (f32[66,128]{1,0:T(8,128)S(1)}, f32[66,128]{1,0:T(8,128)S(1)}, u32[]{:S(2)}, u32[]{:S(2)}) collective-permute-start(f32[66,128]{1,0:T(8,128)S(1)} %pad_maximum_fusion), channel_id=1, source_target_pairs={{0,1},{1,2},{2,3},{3,4},{4,5},{5,6},{6,7},{7,8},{8,9},{9,10},{10,1... | collective-permute-start | bytes 101384 | tf_op jit(solution)/shard_map/ppermute | solution.py:461
  50.4 4.4 %collective-permute-done.3.after_row = f32[66,128]{1,0:T(8,128)S(1)} collective-permute-done((f32[66,128]{1,0:T(8,128)S(1)}, f32[66,128]{1,0:T(8,128)S(1)}, u32[]{:S(2)}, u32[]{:S(2)}) %collective-permute-start.3) | collective-permute-done | bytes 33824 | tf_op jit(solution)/shard_map/ppermute | solution.py:461
  54.7 2.5 %collective-permute-done.2.before_row = f32[66,128]{1,0:T(8,128)S(1)} collective-permute-done((f32[66,128]{1,0:T(8,128)S(1)}, f32[66,128]{1,0:T(8,128)S(1)}, u32[]{:S(2)}, u32[]{:S(2)}) %collective-permute-start.2) | collective-permute-done | bytes 33824 | tf_op jit(solution)/shard_map/ppermute | solution.py:461
  57.3 12.0 %variation.1.base = f32[64,96,128]{2,1,0:T(8,128)S(1)} custom-call(f32[96,64,128]{2,1,0:T(8,128)} %volume.3, f32[96,128]{1,0:T(8,128)S(1)} %collective-permute-done.before_slice, f32[96,128]{1,0:T(8,128)S(1)} %collective-permute-done.1.after_slice, f32[66,128]{1,0:T(8,128)S(1)} %collective-permute-done.2.before_row, ...), custom_call_target="tpu_custom_call" | custom-call | tf_op jit(solution)/shard_map/variation/pallas_call | solution.py:322
  69.3 0.0 all-to-all-done.1.returned
  69.3 7.9 %backward.1 = f32[96,64,128]{2,1,0:T(8,128)} custom-call(s32[8,128]{1,0:T(8,128)S(1)} %get-tuple-element.20.table, bf16[32,64,128]{2,1,0:T(8,128)(2,1)} %all-to-all-done.1.returned, bf16[32,128,128]{2,1,0:T(8,128)(2,1)} %prints.3, bf16[96,512]{1,0:T(8,128)(2,1)S(1)} %get-tuple-element.29.counts_turned, f32[64,96,128]{2,1,0:T(8,128)S(1)} %variation.1.base), custom_call_target="tpu_custom_call" | custom-call | tf_op jit(solution)/shard_map/backward/pallas_call | solution.py:436
  (4 shorter events, 0.0 us)
Async XLA Ops:
  0.0 25.9 %copy-start.3 = (s32[64]{0:T(128)S(1)}, s32[64]{0:T(128)}, u32[]{:S(2)}) copy-start(s32[64]{0:T(128)} %ray_slot.3) | copy-start | bytes 772
  0.0 25.9 %copy-start = (s32[3072,8]{0,1:T(8,128)S(1)}, s32[3072,8]{0,1:T(8,128)}, u32[]{:S(2)}) copy-start(s32[3072,8]{0,1:T(8,128)} %param.10) | copy-start | bytes 294916
  0.0 37.5 %copy-start.2 = (f32[2,64,128]{2,1,0:T(8,128)S(1)}, f32[2,64,128]{2,1,0:T(8,128)}, u32[]{:S(2)}) copy-start(f32[2,64,128]{2,1,0:T(8,128)} %weights.1) | copy-start | bytes 196612
  0.0 37.5 %copy-start.1 = (f32[2,64,128]{2,1,0:T(8,128)S(1)}, f32[2,64,128]{2,1,0:T(8,128)}, u32[]{:S(2)}) copy-start(f32[2,64,128]{2,1,0:T(8,128)} %measured.1) | copy-start | bytes 196612
  9.2 28.4 %all-to-all-start = ((bf16[32,64,128]{2,1,0:T(8,128)(2,1)}), bf16[32,64,128]{2,1,0:T(8,128)(2,1)S(1)}, u32[]{:S(2)}, u32[]{:S(2)}) async-start(bf16[32,64,128]{2,1,0:T(8,128)(2,1)} %get-tuple-element.21), calls=%async_computation | async-start | bytes 1048576 | tf_op jit(solution)/shard_map/all_to_all | solution.py:473
  20.3 6.6 %collective-permute-start = (f32[96,128]{1,0:T(8,128)S(1)}, f32[96,128]{1,0:T(8,128)S(1)}, u32[]{:S(2)}, u32[]{:S(2)}) collective-permute-start(f32[96,128]{1,0:T(8,128)S(1)} %get-tuple-element.22), channel_id=1, source_target_pairs={{0,32},{32,64},{64,96},{96,128},{128,160},{160,192},{192,224},{1,3... | collective-permute-start | bytes 147464 | tf_op jit(solution)/shard_map/ppermute | solution.py:461
  22.3 5.4 %collective-permute-start.1 = (f32[96,128]{1,0:T(8,128)S(1)}, f32[96,128]{1,0:T(8,128)S(1)}, u32[]{:S(2)}, u32[]{:S(2)}) collective-permute-start(f32[96,128]{1,0:T(8,128)S(1)} %get-tuple-element.24), channel_id=1, source_target_pairs={{32,0},{64,32},{96,64},{128,96},{160,128},{192,160},{224,192},{33,... | collective-permute-start | bytes 147464 | tf_op jit(solution)/shard_map/ppermute | solution.py:461
  38.6 30.7 %all-to-all-start.1 = ((bf16[32,64,128]{2,1,0:T(8,128)(2,1)}), bf16[32,64,128]{2,1,0:T(8,128)(2,1)}, u32[]{:S(2)}, u32[]{:S(2)}) async-start(bf16[32,64,128]{2,1,0:T(8,128)(2,1)} %residual.1), calls=%async_computation.1 | async-start | bytes 1048576 | tf_op jit(solution)/shard_map/all_to_all | solution.py:488
  43.9 10.9 %collective-permute-start.3 = (f32[66,128]{1,0:T(8,128)S(1)}, f32[66,128]{1,0:T(8,128)S(1)}, u32[]{:S(2)}, u32[]{:S(2)}) collective-permute-start(f32[66,128]{1,0:T(8,128)S(1)} %pad_maximum_fusion.1), channel_id=1, source_target_pairs={{1,0},{2,1},{3,2},{4,3},{5,4},{6,5},{7,6},{8,7},{9,8},{10,9},{11,1... | collective-permute-start | bytes 101384 | tf_op jit(solution)/shard_map/ppermute | solution.py:461
  48.5 8.8 %collective-permute-start.2 = (f32[66,128]{1,0:T(8,128)S(1)}, f32[66,128]{1,0:T(8,128)S(1)}, u32[]{:S(2)}, u32[]{:S(2)}) collective-permute-start(f32[66,128]{1,0:T(8,128)S(1)} %pad_maximum_fusion), channel_id=1, source_target_pairs={{0,1},{1,2},{2,3},{3,4},{4,5},{5,6},{6,7},{7,8},{8,9},{9,10},{10,1... | collective-permute-start | bytes 101384 | tf_op jit(solution)/shard_map/ppermute | solution.py:461

commit v8 on v7

--- a/solution.py
+++ b/solution.py
@@ -97,7 +97,6 @@
     foots_here = jnp.concatenate(
         [foots_buf[...], jnp.zeros((crossings, lanes - row_count), jnp.int32)], axis=1
     )
-    step = 4
     hits, feet = [], []
     rank_id = iota((touch, lanes), 0)
     for k in range(crossings):
@@ -115,6 +114,8 @@
             terms = [x + y for x, y in zip(terms[::2], terms[1::2])]
         counts[f * touch : (f + 1) * touch] = terms[0]
 
+    wide = 16
+
     @pl.loop(0, groups)
     def _(i):
         both = by_slice.at[pl.ds(0, 2 * group_size)]
@@ -122,13 +123,13 @@
         for j in range(group_size):
             z = i * group_size + j
             pair = jnp.concatenate([by_slice[z], by_slice[z + half]], axis=1).astype(BF16)
-            for first in range(0, foot_count, step):
+            for first in range(0, foot_count, wide):
                 group = jnp.dot(
-                    counts[first * touch : (first + step) * touch, :row_count],
+                    counts[first * touch : (first + wide) * touch, :row_count],
                     pair,
                     preferred_element_type=F32,
                 ).astype(BF16)
-                for f in range(step):
+                for f in range(wide):
                     grouped[first + f, pl.ds(pl.multiple_of(z * touch, touch), touch), :] = group[
                         f * touch : (f + 1) * touch
                     ]
@@ -136,27 +137,20 @@
     head[...] = by_slice[0]
     tail[...] = by_slice[slice_count - 1]
     prints_copy.wait()
-    sums[...] = jnp.zeros_like(sums)
-    deep = 16
     block = 256
     zero = jnp.zeros(prints.shape[1:], BF16)
-
-    @pl.loop(0, foot_count // deep)
-    def _(g):
-        weights = []
-        for h in range(deep):
-            weight = prints_buf[g * deep + h]
-            weights.append(jnp.concatenate([weight, zero], axis=1))
-            weights.append(jnp.concatenate([zero, weight], axis=1))
-        weights = jnp.concatenate(weights, axis=0)
-        for m in range(0, half * touch, block):
-            left = [grouped[g * deep + h, m : m + block, :] for h in range(deep)]
-            both = jnp.dot(
-                jnp.concatenate(left, axis=1), weights, preferred_element_type=F32
-            )
-            rays = both.shape[1] // 2
-            sums[m : m + block] += both[:, :rays]
-            sums[half * touch + m : half * touch + m + block] += both[:, rays:]
+    weights = []
+    for f in range(foot_count):
+        weight = prints_buf[f]
+        weights.append(jnp.concatenate([weight, zero], axis=1))
+        weights.append(jnp.concatenate([zero, weight], axis=1))
+    weights = jnp.concatenate(weights, axis=0)
+    for m in range(0, half * touch, block):
+        left = [grouped[f, m : m + block, :] for f in range(foot_count)]
+        both = jnp.dot(jnp.concatenate(left, axis=1), weights, preferred_element_type=F32)
+        rays = both.shape[1] // 2
+        sums[m : m + block] = both[:, :rays]
+        sums[half * touch + m : half * touch + m + block] = both[:, rays:]
 
     compact[...] = jnp.swapaxes(sums[...].reshape(slice_count, touch, -1), 0, 1).astype(BF16)
     for copy in small[3:]:
@@ -271,9 +265,9 @@
     def scale(a, b, c):
         return lax.rsqrt(a * a + b * b + c * c + smoothing)
 
-    low = before_row[1 : slices + 1]
+    low = before_row[:slices]
     z_id = iota((slices, 1), 0)
-    grad_slices = before_row[2 : slices + 2] - low
+    grad_slices = before_row[1 : slices + 1] - low
     grad_slices = jnp.where((z_id == slices - 1) & (layer == last_layer), 0.0, grad_slices)
     grad_rows = first_row[...] - low
     flux = grad_rows * scale(grad_rows, grad_slices, col_grad(low))
@@ -293,12 +287,12 @@
         return grad_rows * inverse, grad_slices * inverse, grad_cols * inverse
 
     wait_group(0)
-    _, start, _ = fluxes(before_slice[...], by_slice[0], after_row[0:1], False)
+    _, start, _ = fluxes(before_slice[...], by_slice[0], after_row[slices : slices + 1], False)
     start = jnp.where(layer == 0, 0.0, start)
 
     def one(z, here, next_slice, previous, last):
         flux_rows, flux_slices, flux_cols = fluxes(
-            here, next_slice, after_row[pl.ds(z + 1, 1), :], last
+            here, next_slice, after_row[pl.ds(z, 1), :], last
         )
         below = jnp.where(bottom, row_flux[pl.ds(z, 1), :], pltpu.roll(flux_rows, 1, 0))
         left = jnp.where(first, 0.0, pltpu.roll(flux_cols, 1, 1))
@@ -445,7 +439,7 @@
             pltpu.VMEM((slices, rows, pixels), F32),
             pltpu.VMEM(prints.shape, BF16),
             pltpu.SemaphoreType.DMA((4,)),
-            pltpu.SemaphoreType.DMA((4,)),
+            pltpu.SemaphoreType.DMA((2,)),
         ],
         compiler_params=pltpu.CompilerParams(vmem_limit_bytes=24 << 20),
         name="backward",
@@ -475,15 +469,11 @@
     after_slice = shifted(head, "slab", False)
     counts_turned, picks = tables(owned, owners, row_count, ray_slot, blocks, counts)
 
-    def edge(r, x):
-        return jnp.concatenate(
-            [before_slice[r : r + 1], x, after_slice[r : r + 1]], axis=0
-        )
-
-    edges = (edge(row_count - 1, last_row), edge(0, first_row))
-    before_row = shifted(edges[0], "tile", True)
-    after_row = shifted(edges[1], "tile", False)
-    arrived, _ = lax.optimization_barrier((arrived, edges))
+    last_edge = jnp.concatenate([last_row, after_slice[row_count - 1 :]], axis=0)
+    first_edge = jnp.concatenate([first_row, before_slice[:1]], axis=0)
+    before_row = shifted(last_edge, "tile", True)
+    after_row = shifted(first_edge, "tile", False)
+    arrived, _, _ = lax.optimization_barrier((arrived, first_edge, last_edge))
     answer = residual(arrived, picks, measured, weights)
     returned = lax.all_to_all(answer, "tile", split_axis=0, concat_axis=0, tiled=True)
     halos, _ = lax.optimization_barrier(

time: 77.6 us -> 77 us (level)
  no operation moved by 1% of the time
where the time goes in v8:
time: 77 us; the launch traced here: 76.6 us
  Pallas kernels  30.4 us (39%)
  starting transfers between devices  28.5 us (37%)
  waiting for transfers between devices  17.5 us (23%)
    ppermute x4, starting transfers between devices, shifted(): return lax.ppermute(x, axis, pairs)  12.1 us
    pallas_call x1, Pallas kernels, variation(): pl.pallas_call(variation_kernel, out_shape=jax.ShapeDtypeStruct((slices,...  12 us
    all_to_all x1, starting transfers between devices, per_device(): lax.all_to_all(sent, 'tile', split_axis=0, concat_axis=0, tiled=True)  11.2 us
    all_to_all x1, waiting for transfers between devices, per_device(): lax.all_to_all(sent, 'tile', split_axis=0, concat_axis=0, tiled=True)  9.86 us
    pallas_call x1, Pallas kernels, forward(): pl.pallas_call(functools.partial(forward_kernel, touch, owned), out_shape...  8.82 us
    ppermute x4, waiting for transfers between devices, shifted(): return lax.ppermute(x, axis, pairs)  7.62 us
    pallas_call x1, Pallas kernels, backward(): pl.pallas_call(functools.partial(backward_kernel, touch), out_shape=jax.S...  7.52 us
    all_to_all x1, starting transfers between devices, per_device(): lax.all_to_all(answer, 'tile', split_axis=0, concat_axis=0, tiled=True)  5.26 us
  transfers between devices with their start and end apart: 6, of which 4 were waited for; matrix products, arithmetic and copies ran while one was open for 0% of the time, Pallas kernels for 17%

profile of v8, /device:TPU:56, one launch (start us, length us, event | category | flops | bytes accessed | tf_op | source)
XLA Modules:
  0.0 76.6 jit_solution(15671709945064418025)
XLA Ops:
  0.0 0.0 copy-start.3
  0.0 0.0 copy-start
  0.0 0.0 copy-start.2
  0.0 0.0 copy-start.1
  0.0 8.8 %forward.1 = (bf16[32,64,128]{2,1,0:T(8,128)(2,1)}, s32[8,128]{1,0:T(8,128)S(1)}, bf16[512,128]{1,0:T(8,128)(2,1)S(1)}, f32[96,128]{1,0:T(8,128)S(1)}, f32[96,12...) custom-call(s32[64]{0:T(128)} %ray_slot.3, s32[8,3072]{1,0:T(8,128)} %bitcast.2, s32[8,96]{1,0:T(8,128)} %bitcast.4, ...), custom_call_target="tpu_custom_call" | custom-call | tf_op jit(solution)/shard_map/forward/pallas_call | solution.py:168
  8.8 11.2 %all-to-all-start = ((bf16[32,64,128]{2,1,0:T(8,128)(2,1)}), bf16[32,64,128]{2,1,0:T(8,128)(2,1)S(1)}, u32[]{:S(2)}, u32[]{:S(2)}) async-start(bf16[32,64,128]{2,1,0:T(8,128)(2,1)} %get-tuple-element.21), calls=%async_computation | async-start | bytes 1048576 | tf_op jit(solution)/shard_map/all_to_all | solution.py:467
  20.1 1.9 %collective-permute-start = (f32[96,128]{1,0:T(8,128)S(1)}, f32[96,128]{1,0:T(8,128)S(1)}, u32[]{:S(2)}, u32[]{:S(2)}) collective-permute-start(f32[96,128]{1,0:T(8,128)S(1)} %get-tuple-element.23), channel_id=1, source_target_pairs={{0,32},{32,64},{64,96},{96,128},{128,160},{160,192},{192,224},{1,3... | collective-permute-start | bytes 147464 | tf_op jit(solution)/shard_map/ppermute | solution.py:455
  22.0 3.6 %collective-permute-start.1 = (f32[96,128]{1,0:T(8,128)S(1)}, f32[96,128]{1,0:T(8,128)S(1)}, u32[]{:S(2)}, u32[]{:S(2)}) collective-permute-start(f32[96,128]{1,0:T(8,128)S(1)} %get-tuple-element.25), channel_id=1, source_target_pairs={{32,0},{64,32},{96,64},{128,96},{160,128},{192,160},{224,192},{33,... | collective-permute-start | bytes 147464 | tf_op jit(solution)/shard_map/ppermute | solution.py:455
  25.6 0.0 copy-done.3
  25.6 0.0 copy-done
  25.7 1.0 %tables.1 = (bf16[96,512]{1,0:T(8,128)(2,1)S(1)}, f32[32,128]{1,0:T(8,128)S(1)}) custom-call(s32[64]{0:T(128)S(1)} %copy-done.3, s32[8,3072]{1,0:T(8,128)S(1)} %bitcast.3, bf16[512,128]{1,0:T(8,128)(2,1)S(1)} %get-tuple-element.27.counts), custom_call_target="tpu_custom_call" | custom-call | tf_op jit(solution)/shard_map/tables/pallas_call | solution.py:226
  26.6 0.0 collective-permute-done.before_slice
  26.6 0.7 collective-permute-done.1.after_slice
  27.4 9.9 %all-to-all-done.arrived = bf16[32,64,128]{2,1,0:T(8,128)(2,1)S(1)} async-done(((bf16[32,64,128]{2,1,0:T(8,128)(2,1)}), bf16[32,64,128]{2,1,0:T(8,128)(2,1)S(1)}, u32[]{:S(2)}, u32[]{:S(2)}) %all-to-all-start) | async-done | bytes 524320 | tf_op jit(solution)/shard_map/all_to_all | solution.py:467
  37.3 0.0 copy-done.2
  37.3 0.0 copy-done.1
  37.3 1.1 %residual.1 = bf16[32,64,128]{2,1,0:T(8,128)(2,1)} custom-call(bf16[32,64,128]{2,1,0:T(8,128)(2,1)S(1)} %all-to-all-done.arrived, f32[32,128]{1,0:T(8,128)S(1)} %get-tuple-element.28.picks, f32[2,64,128]{2,1,0:T(8,128)S(1)} %copy-done.1, f32[2,64,128]{2,1,0:T(8,128)S(1)} %copy-done.2), custom_call_target="tpu_custom_call" | custom-call | tf_op jit(solution)/shard_map/residual/pallas_call | solution.py:345
  38.3 5.3 %all-to-all-start.1 = ((bf16[32,64,128]{2,1,0:T(8,128)(2,1)}), bf16[32,64,128]{2,1,0:T(8,128)(2,1)}, u32[]{:S(2)}, u32[]{:S(2)}) async-start(bf16[32,64,128]{2,1,0:T(8,128)(2,1)} %residual.1), calls=%async_computation.1 | async-start | bytes 1048576 | tf_op jit(solution)/shard_map/all_to_all | solution.py:478
  43.6 4.6 %collective-permute-start.3 = (f32[65,128]{1,0:T(8,128)S(1)}, f32[65,128]{1,0:T(8,128)S(1)}, u32[]{:S(2)}, u32[]{:S(2)}) collective-permute-start(f32[65,128]{1,0:T(8,128)S(1)} %pad_maximum_fusion), channel_id=1, source_target_pairs={{1,0},{2,1},{3,2},{4,3},{5,4},{6,5},{7,6},{8,7},{9,8},{10,9},{11,1... | collective-permute-start | bytes 99848 | tf_op jit(solution)/shard_map/ppermute | solution.py:455
  48.2 1.9 %collective-permute-start.2 = (f32[65,128]{1,0:T(8,128)S(1)}, f32[65,128]{1,0:T(8,128)S(1)}, u32[]{:S(2)}, u32[]{:S(2)}) collective-permute-start(f32[65,128]{1,0:T(8,128)S(1)} %pad_maximum_fusion.1), channel_id=1, source_target_pairs={{0,1},{1,2},{2,3},{3,4},{4,5},{5,6},{6,7},{7,8},{8,9},{9,10},{10,1... | collective-permute-start | bytes 99848 | tf_op jit(solution)/shard_map/ppermute | solution.py:455
  50.1 4.4 %collective-permute-done.3.after_row = f32[65,128]{1,0:T(8,128)S(1)} collective-permute-done((f32[65,128]{1,0:T(8,128)S(1)}, f32[65,128]{1,0:T(8,128)S(1)}, u32[]{:S(2)}, u32[]{:S(2)}) %collective-permute-start.3) | collective-permute-done | bytes 33312 | tf_op jit(solution)/shard_map/ppermute | solution.py:455
  54.5 2.5 %collective-permute-done.2.before_row = f32[65,128]{1,0:T(8,128)S(1)} collective-permute-done((f32[65,128]{1,0:T(8,128)S(1)}, f32[65,128]{1,0:T(8,128)S(1)}, u32[]{:S(2)}, u32[]{:S(2)}) %collective-permute-start.2) | collective-permute-done | bytes 33312 | tf_op jit(solution)/shard_map/ppermute | solution.py:455
  57.0 12.0 %variation.1.base = f32[64,96,128]{2,1,0:T(8,128)S(1)} custom-call(f32[96,64,128]{2,1,0:T(8,128)} %volume.3, f32[96,128]{1,0:T(8,128)S(1)} %collective-permute-done.before_slice, f32[96,128]{1,0:T(8,128)S(1)} %collective-permute-done.1.after_slice, f32[65,128]{1,0:T(8,128)S(1)} %collective-permute-done.2.before_row, ...), custom_call_target="tpu_custom_call" | custom-call | tf_op jit(solution)/shard_map/variation/pallas_call | solution.py:316
  69.0 0.0 all-to-all-done.1.returned
  69.0 7.5 %backward.1 = f32[96,64,128]{2,1,0:T(8,128)} custom-call(s32[8,128]{1,0:T(8,128)S(1)} %get-tuple-element.20.table, bf16[32,64,128]{2,1,0:T(8,128)(2,1)} %all-to-all-done.1.returned, bf16[32,128,128]{2,1,0:T(8,128)(2,1)} %prints.3, bf16[96,512]{1,0:T(8,128)(2,1)S(1)} %get-tuple-element.29.counts_turned, f32[64,96,128]{2,1,0:T(8,128)S(1)} %variation.1.base), custom_call_target="tpu_custom_call" | custom-call | tf_op jit(solution)/shard_map/backward/pallas_call | solution.py:430
  (4 shorter events, 0.0 us)
Async XLA Ops:
  0.0 25.6 %copy-start.3 = (s32[64]{0:T(128)S(1)}, s32[64]{0:T(128)}, u32[]{:S(2)}) copy-start(s32[64]{0:T(128)} %ray_slot.3) | copy-start | bytes 772
  0.0 25.6 %copy-start = (s32[3072,8]{0,1:T(8,128)S(1)}, s32[3072,8]{0,1:T(8,128)}, u32[]{:S(2)}) copy-start(s32[3072,8]{0,1:T(8,128)} %param.10) | copy-start | bytes 294916
  0.0 37.3 %copy-start.2 = (f32[2,64,128]{2,1,0:T(8,128)S(1)}, f32[2,64,128]{2,1,0:T(8,128)}, u32[]{:S(2)}) copy-start(f32[2,64,128]{2,1,0:T(8,128)} %weights.1) | copy-start | bytes 196612
  0.0 37.3 %copy-start.1 = (f32[2,64,128]{2,1,0:T(8,128)S(1)}, f32[2,64,128]{2,1,0:T(8,128)}, u32[]{:S(2)}) copy-start(f32[2,64,128]{2,1,0:T(8,128)} %measured.1) | copy-start | bytes 196612
  8.8 28.4 %all-to-all-start = ((bf16[32,64,128]{2,1,0:T(8,128)(2,1)}), bf16[32,64,128]{2,1,0:T(8,128)(2,1)S(1)}, u32[]{:S(2)}, u32[]{:S(2)}) async-start(bf16[32,64,128]{2,1,0:T(8,128)(2,1)} %get-tuple-element.21), calls=%async_computation | async-start | bytes 1048576 | tf_op jit(solution)/shard_map/all_to_all | solution.py:467
  20.1 6.6 %collective-permute-start = (f32[96,128]{1,0:T(8,128)S(1)}, f32[96,128]{1,0:T(8,128)S(1)}, u32[]{:S(2)}, u32[]{:S(2)}) collective-permute-start(f32[96,128]{1,0:T(8,128)S(1)} %get-tuple-element.23), channel_id=1, source_target_pairs={{0,32},{32,64},{64,96},{96,128},{128,160},{160,192},{192,224},{1,3... | collective-permute-start | bytes 147464 | tf_op jit(solution)/shard_map/ppermute | solution.py:455
  22.0 5.4 %collective-permute-start.1 = (f32[96,128]{1,0:T(8,128)S(1)}, f32[96,128]{1,0:T(8,128)S(1)}, u32[]{:S(2)}, u32[]{:S(2)}) collective-permute-start(f32[96,128]{1,0:T(8,128)S(1)} %get-tuple-element.25), channel_id=1, source_target_pairs={{32,0},{64,32},{96,64},{128,96},{160,128},{192,160},{224,192},{33,... | collective-permute-start | bytes 147464 | tf_op jit(solution)/shard_map/ppermute | solution.py:455
  38.3 30.7 %all-to-all-start.1 = ((bf16[32,64,128]{2,1,0:T(8,128)(2,1)}), bf16[32,64,128]{2,1,0:T(8,128)(2,1)}, u32[]{:S(2)}, u32[]{:S(2)}) async-start(bf16[32,64,128]{2,1,0:T(8,128)(2,1)} %residual.1), calls=%async_computation.1 | async-start | bytes 1048576 | tf_op jit(solution)/shard_map/all_to_all | solution.py:478
  43.6 10.9 %collective-permute-start.3 = (f32[65,128]{1,0:T(8,128)S(1)}, f32[65,128]{1,0:T(8,128)S(1)}, u32[]{:S(2)}, u32[]{:S(2)}) collective-permute-start(f32[65,128]{1,0:T(8,128)S(1)} %pad_maximum_fusion), channel_id=1, source_target_pairs={{1,0},{2,1},{3,2},{4,3},{5,4},{6,5},{7,6},{8,7},{9,8},{10,9},{11,1... | collective-permute-start | bytes 99848 | tf_op jit(solution)/shard_map/ppermute | solution.py:455
  48.2 8.8 %collective-permute-start.2 = (f32[65,128]{1,0:T(8,128)S(1)}, f32[65,128]{1,0:T(8,128)S(1)}, u32[]{:S(2)}, u32[]{:S(2)}) collective-permute-start(f32[65,128]{1,0:T(8,128)S(1)} %pad_maximum_fusion.1), channel_id=1, source_target_pairs={{0,1},{1,2},{2,3},{3,4},{4,5},{5,6},{6,7},{7,8},{8,9},{9,10},{10,1... | collective-permute-start | bytes 99848 | tf_op jit(solution)/shard_map/ppermute | solution.py:455

commit v9 on v8

--- a/solution.py
+++ b/solution.py
@@ -32,6 +32,7 @@
     touch, owned, ray_slot, blocks, foots, volume, prints,
     sent, table, counts, head, tail, first_row, last_row,
     window, foots_buf, slot_buf, by_slice, prints_buf, grouped, sums, compact, table_buf,
+    sent_buf, sent_sem,
     sems, small_sems, table_sem, prints_sem,
 ):
     row_count, slice_count, _ = volume.shape
@@ -159,7 +160,11 @@
     for t in range(owners):
         place = table[0, t]
         block = compact[jnp.maximum(place, 0)]
-        sent[t] = jnp.where(place >= 0, block, jnp.zeros_like(block))
+        sent_buf[t] = jnp.where(place >= 0, block, jnp.zeros_like(block))
+        if t % 4 == 3:
+            span = pl.ds(t - 3, 4)
+            pltpu.make_async_copy(sent_buf.at[span], sent.at[span], sent_sem).start()
+    pltpu.make_async_copy(sent_buf, sent, sent_sem).wait()
 
 
 def forward(touch, owned, owners, ray_slot, blocks, foots, volume, prints):
@@ -177,7 +182,7 @@
             jax.ShapeDtypeStruct((slices, pixels), F32),
         ),
         in_specs=[HBM] * 5,
-        out_specs=(VMEM, SMEM) + (VMEM,) * 5,
+        out_specs=(HBM, SMEM) + (VMEM,) * 5,
         scratch_shapes=[
             pltpu.VMEM((blocks.shape[0], 2 * lanes), jnp.int32),
             pltpu.VMEM(foots.shape, jnp.int32),
@@ -188,6 +193,8 @@
             pltpu.VMEM((slices * touch, rays), F32),
             pltpu.VMEM((touch, slices, rays), BF16),
             pltpu.VMEM((8, lanes), jnp.int32),
+            pltpu.VMEM((owners, slices, rays), BF16),
+            pltpu.SemaphoreType.DMA,
             pltpu.SemaphoreType.DMA((4,)),
             pltpu.SemaphoreType.DMA((5,)),
             pltpu.SemaphoreType.DMA,
@@ -328,7 +335,7 @@
     )(*in_hbm(volume), *halos)
 
 
-def residual_kernel(arrived, picks, measured, weights, returned):
+def residual_kernel(arrived, picks, measured, weights, returned, answer, sem):
     owners = arrived.shape[0]
     sums = [jnp.zeros(measured.shape[1:], F32) for _ in range(2)]
     for j in range(owners):
@@ -338,7 +345,11 @@
         sums[1] = sums[1] + jnp.where(chosen, part, 0.0)
     out = [(weights[i] * (sums[i] - measured[i])).astype(BF16).astype(F32) for i in range(2)]
     for j in range(owners):
-        returned[j] = jnp.where(picks[j : j + 1, :] > 0.5, out[1], out[0]).astype(BF16)
+        answer[j] = jnp.where(picks[j : j + 1, :] > 0.5, out[1], out[0]).astype(BF16)
+        if j % 4 == 3:
+            span = pl.ds(j - 3, 4)
+            pltpu.make_async_copy(answer.at[span], returned.at[span], sem).start()
+    pltpu.make_async_copy(answer, returned, sem).wait()
 
 
 def residual(arrived, picks, measured, weights):
@@ -346,7 +357,8 @@
         residual_kernel,
         out_shape=jax.ShapeDtypeStruct(arrived.shape, BF16),
         in_specs=[VMEM] * 4,
-        out_specs=VMEM,
+        out_specs=HBM,
+        scratch_shapes=[pltpu.VMEM(arrived.shape, BF16), pltpu.SemaphoreType.DMA],
         compiler_params=pltpu.CompilerParams(vmem_limit_bytes=4 << 20),
         name="residual",
     )(arrived, picks, measured, weights)
@@ -414,10 +426,9 @@
                 out_buf[at] = jnp.maximum(
                     base[at] - step_length * grad[:, g * pixels : (g + 1) * pixels], 0.0
                 )
-        for j in range(group_size):
-            for g in range(2):
-                at = i * group_size + j + g * half
-                pltpu.make_async_copy(out_buf.at[at], out.at[:, at, :], sems.at[i]).start()
+            if j % 4 == 3:
+                for at in [z - 3 + k + g * half for k in range(4) for g in range(2)]:
+                    pltpu.make_async_copy(out_buf.at[at], out.at[:, at, :], sems.at[i]).start()
 
     for i in range(groups):
         both = out_buf.at[pl.ds(0, 2 * group_size)]

time: 77 us -> 77.3 us (level)
  no operation moved by 1% of the time
where the time goes in v9:
time: 77.3 us; the launch traced here: 76.9 us
  Pallas kernels  30.7 us (40%)
  starting transfers between devices  28.5 us (37%)
  waiting for transfers between devices  17.5 us (23%)
    ppermute x4, starting transfers between devices, shifted(): return lax.ppermute(x, axis, pairs)  12.1 us
    pallas_call x1, Pallas kernels, variation(): pl.pallas_call(variation_kernel, out_shape=jax.ShapeDtypeStruct((slices,...  12 us
    all_to_all x1, starting transfers between devices, per_device(): lax.all_to_all(sent, 'tile', split_axis=0, concat_axis=0, tiled=True)  11.2 us
    all_to_all x1, waiting for transfers between devices, per_device(): lax.all_to_all(sent, 'tile', split_axis=0, concat_axis=0, tiled=True)  9.85 us
    pallas_call x1, Pallas kernels, forward(): pl.pallas_call(functools.partial(forward_kernel, touch, owned), out_shape...  9.32 us
    ppermute x4, waiting for transfers between devices, shifted(): return lax.ppermute(x, axis, pairs)  7.62 us
    pallas_call x1, Pallas kernels, backward(): pl.pallas_call(functools.partial(backward_kernel, touch), out_shape=jax.S...  7.38 us
    all_to_all x1, starting transfers between devices, per_device(): lax.all_to_all(answer, 'tile', split_axis=0, concat_axis=0, tiled=True)  5.27 us
  transfers between devices with their start and end apart: 6, of which 4 were waited for; matrix products, arithmetic and copies ran while one was open for 0% of the time, Pallas kernels for 17%

profile of v9, /device:TPU:56, one launch (start us, length us, event | category | flops | bytes accessed | tf_op | source)
XLA Modules:
  0.0 76.9 jit_solution(13300172731285763867)
XLA Ops:
  0.0 0.0 copy-start.3
  0.0 0.0 copy-start
  0.0 0.0 copy-start.2
  0.0 0.0 copy-start.1
  0.0 9.3 %forward.1 = (bf16[32,64,128]{2,1,0:T(8,128)(2,1)}, s32[8,128]{1,0:T(8,128)S(1)}, bf16[512,128]{1,0:T(8,128)(2,1)S(1)}, f32[96,128]{1,0:T(8,128)S(1)}, f32[96,12...) custom-call(s32[64]{0:T(128)} %ray_slot.3, s32[8,3072]{1,0:T(8,128)} %bitcast.2, s32[8,96]{1,0:T(8,128)} %bitcast.4, ...), custom_call_target="tpu_custom_call" | custom-call | tf_op jit(solution)/shard_map/forward/pallas_call | solution.py:173
  9.3 11.2 %all-to-all-start = ((bf16[32,64,128]{2,1,0:T(8,128)(2,1)}), bf16[32,64,128]{2,1,0:T(8,128)(2,1)S(1)}, u32[]{:S(2)}, u32[]{:S(2)}) async-start(bf16[32,64,128]{2,1,0:T(8,128)(2,1)} %get-tuple-element.21), calls=%async_computation | async-start | bytes 1048576 | tf_op jit(solution)/shard_map/all_to_all | solution.py:478
  20.6 1.9 %collective-permute-start = (f32[96,128]{1,0:T(8,128)S(1)}, f32[96,128]{1,0:T(8,128)S(1)}, u32[]{:S(2)}, u32[]{:S(2)}) collective-permute-start(f32[96,128]{1,0:T(8,128)S(1)} %get-tuple-element.23), channel_id=1, source_target_pairs={{0,32},{32,64},{64,96},{96,128},{128,160},{160,192},{192,224},{1,3... | collective-permute-start | bytes 147464 | tf_op jit(solution)/shard_map/ppermute | solution.py:466
  22.5 3.6 %collective-permute-start.1 = (f32[96,128]{1,0:T(8,128)S(1)}, f32[96,128]{1,0:T(8,128)S(1)}, u32[]{:S(2)}, u32[]{:S(2)}) collective-permute-start(f32[96,128]{1,0:T(8,128)S(1)} %get-tuple-element.25), channel_id=1, source_target_pairs={{32,0},{64,32},{96,64},{128,96},{160,128},{192,160},{224,192},{33,... | collective-permute-start | bytes 147464 | tf_op jit(solution)/shard_map/ppermute | solution.py:466
  26.1 0.0 copy-done.3
  26.2 0.0 copy-done
  26.2 1.0 %tables.1 = (bf16[96,512]{1,0:T(8,128)(2,1)S(1)}, f32[32,128]{1,0:T(8,128)S(1)}) custom-call(s32[64]{0:T(128)S(1)} %copy-done.3, s32[8,3072]{1,0:T(8,128)S(1)} %bitcast.3, bf16[512,128]{1,0:T(8,128)(2,1)S(1)} %get-tuple-element.27.counts), custom_call_target="tpu_custom_call" | custom-call | tf_op jit(solution)/shard_map/tables/pallas_call | solution.py:233
  27.1 0.0 collective-permute-done.before_slice
  27.2 0.7 collective-permute-done.1.after_slice
  27.9 9.9 %all-to-all-done.arrived = bf16[32,64,128]{2,1,0:T(8,128)(2,1)S(1)} async-done(((bf16[32,64,128]{2,1,0:T(8,128)(2,1)}), bf16[32,64,128]{2,1,0:T(8,128)(2,1)S(1)}, u32[]{:S(2)}, u32[]{:S(2)}) %all-to-all-start) | async-done | bytes 524320 | tf_op jit(solution)/shard_map/all_to_all | solution.py:478
  37.8 0.0 copy-done.2
  37.8 0.0 copy-done.1
  37.8 1.0 %residual.1 = bf16[32,64,128]{2,1,0:T(8,128)(2,1)} custom-call(bf16[32,64,128]{2,1,0:T(8,128)(2,1)S(1)} %all-to-all-done.arrived, f32[32,128]{1,0:T(8,128)S(1)} %get-tuple-element.28.picks, f32[2,64,128]{2,1,0:T(8,128)S(1)} %copy-done.1, f32[2,64,128]{2,1,0:T(8,128)S(1)} %copy-done.2), custom_call_target="tpu_custom_call" | custom-call | tf_op jit(solution)/shard_map/residual/pallas_call | solution.py:356
  38.8 5.3 %all-to-all-start.1 = ((bf16[32,64,128]{2,1,0:T(8,128)(2,1)}), bf16[32,64,128]{2,1,0:T(8,128)(2,1)}, u32[]{:S(2)}, u32[]{:S(2)}) async-start(bf16[32,64,128]{2,1,0:T(8,128)(2,1)} %residual.1), calls=%async_computation.1 | async-start | bytes 1048576 | tf_op jit(solution)/shard_map/all_to_all | solution.py:489
  44.0 4.6 %collective-permute-start.3 = (f32[65,128]{1,0:T(8,128)S(1)}, f32[65,128]{1,0:T(8,128)S(1)}, u32[]{:S(2)}, u32[]{:S(2)}) collective-permute-start(f32[65,128]{1,0:T(8,128)S(1)} %pad_maximum_fusion), channel_id=1, source_target_pairs={{1,0},{2,1},{3,2},{4,3},{5,4},{6,5},{7,6},{8,7},{9,8},{10,9},{11,1... | collective-permute-start | bytes 99848 | tf_op jit(solution)/shard_map/ppermute | solution.py:466
  48.6 1.9 %collective-permute-start.2 = (f32[65,128]{1,0:T(8,128)S(1)}, f32[65,128]{1,0:T(8,128)S(1)}, u32[]{:S(2)}, u32[]{:S(2)}) collective-permute-start(f32[65,128]{1,0:T(8,128)S(1)} %pad_maximum_fusion.1), channel_id=1, source_target_pairs={{0,1},{1,2},{2,3},{3,4},{4,5},{5,6},{6,7},{7,8},{8,9},{9,10},{10,1... | collective-permute-start | bytes 99848 | tf_op jit(solution)/shard_map/ppermute | solution.py:466
  50.6 4.4 %collective-permute-done.3.after_row = f32[65,128]{1,0:T(8,128)S(1)} collective-permute-done((f32[65,128]{1,0:T(8,128)S(1)}, f32[65,128]{1,0:T(8,128)S(1)}, u32[]{:S(2)}, u32[]{:S(2)}) %collective-permute-start.3) | collective-permute-done | bytes 33312 | tf_op jit(solution)/shard_map/ppermute | solution.py:466
  54.9 2.5 %collective-permute-done.2.before_row = f32[65,128]{1,0:T(8,128)S(1)} collective-permute-done((f32[65,128]{1,0:T(8,128)S(1)}, f32[65,128]{1,0:T(8,128)S(1)}, u32[]{:S(2)}, u32[]{:S(2)}) %collective-permute-start.2) | collective-permute-done | bytes 33312 | tf_op jit(solution)/shard_map/ppermute | solution.py:466
  57.5 12.0 %variation.1.base = f32[64,96,128]{2,1,0:T(8,128)S(1)} custom-call(f32[96,64,128]{2,1,0:T(8,128)} %volume.3, f32[96,128]{1,0:T(8,128)S(1)} %collective-permute-done.before_slice, f32[96,128]{1,0:T(8,128)S(1)} %collective-permute-done.1.after_slice, f32[65,128]{1,0:T(8,128)S(1)} %collective-permute-done.2.before_row, ...), custom_call_target="tpu_custom_call" | custom-call | tf_op jit(solution)/shard_map/variation/pallas_call | solution.py:323
  69.5 0.0 all-to-all-done.1.returned
  69.5 7.4 %backward.1 = f32[96,64,128]{2,1,0:T(8,128)} custom-call(s32[8,128]{1,0:T(8,128)S(1)} %get-tuple-element.20.table, bf16[32,64,128]{2,1,0:T(8,128)(2,1)} %all-to-all-done.1.returned, bf16[32,128,128]{2,1,0:T(8,128)(2,1)} %prints.3, bf16[96,512]{1,0:T(8,128)(2,1)S(1)} %get-tuple-element.29.counts_turned, f32[64,96,128]{2,1,0:T(8,128)S(1)} %variation.1.base), custom_call_target="tpu_custom_call" | custom-call | tf_op jit(solution)/shard_map/backward/pallas_call | solution.py:441
  (4 shorter events, 0.0 us)
Async XLA Ops:
  0.0 26.2 %copy-start.3 = (s32[64]{0:T(128)S(1)}, s32[64]{0:T(128)}, u32[]{:S(2)}) copy-start(s32[64]{0:T(128)} %ray_slot.3) | copy-start | bytes 772
  0.0 26.2 %copy-start = (s32[3072,8]{0,1:T(8,128)S(1)}, s32[3072,8]{0,1:T(8,128)}, u32[]{:S(2)}) copy-start(s32[3072,8]{0,1:T(8,128)} %param.10) | copy-start | bytes 294916
  0.0 37.8 %copy-start.2 = (f32[2,64,128]{2,1,0:T(8,128)S(1)}, f32[2,64,128]{2,1,0:T(8,128)}, u32[]{:S(2)}) copy-start(f32[2,64,128]{2,1,0:T(8,128)} %weights.1) | copy-start | bytes 196612
  0.0 37.8 %copy-start.1 = (f32[2,64,128]{2,1,0:T(8,128)S(1)}, f32[2,64,128]{2,1,0:T(8,128)}, u32[]{:S(2)}) copy-start(f32[2,64,128]{2,1,0:T(8,128)} %measured.1) | copy-start | bytes 196612
  9.3 28.4 %all-to-all-start = ((bf16[32,64,128]{2,1,0:T(8,128)(2,1)}), bf16[32,64,128]{2,1,0:T(8,128)(2,1)S(1)}, u32[]{:S(2)}, u32[]{:S(2)}) async-start(bf16[32,64,128]{2,1,0:T(8,128)(2,1)} %get-tuple-element.21), calls=%async_computation | async-start | bytes 1048576 | tf_op jit(solution)/shard_map/all_to_all | solution.py:478
  20.6 6.6 %collective-permute-start = (f32[96,128]{1,0:T(8,128)S(1)}, f32[96,128]{1,0:T(8,128)S(1)}, u32[]{:S(2)}, u32[]{:S(2)}) collective-permute-start(f32[96,128]{1,0:T(8,128)S(1)} %get-tuple-element.23), channel_id=1, source_target_pairs={{0,32},{32,64},{64,96},{96,128},{128,160},{160,192},{192,224},{1,3... | collective-permute-start | bytes 147464 | tf_op jit(solution)/shard_map/ppermute | solution.py:466
  22.5 5.4 %collective-permute-start.1 = (f32[96,128]{1,0:T(8,128)S(1)}, f32[96,128]{1,0:T(8,128)S(1)}, u32[]{:S(2)}, u32[]{:S(2)}) collective-permute-start(f32[96,128]{1,0:T(8,128)S(1)} %get-tuple-element.25), channel_id=1, source_target_pairs={{32,0},{64,32},{96,64},{128,96},{160,128},{192,160},{224,192},{33,... | collective-permute-start | bytes 147464 | tf_op jit(solution)/shard_map/ppermute | solution.py:466
  38.8 30.7 %all-to-all-start.1 = ((bf16[32,64,128]{2,1,0:T(8,128)(2,1)}), bf16[32,64,128]{2,1,0:T(8,128)(2,1)}, u32[]{:S(2)}, u32[]{:S(2)}) async-start(bf16[32,64,128]{2,1,0:T(8,128)(2,1)} %residual.1), calls=%async_computation.1 | async-start | bytes 1048576 | tf_op jit(solution)/shard_map/all_to_all | solution.py:489
  44.0 10.9 %collective-permute-start.3 = (f32[65,128]{1,0:T(8,128)S(1)}, f32[65,128]{1,0:T(8,128)S(1)}, u32[]{:S(2)}, u32[]{:S(2)}) collective-permute-start(f32[65,128]{1,0:T(8,128)S(1)} %pad_maximum_fusion), channel_id=1, source_target_pairs={{1,0},{2,1},{3,2},{4,3},{5,4},{6,5},{7,6},{8,7},{9,8},{10,9},{11,1... | collective-permute-start | bytes 99848 | tf_op jit(solution)/shard_map/ppermute | solution.py:466
  48.6 8.8 %collective-permute-start.2 = (f32[65,128]{1,0:T(8,128)S(1)}, f32[65,128]{1,0:T(8,128)S(1)}, u32[]{:S(2)}, u32[]{:S(2)}) collective-permute-start(f32[65,128]{1,0:T(8,128)S(1)} %pad_maximum_fusion.1), channel_id=1, source_target_pairs={{0,1},{1,2},{2,3},{3,4},{4,5},{5,6},{6,7},{7,8},{8,9},{9,10},{10,1... | collective-permute-start | bytes 99848 | tf_op jit(solution)/shard_map/ppermute | solution.py:466

commit v10 on v9

--- a/solution.py
+++ b/solution.py
@@ -32,7 +32,6 @@
     touch, owned, ray_slot, blocks, foots, volume, prints,
     sent, table, counts, head, tail, first_row, last_row,
     window, foots_buf, slot_buf, by_slice, prints_buf, grouped, sums, compact, table_buf,
-    sent_buf, sent_sem,
     sems, small_sems, table_sem, prints_sem,
 ):
     row_count, slice_count, _ = volume.shape
@@ -160,11 +159,7 @@
     for t in range(owners):
         place = table[0, t]
         block = compact[jnp.maximum(place, 0)]
-        sent_buf[t] = jnp.where(place >= 0, block, jnp.zeros_like(block))
-        if t % 4 == 3:
-            span = pl.ds(t - 3, 4)
-            pltpu.make_async_copy(sent_buf.at[span], sent.at[span], sent_sem).start()
-    pltpu.make_async_copy(sent_buf, sent, sent_sem).wait()
+        sent[t] = jnp.where(place >= 0, block, jnp.zeros_like(block))
 
 
 def forward(touch, owned, owners, ray_slot, blocks, foots, volume, prints):
@@ -182,7 +177,7 @@
             jax.ShapeDtypeStruct((slices, pixels), F32),
         ),
         in_specs=[HBM] * 5,
-        out_specs=(HBM, SMEM) + (VMEM,) * 5,
+        out_specs=(VMEM, SMEM) + (VMEM,) * 5,
         scratch_shapes=[
             pltpu.VMEM((blocks.shape[0], 2 * lanes), jnp.int32),
             pltpu.VMEM(foots.shape, jnp.int32),
@@ -193,8 +188,6 @@
             pltpu.VMEM((slices * touch, rays), F32),
             pltpu.VMEM((touch, slices, rays), BF16),
             pltpu.VMEM((8, lanes), jnp.int32),
-            pltpu.VMEM((owners, slices, rays), BF16),
-            pltpu.SemaphoreType.DMA,
             pltpu.SemaphoreType.DMA((4,)),
             pltpu.SemaphoreType.DMA((5,)),
             pltpu.SemaphoreType.DMA,
@@ -366,7 +359,7 @@
 
 def backward_kernel(
     touch, table, returned, prints, counts_turned, base,
-    out, gathered, mixed, spread, out_buf, prints_buf, sems, prints_sems,
+    out, returned_buf, gathered, mixed, spread, out_buf, prints_buf, sems, prints_sems, returned_sem,
 ):
     slices, _, pixels = base.shape
     foot_count, _, rays = prints.shape
@@ -377,11 +370,14 @@
         span = pl.ds(g * per_part, per_part)
         return pltpu.make_async_copy(prints.at[span], prints_buf.at[span], prints_sems.at[g])
 
+    returned_copy = pltpu.make_async_copy(returned, returned_buf, returned_sem)
+    returned_copy.start()
     for g in range(parts):
         prints_copy(g).start()
+    returned_copy.wait()
     for s in range(touch):
         owner = table[1, s]
-        block = returned[jnp.maximum(owner, 0)].astype(F32)
+        block = returned_buf[jnp.maximum(owner, 0)].astype(F32)
         gathered[s] = jnp.where(owner >= 0, block, 0.0)
     mixed[...] = jnp.swapaxes(gathered[...], 0, 1).reshape(slices * touch, rays).astype(BF16)
     half = slices // 2
@@ -441,9 +437,10 @@
     return pl.pallas_call(
         functools.partial(backward_kernel, touch),
         out_shape=jax.ShapeDtypeStruct((rows, slices, pixels), F32),
-        in_specs=[SMEM, VMEM, HBM, VMEM, VMEM],
+        in_specs=[SMEM, HBM, HBM, VMEM, VMEM],
         out_specs=HBM,
         scratch_shapes=[
+            pltpu.VMEM(returned.shape, BF16),
             pltpu.VMEM((touch, slices, prints.shape[2]), F32),
             pltpu.VMEM((slices * touch, prints.shape[2]), BF16),
             pltpu.VMEM((slices // 2, codes, 2 * pixels), BF16),
@@ -451,10 +448,11 @@
             pltpu.VMEM(prints.shape, BF16),
             pltpu.SemaphoreType.DMA((4,)),
             pltpu.SemaphoreType.DMA((2,)),
+            pltpu.SemaphoreType.DMA,
         ],
         compiler_params=pltpu.CompilerParams(vmem_limit_bytes=24 << 20),
         name="backward",
-    )(table, returned, *in_hbm(prints), counts_turned, base)
+    )(table, *in_hbm(returned, prints), counts_turned, base)
 
 
 def shifted(x, axis, forward_way):

time: 77.3 us -> 76.7 us (level)
  no operation moved by 1% of the time
where the time goes in v10:
time: 76.7 us; the launch traced here: 76.2 us
  Pallas kernels  30 us (39%)
  starting transfers between devices  28.5 us (37%)
  waiting for transfers between devices  17.5 us (23%)
    ppermute x4, starting transfers between devices, shifted(): return lax.ppermute(x, axis, pairs)  12.1 us
    pallas_call x1, Pallas kernels, variation(): pl.pallas_call(variation_kernel, out_shape=jax.ShapeDtypeStruct((slices,...  12 us
    all_to_all x1, starting transfers between devices, per_device(): lax.all_to_all(sent, 'tile', split_axis=0, concat_axis=0, tiled=True)  11.2 us
    all_to_all x1, waiting for transfers between devices, per_device(): lax.all_to_all(sent, 'tile', split_axis=0, concat_axis=0, tiled=True)  9.86 us
    pallas_call x1, Pallas kernels, forward(): pl.pallas_call(functools.partial(forward_kernel, touch, owned), out_shape...  8.82 us
    ppermute x4, waiting for transfers between devices, shifted(): return lax.ppermute(x, axis, pairs)  7.62 us
    pallas_call x1, Pallas kernels, backward(): pl.pallas_call(functools.partial(backward_kernel, touch), out_shape=jax.S...  7.23 us
    all_to_all x1, starting transfers between devices, per_device(): lax.all_to_all(answer, 'tile', split_axis=0, concat_axis=0, tiled=True)  5.27 us
  transfers between devices with their start and end apart: 6, of which 4 were waited for; matrix products, arithmetic and copies ran while one was open for 0% of the time, Pallas kernels for 17%

profile of v10, /device:TPU:56, one launch (start us, length us, event | category | flops | bytes accessed | tf_op | source)
XLA Modules:
  0.0 76.2 jit_solution(12599125983177097926)
XLA Ops:
  0.0 0.0 copy-start.3
  0.0 0.0 copy-start
  0.0 0.0 copy-start.2
  0.0 0.0 copy-start.1
  0.0 8.8 %forward.1 = (bf16[32,64,128]{2,1,0:T(8,128)(2,1)}, s32[8,128]{1,0:T(8,128)S(1)}, bf16[512,128]{1,0:T(8,128)(2,1)S(1)}, f32[96,128]{1,0:T(8,128)S(1)}, f32[96,12...) custom-call(s32[64]{0:T(128)} %ray_slot.3, s32[8,3072]{1,0:T(8,128)} %bitcast.2, s32[8,96]{1,0:T(8,128)} %bitcast.4, ...), custom_call_target="tpu_custom_call" | custom-call | tf_op jit(solution)/shard_map/forward/pallas_call | solution.py:168
  8.8 11.2 %all-to-all-start = ((bf16[32,64,128]{2,1,0:T(8,128)(2,1)}), bf16[32,64,128]{2,1,0:T(8,128)(2,1)S(1)}, u32[]{:S(2)}, u32[]{:S(2)}) async-start(bf16[32,64,128]{2,1,0:T(8,128)(2,1)} %get-tuple-element.21), calls=%async_computation | async-start | bytes 1048576 | tf_op jit(solution)/shard_map/all_to_all | solution.py:476
  20.1 1.9 %collective-permute-start = (f32[96,128]{1,0:T(8,128)S(1)}, f32[96,128]{1,0:T(8,128)S(1)}, u32[]{:S(2)}, u32[]{:S(2)}) collective-permute-start(f32[96,128]{1,0:T(8,128)S(1)} %get-tuple-element.23), channel_id=1, source_target_pairs={{0,32},{32,64},{64,96},{96,128},{128,160},{160,192},{192,224},{1,3... | collective-permute-start | bytes 147464 | tf_op jit(solution)/shard_map/ppermute | solution.py:464
  22.0 3.6 %collective-permute-start.1 = (f32[96,128]{1,0:T(8,128)S(1)}, f32[96,128]{1,0:T(8,128)S(1)}, u32[]{:S(2)}, u32[]{:S(2)}) collective-permute-start(f32[96,128]{1,0:T(8,128)S(1)} %get-tuple-element.25), channel_id=1, source_target_pairs={{32,0},{64,32},{96,64},{128,96},{160,128},{192,160},{224,192},{33,... | collective-permute-start | bytes 147464 | tf_op jit(solution)/shard_map/ppermute | solution.py:464
  25.6 0.0 copy-done.3
  25.6 0.0 copy-done
  25.7 1.0 %tables.1 = (bf16[96,512]{1,0:T(8,128)(2,1)S(1)}, f32[32,128]{1,0:T(8,128)S(1)}) custom-call(s32[64]{0:T(128)S(1)} %copy-done.3, s32[8,3072]{1,0:T(8,128)S(1)} %bitcast.3, bf16[512,128]{1,0:T(8,128)(2,1)S(1)} %get-tuple-element.27.counts), custom_call_target="tpu_custom_call" | custom-call | tf_op jit(solution)/shard_map/tables/pallas_call | solution.py:226
  26.6 0.0 collective-permute-done.before_slice
  26.6 0.7 collective-permute-done.1.after_slice
  27.4 9.9 %all-to-all-done.arrived = bf16[32,64,128]{2,1,0:T(8,128)(2,1)S(1)} async-done(((bf16[32,64,128]{2,1,0:T(8,128)(2,1)}), bf16[32,64,128]{2,1,0:T(8,128)(2,1)S(1)}, u32[]{:S(2)}, u32[]{:S(2)}) %all-to-all-start) | async-done | bytes 524320 | tf_op jit(solution)/shard_map/all_to_all | solution.py:476
  37.3 0.0 copy-done.2
  37.3 0.0 copy-done.1
  37.3 1.0 %residual.1 = bf16[32,64,128]{2,1,0:T(8,128)(2,1)} custom-call(bf16[32,64,128]{2,1,0:T(8,128)(2,1)S(1)} %all-to-all-done.arrived, f32[32,128]{1,0:T(8,128)S(1)} %get-tuple-element.28.picks, f32[2,64,128]{2,1,0:T(8,128)S(1)} %copy-done.1, f32[2,64,128]{2,1,0:T(8,128)S(1)} %copy-done.2), custom_call_target="tpu_custom_call" | custom-call | tf_op jit(solution)/shard_map/residual/pallas_call | solution.py:349
  38.3 5.3 %all-to-all-start.1 = ((bf16[32,64,128]{2,1,0:T(8,128)(2,1)}), bf16[32,64,128]{2,1,0:T(8,128)(2,1)}, u32[]{:S(2)}, u32[]{:S(2)}) async-start(bf16[32,64,128]{2,1,0:T(8,128)(2,1)} %residual.1), calls=%async_computation.1 | async-start | bytes 1048576 | tf_op jit(solution)/shard_map/all_to_all | solution.py:487
  43.5 4.6 %collective-permute-start.3 = (f32[65,128]{1,0:T(8,128)S(1)}, f32[65,128]{1,0:T(8,128)S(1)}, u32[]{:S(2)}, u32[]{:S(2)}) collective-permute-start(f32[65,128]{1,0:T(8,128)S(1)} %pad_maximum_fusion), channel_id=1, source_target_pairs={{1,0},{2,1},{3,2},{4,3},{5,4},{6,5},{7,6},{8,7},{9,8},{10,9},{11,1... | collective-permute-start | bytes 99848 | tf_op jit(solution)/shard_map/ppermute | solution.py:464
  48.1 1.9 %collective-permute-start.2 = (f32[65,128]{1,0:T(8,128)S(1)}, f32[65,128]{1,0:T(8,128)S(1)}, u32[]{:S(2)}, u32[]{:S(2)}) collective-permute-start(f32[65,128]{1,0:T(8,128)S(1)} %pad_maximum_fusion.1), channel_id=1, source_target_pairs={{0,1},{1,2},{2,3},{3,4},{4,5},{5,6},{6,7},{7,8},{8,9},{9,10},{10,1... | collective-permute-start | bytes 99848 | tf_op jit(solution)/shard_map/ppermute | solution.py:464
  50.1 4.4 %collective-permute-done.3.after_row = f32[65,128]{1,0:T(8,128)S(1)} collective-permute-done((f32[65,128]{1,0:T(8,128)S(1)}, f32[65,128]{1,0:T(8,128)S(1)}, u32[]{:S(2)}, u32[]{:S(2)}) %collective-permute-start.3) | collective-permute-done | bytes 33312 | tf_op jit(solution)/shard_map/ppermute | solution.py:464
  54.4 2.5 %collective-permute-done.2.before_row = f32[65,128]{1,0:T(8,128)S(1)} collective-permute-done((f32[65,128]{1,0:T(8,128)S(1)}, f32[65,128]{1,0:T(8,128)S(1)}, u32[]{:S(2)}, u32[]{:S(2)}) %collective-permute-start.2) | collective-permute-done | bytes 33312 | tf_op jit(solution)/shard_map/ppermute | solution.py:464
  57.0 12.0 %variation.1.base = f32[64,96,128]{2,1,0:T(8,128)S(1)} custom-call(f32[96,64,128]{2,1,0:T(8,128)} %volume.3, f32[96,128]{1,0:T(8,128)S(1)} %collective-permute-done.before_slice, f32[96,128]{1,0:T(8,128)S(1)} %collective-permute-done.1.after_slice, f32[65,128]{1,0:T(8,128)S(1)} %collective-permute-done.2.before_row, ...), custom_call_target="tpu_custom_call" | custom-call | tf_op jit(solution)/shard_map/variation/pallas_call | solution.py:316
  69.0 0.0 all-to-all-done.1.returned
  69.0 7.2 %backward.1 = f32[96,64,128]{2,1,0:T(8,128)} custom-call(s32[8,128]{1,0:T(8,128)S(1)} %get-tuple-element.20.table, bf16[32,64,128]{2,1,0:T(8,128)(2,1)} %all-to-all-done.1.returned, bf16[32,128,128]{2,1,0:T(8,128)(2,1)} %prints.3, bf16[96,512]{1,0:T(8,128)(2,1)S(1)} %get-tuple-element.29.counts_turned, f32[64,96,128]{2,1,0:T(8,128)S(1)} %variation.1.base), custom_call_target="tpu_custom_call" | custom-call | tf_op jit(solution)/shard_map/backward/pallas_call | solution.py:437
  (4 shorter events, 0.0 us)
Async XLA Ops:
  0.0 25.6 %copy-start.3 = (s32[64]{0:T(128)S(1)}, s32[64]{0:T(128)}, u32[]{:S(2)}) copy-start(s32[64]{0:T(128)} %ray_slot.3) | copy-start | bytes 772
  0.0 25.6 %copy-start = (s32[3072,8]{0,1:T(8,128)S(1)}, s32[3072,8]{0,1:T(8,128)}, u32[]{:S(2)}) copy-start(s32[3072,8]{0,1:T(8,128)} %param.10) | copy-start | bytes 294916
  0.0 37.3 %copy-start.2 = (f32[2,64,128]{2,1,0:T(8,128)S(1)}, f32[2,64,128]{2,1,0:T(8,128)}, u32[]{:S(2)}) copy-start(f32[2,64,128]{2,1,0:T(8,128)} %weights.1) | copy-start | bytes 196612
  0.0 37.3 %copy-start.1 = (f32[2,64,128]{2,1,0:T(8,128)S(1)}, f32[2,64,128]{2,1,0:T(8,128)}, u32[]{:S(2)}) copy-start(f32[2,64,128]{2,1,0:T(8,128)} %measured.1) | copy-start | bytes 196612
  8.8 28.4 %all-to-all-start = ((bf16[32,64,128]{2,1,0:T(8,128)(2,1)}), bf16[32,64,128]{2,1,0:T(8,128)(2,1)S(1)}, u32[]{:S(2)}, u32[]{:S(2)}) async-start(bf16[32,64,128]{2,1,0:T(8,128)(2,1)} %get-tuple-element.21), calls=%async_computation | async-start | bytes 1048576 | tf_op jit(solution)/shard_map/all_to_all | solution.py:476
  20.1 6.6 %collective-permute-start = (f32[96,128]{1,0:T(8,128)S(1)}, f32[96,128]{1,0:T(8,128)S(1)}, u32[]{:S(2)}, u32[]{:S(2)}) collective-permute-start(f32[96,128]{1,0:T(8,128)S(1)} %get-tuple-element.23), channel_id=1, source_target_pairs={{0,32},{32,64},{64,96},{96,128},{128,160},{160,192},{192,224},{1,3... | collective-permute-start | bytes 147464 | tf_op jit(solution)/shard_map/ppermute | solution.py:464
  22.0 5.4 %collective-permute-start.1 = (f32[96,128]{1,0:T(8,128)S(1)}, f32[96,128]{1,0:T(8,128)S(1)}, u32[]{:S(2)}, u32[]{:S(2)}) collective-permute-start(f32[96,128]{1,0:T(8,128)S(1)} %get-tuple-element.25), channel_id=1, source_target_pairs={{32,0},{64,32},{96,64},{128,96},{160,128},{192,160},{224,192},{33,... | collective-permute-start | bytes 147464 | tf_op jit(solution)/shard_map/ppermute | solution.py:464
  38.3 30.7 %all-to-all-start.1 = ((bf16[32,64,128]{2,1,0:T(8,128)(2,1)}), bf16[32,64,128]{2,1,0:T(8,128)(2,1)}, u32[]{:S(2)}, u32[]{:S(2)}) async-start(bf16[32,64,128]{2,1,0:T(8,128)(2,1)} %residual.1), calls=%async_computation.1 | async-start | bytes 1048576 | tf_op jit(solution)/shard_map/all_to_all | solution.py:487
  43.5 10.9 %collective-permute-start.3 = (f32[65,128]{1,0:T(8,128)S(1)}, f32[65,128]{1,0:T(8,128)S(1)}, u32[]{:S(2)}, u32[]{:S(2)}) collective-permute-start(f32[65,128]{1,0:T(8,128)S(1)} %pad_maximum_fusion), channel_id=1, source_target_pairs={{1,0},{2,1},{3,2},{4,3},{5,4},{6,5},{7,6},{8,7},{9,8},{10,9},{11,1... | collective-permute-start | bytes 99848 | tf_op jit(solution)/shard_map/ppermute | solution.py:464
  48.1 8.8 %collective-permute-start.2 = (f32[65,128]{1,0:T(8,128)S(1)}, f32[65,128]{1,0:T(8,128)S(1)}, u32[]{:S(2)}, u32[]{:S(2)}) collective-permute-start(f32[65,128]{1,0:T(8,128)S(1)} %pad_maximum_fusion.1), channel_id=1, source_target_pairs={{0,1},{1,2},{2,3},{3,4},{4,5},{5,6},{6,7},{7,8},{8,9},{9,10},{10,1... | collective-permute-start | bytes 99848 | tf_op jit(solution)/shard_map/ppermute | solution.py:464

commit v11 on v10

--- a/solution.py
+++ b/solution.py
@@ -114,7 +114,7 @@
             terms = [x + y for x, y in zip(terms[::2], terms[1::2])]
         counts[f * touch : (f + 1) * touch] = terms[0]
 
-    wide = 16
+    wide = 32
 
     @pl.loop(0, groups)
     def _(i):
@@ -152,14 +152,14 @@
         sums[m : m + block] = both[:, :rays]
         sums[half * touch + m : half * touch + m + block] = both[:, rays:]
 
-    compact[...] = jnp.swapaxes(sums[...].reshape(slice_count, touch, -1), 0, 1).astype(BF16)
+    compact[touch] = jnp.zeros(compact.shape[1:], BF16)
+    compact[:touch] = jnp.swapaxes(sums[...].reshape(slice_count, touch, -1), 0, 1).astype(BF16)
     for copy in small[3:]:
         copy.wait()
     table_copy.wait()
     for t in range(owners):
         place = table[0, t]
-        block = compact[jnp.maximum(place, 0)]
-        sent[t] = jnp.where(place >= 0, block, jnp.zeros_like(block))
+        sent[t] = compact[jnp.where(place >= 0, place, touch)]
 
 
 def forward(touch, owned, owners, ray_slot, blocks, foots, volume, prints):
@@ -186,7 +186,7 @@
             pltpu.VMEM(prints.shape, BF16),
             pltpu.VMEM((foot_count, slices // 2 * touch, 2 * pixels), BF16),
             pltpu.VMEM((slices * touch, rays), F32),
-            pltpu.VMEM((touch, slices, rays), BF16),
+            pltpu.VMEM((touch + 1, slices, rays), BF16),
             pltpu.VMEM((8, lanes), jnp.int32),
             pltpu.SemaphoreType.DMA((4,)),
             pltpu.SemaphoreType.DMA((5,)),
@@ -446,7 +446,7 @@
             pltpu.VMEM((slices // 2, codes, 2 * pixels), BF16),
             pltpu.VMEM((slices, rows, pixels), F32),
             pltpu.VMEM(prints.shape, BF16),
-            pltpu.SemaphoreType.DMA((4,)),
+            pltpu.SemaphoreType.DMA((2,)),
             pltpu.SemaphoreType.DMA((2,)),
             pltpu.SemaphoreType.DMA,
         ],

time: 76.7 us -> 76.7 us (level)
  the two profiles are of different devices: /device:TPU:56 before, /device:TPU:32 now
where the time goes in v11:
time: 76.7 us; the launch traced here: 76.2 us
  Pallas kernels  30 us (39%)
  starting transfers between devices  25.6 us (33%)
  waiting for transfers between devices  20.5 us (27%)
    pallas_call x1, Pallas kernels, variation(): pl.pallas_call(variation_kernel, out_shape=jax.ShapeDtypeStruct((slices,...  12 us
    all_to_all x1, starting transfers between devices, per_device(): lax.all_to_all(sent, 'tile', split_axis=0, concat_axis=0, tiled=True)  11.2 us
    all_to_all x1, waiting for transfers between devices, per_device(): lax.all_to_all(sent, 'tile', split_axis=0, concat_axis=0, tiled=True)  10.9 us
    ppermute x4, waiting for transfers between devices, shifted(): return lax.ppermute(x, axis, pairs)  9.53 us
    pallas_call x1, Pallas kernels, forward(): pl.pallas_call(functools.partial(forward_kernel, touch, owned), out_shape...  9.15 us
    ppermute x4, starting transfers between devices, shifted(): return lax.ppermute(x, axis, pairs)  9.09 us
    pallas_call x1, Pallas kernels, backward(): pl.pallas_call(functools.partial(backward_kernel, touch), out_shape=jax.S...  6.93 us
    all_to_all x1, starting transfers between devices, per_device(): lax.all_to_all(answer, 'tile', split_axis=0, concat_axis=0, tiled=True)  5.27 us
  transfers between devices with their start and end apart: 6, of which 4 were waited for; matrix products, arithmetic and copies ran while one was open for 0% of the time, Pallas kernels for 17%

profile of v11, /device:TPU:32, one launch (start us, length us, event | category | flops | bytes accessed | tf_op | source)
XLA Modules:
  0.0 76.2 jit_solution(8157903480916581972)
XLA Ops:
  0.0 0.0 copy-start.3
  0.0 0.0 copy-start
  0.0 0.0 copy-start.2
  0.0 0.0 copy-start.1
  0.0 9.2 %forward.1 = (bf16[32,64,128]{2,1,0:T(8,128)(2,1)}, s32[8,128]{1,0:T(8,128)S(1)}, bf16[512,128]{1,0:T(8,128)(2,1)S(1)}, f32[96,128]{1,0:T(8,128)S(1)}, f32[96,12...) custom-call(s32[64]{0:T(128)} %ray_slot.3, s32[8,3072]{1,0:T(8,128)} %bitcast.2, s32[8,96]{1,0:T(8,128)} %bitcast.4, ...), custom_call_target="tpu_custom_call" | custom-call | tf_op jit(solution)/shard_map/forward/pallas_call | solution.py:168
  9.2 11.2 %all-to-all-start = ((bf16[32,64,128]{2,1,0:T(8,128)(2,1)}), bf16[32,64,128]{2,1,0:T(8,128)(2,1)S(1)}, u32[]{:S(2)}, u32[]{:S(2)}) async-start(bf16[32,64,128]{2,1,0:T(8,128)(2,1)} %get-tuple-element.21), calls=%async_computation | async-start | bytes 1048576 | tf_op jit(solution)/shard_map/all_to_all | solution.py:476
  20.4 1.3 %collective-permute-start = (f32[96,128]{1,0:T(8,128)S(1)}, f32[96,128]{1,0:T(8,128)S(1)}, u32[]{:S(2)}, u32[]{:S(2)}) collective-permute-start(f32[96,128]{1,0:T(8,128)S(1)} %get-tuple-element.23), channel_id=1, source_target_pairs={{0,32},{32,64},{64,96},{96,128},{128,160},{160,192},{192,224},{1,3... | collective-permute-start | bytes 147464 | tf_op jit(solution)/shard_map/ppermute | solution.py:464
  21.7 1.3 %collective-permute-start.1 = (f32[96,128]{1,0:T(8,128)S(1)}, f32[96,128]{1,0:T(8,128)S(1)}, u32[]{:S(2)}, u32[]{:S(2)}) collective-permute-start(f32[96,128]{1,0:T(8,128)S(1)} %get-tuple-element.25), channel_id=1, source_target_pairs={{32,0},{64,32},{96,64},{128,96},{160,128},{192,160},{224,192},{33,... | collective-permute-start | bytes 147464 | tf_op jit(solution)/shard_map/ppermute | solution.py:464
  23.0 0.0 copy-done.3
  23.0 0.0 copy-done
  23.0 1.0 %tables.1 = (bf16[96,512]{1,0:T(8,128)(2,1)S(1)}, f32[32,128]{1,0:T(8,128)S(1)}) custom-call(s32[64]{0:T(128)S(1)} %copy-done.3, s32[8,3072]{1,0:T(8,128)S(1)} %bitcast.3, bf16[512,128]{1,0:T(8,128)(2,1)S(1)} %get-tuple-element.27.counts), custom_call_target="tpu_custom_call" | custom-call | tf_op jit(solution)/shard_map/tables/pallas_call | solution.py:226
  24.0 0.0 collective-permute-done.before_slice
  24.0 2.6 %collective-permute-done.1.after_slice = f32[96,128]{1,0:T(8,128)S(1)} collective-permute-done((f32[96,128]{1,0:T(8,128)S(1)}, f32[96,128]{1,0:T(8,128)S(1)}, u32[]{:S(2)}, u32[]{:S(2)}) %collective-permute-start.1) | collective-permute-done | bytes 49184 | tf_op jit(solution)/shard_map/ppermute | solution.py:464
  26.7 10.9 %all-to-all-done.arrived = bf16[32,64,128]{2,1,0:T(8,128)(2,1)S(1)} async-done(((bf16[32,64,128]{2,1,0:T(8,128)(2,1)}), bf16[32,64,128]{2,1,0:T(8,128)(2,1)S(1)}, u32[]{:S(2)}, u32[]{:S(2)}) %all-to-all-start) | async-done | bytes 524320 | tf_op jit(solution)/shard_map/all_to_all | solution.py:476
  37.6 0.0 copy-done.2
  37.6 0.0 copy-done.1
  37.6 1.0 %residual.1 = bf16[32,64,128]{2,1,0:T(8,128)(2,1)} custom-call(bf16[32,64,128]{2,1,0:T(8,128)(2,1)S(1)} %all-to-all-done.arrived, f32[32,128]{1,0:T(8,128)S(1)} %get-tuple-element.28.picks, f32[2,64,128]{2,1,0:T(8,128)S(1)} %copy-done.1, f32[2,64,128]{2,1,0:T(8,128)S(1)} %copy-done.2), custom_call_target="tpu_custom_call" | custom-call | tf_op jit(solution)/shard_map/residual/pallas_call | solution.py:349
  38.6 5.3 %all-to-all-start.1 = ((bf16[32,64,128]{2,1,0:T(8,128)(2,1)}), bf16[32,64,128]{2,1,0:T(8,128)(2,1)}, u32[]{:S(2)}, u32[]{:S(2)}) async-start(bf16[32,64,128]{2,1,0:T(8,128)(2,1)} %residual.1), calls=%async_computation.1 | async-start | bytes 1048576 | tf_op jit(solution)/shard_map/all_to_all | solution.py:487
  43.9 4.6 %collective-permute-start.3 = (f32[65,128]{1,0:T(8,128)S(1)}, f32[65,128]{1,0:T(8,128)S(1)}, u32[]{:S(2)}, u32[]{:S(2)}) collective-permute-start(f32[65,128]{1,0:T(8,128)S(1)} %pad_maximum_fusion), channel_id=1, source_target_pairs={{1,0},{2,1},{3,2},{4,3},{5,4},{6,5},{7,6},{8,7},{9,8},{10,9},{11,1... | collective-permute-start | bytes 99848 | tf_op jit(solution)/shard_map/ppermute | solution.py:464
  48.5 1.9 %collective-permute-start.2 = (f32[65,128]{1,0:T(8,128)S(1)}, f32[65,128]{1,0:T(8,128)S(1)}, u32[]{:S(2)}, u32[]{:S(2)}) collective-permute-start(f32[65,128]{1,0:T(8,128)S(1)} %pad_maximum_fusion.1), channel_id=1, source_target_pairs={{0,1},{1,2},{2,3},{3,4},{4,5},{5,6},{6,7},{7,8},{8,9},{9,10},{10,1... | collective-permute-start | bytes 99848 | tf_op jit(solution)/shard_map/ppermute | solution.py:464
  50.4 4.4 %collective-permute-done.3.after_row = f32[65,128]{1,0:T(8,128)S(1)} collective-permute-done((f32[65,128]{1,0:T(8,128)S(1)}, f32[65,128]{1,0:T(8,128)S(1)}, u32[]{:S(2)}, u32[]{:S(2)}) %collective-permute-start.3) | collective-permute-done | bytes 33312 | tf_op jit(solution)/shard_map/ppermute | solution.py:464
  54.7 2.5 %collective-permute-done.2.before_row = f32[65,128]{1,0:T(8,128)S(1)} collective-permute-done((f32[65,128]{1,0:T(8,128)S(1)}, f32[65,128]{1,0:T(8,128)S(1)}, u32[]{:S(2)}, u32[]{:S(2)}) %collective-permute-start.2) | collective-permute-done | bytes 33312 | tf_op jit(solution)/shard_map/ppermute | solution.py:464
  57.3 12.0 %variation.1.base = f32[64,96,128]{2,1,0:T(8,128)S(1)} custom-call(f32[96,64,128]{2,1,0:T(8,128)} %volume.3, f32[96,128]{1,0:T(8,128)S(1)} %collective-permute-done.before_slice, f32[96,128]{1,0:T(8,128)S(1)} %collective-permute-done.1.after_slice, f32[65,128]{1,0:T(8,128)S(1)} %collective-permute-done.2.before_row, ...), custom_call_target="tpu_custom_call" | custom-call | tf_op jit(solution)/shard_map/variation/pallas_call | solution.py:316
  69.3 0.0 all-to-all-done.1.returned
  69.3 6.9 %backward.1 = f32[96,64,128]{2,1,0:T(8,128)} custom-call(s32[8,128]{1,0:T(8,128)S(1)} %get-tuple-element.20.table, bf16[32,64,128]{2,1,0:T(8,128)(2,1)} %all-to-all-done.1.returned, bf16[32,128,128]{2,1,0:T(8,128)(2,1)} %prints.3, bf16[96,512]{1,0:T(8,128)(2,1)S(1)} %get-tuple-element.29.counts_turned, f32[64,96,128]{2,1,0:T(8,128)S(1)} %variation.1.base), custom_call_target="tpu_custom_call" | custom-call | tf_op jit(solution)/shard_map/backward/pallas_call | solution.py:437
  (4 shorter events, 0.0 us)
Async XLA Ops:
  0.0 23.0 %copy-start.3 = (s32[64]{0:T(128)S(1)}, s32[64]{0:T(128)}, u32[]{:S(2)}) copy-start(s32[64]{0:T(128)} %ray_slot.3) | copy-start | bytes 772
  0.0 23.0 %copy-start = (s32[3072,8]{0,1:T(8,128)S(1)}, s32[3072,8]{0,1:T(8,128)}, u32[]{:S(2)}) copy-start(s32[3072,8]{0,1:T(8,128)} %param.10) | copy-start | bytes 294916
  0.0 37.6 %copy-start.2 = (f32[2,64,128]{2,1,0:T(8,128)S(1)}, f32[2,64,128]{2,1,0:T(8,128)}, u32[]{:S(2)}) copy-start(f32[2,64,128]{2,1,0:T(8,128)} %weights.1) | copy-start | bytes 196612
  0.0 37.6 %copy-start.1 = (f32[2,64,128]{2,1,0:T(8,128)S(1)}, f32[2,64,128]{2,1,0:T(8,128)}, u32[]{:S(2)}) copy-start(f32[2,64,128]{2,1,0:T(8,128)} %measured.1) | copy-start | bytes 196612
  9.2 28.4 %all-to-all-start = ((bf16[32,64,128]{2,1,0:T(8,128)(2,1)}), bf16[32,64,128]{2,1,0:T(8,128)(2,1)S(1)}, u32[]{:S(2)}, u32[]{:S(2)}) async-start(bf16[32,64,128]{2,1,0:T(8,128)(2,1)} %get-tuple-element.21), calls=%async_computation | async-start | bytes 1048576 | tf_op jit(solution)/shard_map/all_to_all | solution.py:476
  20.4 3.6 %collective-permute-start = (f32[96,128]{1,0:T(8,128)S(1)}, f32[96,128]{1,0:T(8,128)S(1)}, u32[]{:S(2)}, u32[]{:S(2)}) collective-permute-start(f32[96,128]{1,0:T(8,128)S(1)} %get-tuple-element.23), channel_id=1, source_target_pairs={{0,32},{32,64},{64,96},{96,128},{128,160},{160,192},{192,224},{1,3... | collective-permute-start | bytes 147464 | tf_op jit(solution)/shard_map/ppermute | solution.py:464
  21.7 4.9 %collective-permute-start.1 = (f32[96,128]{1,0:T(8,128)S(1)}, f32[96,128]{1,0:T(8,128)S(1)}, u32[]{:S(2)}, u32[]{:S(2)}) collective-permute-start(f32[96,128]{1,0:T(8,128)S(1)} %get-tuple-element.25), channel_id=1, source_target_pairs={{32,0},{64,32},{96,64},{128,96},{160,128},{192,160},{224,192},{33,... | collective-permute-start | bytes 147464 | tf_op jit(solution)/shard_map/ppermute | solution.py:464
  38.6 30.7 %all-to-all-start.1 = ((bf16[32,64,128]{2,1,0:T(8,128)(2,1)}), bf16[32,64,128]{2,1,0:T(8,128)(2,1)}, u32[]{:S(2)}, u32[]{:S(2)}) async-start(bf16[32,64,128]{2,1,0:T(8,128)(2,1)} %residual.1), calls=%async_computation.1 | async-start | bytes 1048576 | tf_op jit(solution)/shard_map/all_to_all | solution.py:487
  43.9 10.9 %collective-permute-start.3 = (f32[65,128]{1,0:T(8,128)S(1)}, f32[65,128]{1,0:T(8,128)S(1)}, u32[]{:S(2)}, u32[]{:S(2)}) collective-permute-start(f32[65,128]{1,0:T(8,128)S(1)} %pad_maximum_fusion), channel_id=1, source_target_pairs={{1,0},{2,1},{3,2},{4,3},{5,4},{6,5},{7,6},{8,7},{9,8},{10,9},{11,1... | collective-permute-start | bytes 99848 | tf_op jit(solution)/shard_map/ppermute | solution.py:464
  48.5 8.8 %collective-permute-start.2 = (f32[65,128]{1,0:T(8,128)S(1)}, f32[65,128]{1,0:T(8,128)S(1)}, u32[]{:S(2)}, u32[]{:S(2)}) collective-permute-start(f32[65,128]{1,0:T(8,128)S(1)} %pad_maximum_fusion.1), channel_id=1, source_target_pairs={{0,1},{1,2},{2,3},{3,4},{4,5},{5,6},{6,7},{7,8},{8,9},{9,10},{10,1... | collective-permute-start | bytes 99848 | tf_op jit(solution)/shard_map/ppermute | solution.py:464

commit v12 on v11

--- a/solution.py
+++ b/solution.py
@@ -114,7 +114,7 @@
             terms = [x + y for x, y in zip(terms[::2], terms[1::2])]
         counts[f * touch : (f + 1) * touch] = terms[0]
 
-    wide = 32
+    wide = 16
 
     @pl.loop(0, groups)
     def _(i):
@@ -334,8 +334,9 @@
     for j in range(owners):
         part = arrived[j].astype(F32)
         chosen = picks[j : j + 1, :] > 0.5
-        sums[0] = sums[0] + jnp.where(chosen, 0.0, part)
+        sums[0] = sums[0] + part
         sums[1] = sums[1] + jnp.where(chosen, part, 0.0)
+    sums[0] = sums[0] - sums[1]
     out = [(weights[i] * (sums[i] - measured[i])).astype(BF16).astype(F32) for i in range(2)]
     for j in range(owners):
         answer[j] = jnp.where(picks[j : j + 1, :] > 0.5, out[1], out[0]).astype(BF16)

time: 76.7 us -> 76.2 us (level)
  the two profiles are of different devices: /device:TPU:32 before, /device:TPU:56 now
where the time goes in v12:
time: 76.2 us; the launch traced here: 75.8 us
  Pallas kernels  29.6 us (39%)
  starting transfers between devices  28.5 us (37%)
  waiting for transfers between devices  17.5 us (23%)
    ppermute x4, starting transfers between devices, shifted(): return lax.ppermute(x, axis, pairs)  12.1 us
    pallas_call x1, Pallas kernels, variation(): pl.pallas_call(variation_kernel, out_shape=jax.ShapeDtypeStruct((slices,...  12 us
    all_to_all x1, starting transfers between devices, per_device(): lax.all_to_all(sent, 'tile', split_axis=0, concat_axis=0, tiled=True)  11.2 us
    all_to_all x1, waiting for transfers between devices, per_device(): lax.all_to_all(sent, 'tile', split_axis=0, concat_axis=0, tiled=True)  9.86 us
    pallas_call x1, Pallas kernels, forward(): pl.pallas_call(functools.partial(forward_kernel, touch, owned), out_shape...  8.71 us
    ppermute x4, waiting for transfers between devices, shifted(): return lax.ppermute(x, axis, pairs)  7.62 us
    pallas_call x1, Pallas kernels, backward(): pl.pallas_call(functools.partial(backward_kernel, touch), out_shape=jax.S...  6.94 us
    all_to_all x1, starting transfers between devices, per_device(): lax.all_to_all(answer, 'tile', split_axis=0, concat_axis=0, tiled=True)  5.27 us
  transfers between devices with their start and end apart: 6, of which 4 were waited for; matrix products, arithmetic and copies ran while one was open for 0% of the time, Pallas kernels for 17%

profile of v12, /device:TPU:56, one launch (start us, length us, event | category | flops | bytes accessed | tf_op | source)
XLA Modules:
  0.0 75.8 jit_solution(13621242766012450749)
XLA Ops:
  0.0 0.0 copy-start.3
  0.0 0.0 copy-start
  0.0 0.0 copy-start.2
  0.0 0.0 copy-start.1
  0.0 8.7 %forward.1 = (bf16[32,64,128]{2,1,0:T(8,128)(2,1)}, s32[8,128]{1,0:T(8,128)S(1)}, bf16[512,128]{1,0:T(8,128)(2,1)S(1)}, f32[96,128]{1,0:T(8,128)S(1)}, f32[96,12...) custom-call(s32[64]{0:T(128)} %ray_slot.3, s32[8,3072]{1,0:T(8,128)} %bitcast.2, s32[8,96]{1,0:T(8,128)} %bitcast.4, ...), custom_call_target="tpu_custom_call" | custom-call | tf_op jit(solution)/shard_map/forward/pallas_call | solution.py:168
  8.7 11.2 %all-to-all-start = ((bf16[32,64,128]{2,1,0:T(8,128)(2,1)}), bf16[32,64,128]{2,1,0:T(8,128)(2,1)S(1)}, u32[]{:S(2)}, u32[]{:S(2)}) async-start(bf16[32,64,128]{2,1,0:T(8,128)(2,1)} %get-tuple-element.21), calls=%async_computation | async-start | bytes 1048576 | tf_op jit(solution)/shard_map/all_to_all | solution.py:477
  19.9 1.9 %collective-permute-start = (f32[96,128]{1,0:T(8,128)S(1)}, f32[96,128]{1,0:T(8,128)S(1)}, u32[]{:S(2)}, u32[]{:S(2)}) collective-permute-start(f32[96,128]{1,0:T(8,128)S(1)} %get-tuple-element.23), channel_id=1, source_target_pairs={{0,32},{32,64},{64,96},{96,128},{128,160},{160,192},{192,224},{1,3... | collective-permute-start | bytes 147464 | tf_op jit(solution)/shard_map/ppermute | solution.py:465
  21.9 3.6 %collective-permute-start.1 = (f32[96,128]{1,0:T(8,128)S(1)}, f32[96,128]{1,0:T(8,128)S(1)}, u32[]{:S(2)}, u32[]{:S(2)}) collective-permute-start(f32[96,128]{1,0:T(8,128)S(1)} %get-tuple-element.25), channel_id=1, source_target_pairs={{32,0},{64,32},{96,64},{128,96},{160,128},{192,160},{224,192},{33,... | collective-permute-start | bytes 147464 | tf_op jit(solution)/shard_map/ppermute | solution.py:465
  25.5 0.0 copy-done.3
  25.5 0.0 copy-done
  25.5 1.0 %tables.1 = (bf16[96,512]{1,0:T(8,128)(2,1)S(1)}, f32[32,128]{1,0:T(8,128)S(1)}) custom-call(s32[64]{0:T(128)S(1)} %copy-done.3, s32[8,3072]{1,0:T(8,128)S(1)} %bitcast.3, bf16[512,128]{1,0:T(8,128)(2,1)S(1)} %get-tuple-element.27.counts), custom_call_target="tpu_custom_call" | custom-call | tf_op jit(solution)/shard_map/tables/pallas_call | solution.py:226
  26.5 0.0 collective-permute-done.before_slice
  26.5 0.7 collective-permute-done.1.after_slice
  27.3 9.9 %all-to-all-done.arrived = bf16[32,64,128]{2,1,0:T(8,128)(2,1)S(1)} async-done(((bf16[32,64,128]{2,1,0:T(8,128)(2,1)}), bf16[32,64,128]{2,1,0:T(8,128)(2,1)S(1)}, u32[]{:S(2)}, u32[]{:S(2)}) %all-to-all-start) | async-done | bytes 524320 | tf_op jit(solution)/shard_map/all_to_all | solution.py:477
  37.1 0.0 copy-done.2
  37.2 0.0 copy-done.1
  37.2 1.0 %residual.1 = bf16[32,64,128]{2,1,0:T(8,128)(2,1)} custom-call(bf16[32,64,128]{2,1,0:T(8,128)(2,1)S(1)} %all-to-all-done.arrived, f32[32,128]{1,0:T(8,128)S(1)} %get-tuple-element.28.picks, f32[2,64,128]{2,1,0:T(8,128)S(1)} %copy-done.1, f32[2,64,128]{2,1,0:T(8,128)S(1)} %copy-done.2), custom_call_target="tpu_custom_call" | custom-call | tf_op jit(solution)/shard_map/residual/pallas_call | solution.py:350
  38.1 5.3 %all-to-all-start.1 = ((bf16[32,64,128]{2,1,0:T(8,128)(2,1)}), bf16[32,64,128]{2,1,0:T(8,128)(2,1)}, u32[]{:S(2)}, u32[]{:S(2)}) async-start(bf16[32,64,128]{2,1,0:T(8,128)(2,1)} %residual.1), calls=%async_computation.1 | async-start | bytes 1048576 | tf_op jit(solution)/shard_map/all_to_all | solution.py:488
  43.4 4.6 %collective-permute-start.3 = (f32[65,128]{1,0:T(8,128)S(1)}, f32[65,128]{1,0:T(8,128)S(1)}, u32[]{:S(2)}, u32[]{:S(2)}) collective-permute-start(f32[65,128]{1,0:T(8,128)S(1)} %pad_maximum_fusion), channel_id=1, source_target_pairs={{1,0},{2,1},{3,2},{4,3},{5,4},{6,5},{7,6},{8,7},{9,8},{10,9},{11,1... | collective-permute-start | bytes 99848 | tf_op jit(solution)/shard_map/ppermute | solution.py:465
  48.0 1.9 %collective-permute-start.2 = (f32[65,128]{1,0:T(8,128)S(1)}, f32[65,128]{1,0:T(8,128)S(1)}, u32[]{:S(2)}, u32[]{:S(2)}) collective-permute-start(f32[65,128]{1,0:T(8,128)S(1)} %pad_maximum_fusion.1), channel_id=1, source_target_pairs={{0,1},{1,2},{2,3},{3,4},{4,5},{5,6},{6,7},{7,8},{8,9},{9,10},{10,1... | collective-permute-start | bytes 99848 | tf_op jit(solution)/shard_map/ppermute | solution.py:465
  49.9 4.4 %collective-permute-done.3.after_row = f32[65,128]{1,0:T(8,128)S(1)} collective-permute-done((f32[65,128]{1,0:T(8,128)S(1)}, f32[65,128]{1,0:T(8,128)S(1)}, u32[]{:S(2)}, u32[]{:S(2)}) %collective-permute-start.3) | collective-permute-done | bytes 33312 | tf_op jit(solution)/shard_map/ppermute | solution.py:465
  54.3 2.5 %collective-permute-done.2.before_row = f32[65,128]{1,0:T(8,128)S(1)} collective-permute-done((f32[65,128]{1,0:T(8,128)S(1)}, f32[65,128]{1,0:T(8,128)S(1)}, u32[]{:S(2)}, u32[]{:S(2)}) %collective-permute-start.2) | collective-permute-done | bytes 33312 | tf_op jit(solution)/shard_map/ppermute | solution.py:465
  56.8 12.0 %variation.1.base = f32[64,96,128]{2,1,0:T(8,128)S(1)} custom-call(f32[96,64,128]{2,1,0:T(8,128)} %volume.3, f32[96,128]{1,0:T(8,128)S(1)} %collective-permute-done.before_slice, f32[96,128]{1,0:T(8,128)S(1)} %collective-permute-done.1.after_slice, f32[65,128]{1,0:T(8,128)S(1)} %collective-permute-done.2.before_row, ...), custom_call_target="tpu_custom_call" | custom-call | tf_op jit(solution)/shard_map/variation/pallas_call | solution.py:316
  68.8 0.0 all-to-all-done.1.returned
  68.8 6.9 %backward.1 = f32[96,64,128]{2,1,0:T(8,128)} custom-call(s32[8,128]{1,0:T(8,128)S(1)} %get-tuple-element.20.table, bf16[32,64,128]{2,1,0:T(8,128)(2,1)} %all-to-all-done.1.returned, bf16[32,128,128]{2,1,0:T(8,128)(2,1)} %prints.3, bf16[96,512]{1,0:T(8,128)(2,1)S(1)} %get-tuple-element.29.counts_turned, f32[64,96,128]{2,1,0:T(8,128)S(1)} %variation.1.base), custom_call_target="tpu_custom_call" | custom-call | tf_op jit(solution)/shard_map/backward/pallas_call | solution.py:438
  (4 shorter events, 0.0 us)
Async XLA Ops:
  0.0 25.5 %copy-start.3 = (s32[64]{0:T(128)S(1)}, s32[64]{0:T(128)}, u32[]{:S(2)}) copy-start(s32[64]{0:T(128)} %ray_slot.3) | copy-start | bytes 772
  0.0 25.5 %copy-start = (s32[3072,8]{0,1:T(8,128)S(1)}, s32[3072,8]{0,1:T(8,128)}, u32[]{:S(2)}) copy-start(s32[3072,8]{0,1:T(8,128)} %param.10) | copy-start | bytes 294916
  0.0 37.1 %copy-start.2 = (f32[2,64,128]{2,1,0:T(8,128)S(1)}, f32[2,64,128]{2,1,0:T(8,128)}, u32[]{:S(2)}) copy-start(f32[2,64,128]{2,1,0:T(8,128)} %weights.1) | copy-start | bytes 196612
  0.0 37.1 %copy-start.1 = (f32[2,64,128]{2,1,0:T(8,128)S(1)}, f32[2,64,128]{2,1,0:T(8,128)}, u32[]{:S(2)}) copy-start(f32[2,64,128]{2,1,0:T(8,128)} %measured.1) | copy-start | bytes 196612
  8.7 28.4 %all-to-all-start = ((bf16[32,64,128]{2,1,0:T(8,128)(2,1)}), bf16[32,64,128]{2,1,0:T(8,128)(2,1)S(1)}, u32[]{:S(2)}, u32[]{:S(2)}) async-start(bf16[32,64,128]{2,1,0:T(8,128)(2,1)} %get-tuple-element.21), calls=%async_computation | async-start | bytes 1048576 | tf_op jit(solution)/shard_map/all_to_all | solution.py:477
  19.9 6.6 %collective-permute-start = (f32[96,128]{1,0:T(8,128)S(1)}, f32[96,128]{1,0:T(8,128)S(1)}, u32[]{:S(2)}, u32[]{:S(2)}) collective-permute-start(f32[96,128]{1,0:T(8,128)S(1)} %get-tuple-element.23), channel_id=1, source_target_pairs={{0,32},{32,64},{64,96},{96,128},{128,160},{160,192},{192,224},{1,3... | collective-permute-start | bytes 147464 | tf_op jit(solution)/shard_map/ppermute | solution.py:465
  21.9 5.4 %collective-permute-start.1 = (f32[96,128]{1,0:T(8,128)S(1)}, f32[96,128]{1,0:T(8,128)S(1)}, u32[]{:S(2)}, u32[]{:S(2)}) collective-permute-start(f32[96,128]{1,0:T(8,128)S(1)} %get-tuple-element.25), channel_id=1, source_target_pairs={{32,0},{64,32},{96,64},{128,96},{160,128},{192,160},{224,192},{33,... | collective-permute-start | bytes 147464 | tf_op jit(solution)/shard_map/ppermute | solution.py:465
  38.1 30.7 %all-to-all-start.1 = ((bf16[32,64,128]{2,1,0:T(8,128)(2,1)}), bf16[32,64,128]{2,1,0:T(8,128)(2,1)}, u32[]{:S(2)}, u32[]{:S(2)}) async-start(bf16[32,64,128]{2,1,0:T(8,128)(2,1)} %residual.1), calls=%async_computation.1 | async-start | bytes 1048576 | tf_op jit(solution)/shard_map/all_to_all | solution.py:488
  43.4 10.9 %collective-permute-start.3 = (f32[65,128]{1,0:T(8,128)S(1)}, f32[65,128]{1,0:T(8,128)S(1)}, u32[]{:S(2)}, u32[]{:S(2)}) collective-permute-start(f32[65,128]{1,0:T(8,128)S(1)} %pad_maximum_fusion), channel_id=1, source_target_pairs={{1,0},{2,1},{3,2},{4,3},{5,4},{6,5},{7,6},{8,7},{9,8},{10,9},{11,1... | collective-permute-start | bytes 99848 | tf_op jit(solution)/shard_map/ppermute | solution.py:465
  48.0 8.8 %collective-permute-start.2 = (f32[65,128]{1,0:T(8,128)S(1)}, f32[65,128]{1,0:T(8,128)S(1)}, u32[]{:S(2)}, u32[]{:S(2)}) collective-permute-start(f32[65,128]{1,0:T(8,128)S(1)} %pad_maximum_fusion.1), channel_id=1, source_target_pairs={{0,1},{1,2},{2,3},{3,4},{4,5},{5,6},{6,7},{7,8},{8,9},{9,10},{10,1... | collective-permute-start | bytes 99848 | tf_op jit(solution)/shard_map/ppermute | solution.py:465
